TPU v7x, 128 devices: a whole 4x4x4 slice. The times are simulated.
128 devices in a mesh: blk: 32 (over x, z_hi, y), sub: 4 (over z_lo, core).
Axes of the slice: x: 4, y: 4, z: 4 (z_hi: 2, z_lo: 2; z = z_hi * 2 + z_lo), core: 2. Of those that a mesh axis runs over, the one named last changes fastest.
Arguments:
- fluid_temp: float32 [1024, 128, 512], P('blk', 'sub'), may hold values from -6 to 6
- velocity: float32 [3, 1024, 128, 512], P(None, 'blk', 'sub'), may hold values from -6 to 6
- eddy_diff: float32 [1024, 128, 512], P('blk', 'sub'), may hold values from 0.05 to 0.5
- wall_prev: float32 [131072], P(('blk', 'sub')), may hold values from -6 to 6
- row_count: int32 [128], P(('blk', 'sub')), may hold values from 256 to 1024, as said below
- owner_table: int32 [128, 128], P(('blk', 'sub')), may hold values from 0 to 4, as said below
- landing_cell: int32 [128, 1536], P(('blk', 'sub')), may hold values from 0 to 1023
- solid_temp: float32 [1024, 128, 256], P('blk', 'sub'), may hold values from -6 to 6
- conductivity: float32 [1024, 128, 256], P('blk', 'sub'), may hold values from 0.2 to 5
- sink: float32 [1024, 128, 256], P('blk', 'sub'), may hold values from 0.2 to 2
- heat_source: float32 [1024, 128, 256], P('blk', 'sub'), may hold values from -6 to 6
Outputs:
- fluid_new: float32 [1024, 128, 512], P('blk', 'sub')
- solid_new: float32 [1024, 128, 256], P('blk', 'sub')
- wall_new: float32 [131072], P(('blk', 'sub'))
Inputs may be any that keep to these rules, and one draw needn't show every extreme that they name: `row_count`: live rows of a fluid block; some block has all 1024 live in every draw. `owner_table`: no group points outside the grid of blocks; at least half of a block's groups are 0; at most 16 groups of a block have any one direction from 1 to 4, and some solid block receives exactly that many from every neighbour it has.
All inputs are finite; a program needn't handle non-finite values.
Results may differ from a plain program's by a relative error of at most 0.0003.
Values sent between devices are 32-bit elements; how exact they have to be, the bound alone decides.
A program may use at most 128 MiB of HBM per device.

v0:
```python
import jax
import jax.numpy as jnp
from jax import lax
from jax.sharding import PartitionSpec as P

FLUID_SWEEPS = 2
SWEEPS = 8


RELAX_FACTOR = 0.8
EIG_LOW = 0.02
EIG_HIGH = 2.0


def from_behind(value, axis, steps):
    count = lax.axis_size(axis)
    initial, last = (max(0, -steps), min(count, count - steps))
    return lax.ppermute(value, axis, [(source, source + steps) for source in range(initial, last)])


def extended(block, sides, width):
    for axis, dim in sides:
        count = lax.axis_size(axis)
        forward = [(i, i + 1) for i in range(count - 1)]
        backward = [(target, source) for source, target in forward]
        low = lax.ppermute(
            lax.slice_in_dim(block, block.shape[dim] - width, None, axis=dim), axis, forward
        )
        high = lax.ppermute(lax.slice_in_dim(block, 0, width, axis=dim), axis, backward)
        block = jnp.concatenate([low, block, high], axis=dim)
    return block


def face_slice(values_in, axis_no, start):
    slicer = [slice(1, -1)] * 3
    slicer[axis_no] = slice(start, values_in.shape[axis_no] - 1 + start)
    return values_in[tuple(slicer)]


def fluid_update(temp_pad, velo_pad, alpha_pad):
    center_val = temp_pad[1:-1, 1:-1, 1:-1]
    residue = jnp.zeros_like(center_val)
    weight = jnp.zeros_like(center_val)
    for axis_no in range(3):
        lower_val = face_slice(temp_pad, axis_no, 0)
        upper_val = face_slice(temp_pad, axis_no, 1)
        face_speed = 0.5 * (
            face_slice(velo_pad[axis_no], axis_no, 0) + face_slice(velo_pad[axis_no], axis_no, 1)
        )
        face_diff = 0.5 * (face_slice(alpha_pad, axis_no, 0) + face_slice(alpha_pad, axis_no, 1))
        face_flux = (
            jnp.maximum(face_speed, 0.0) * lower_val
            + jnp.minimum(face_speed, 0.0) * upper_val
            - face_diff * (upper_val - lower_val)
        )
        count_faces = face_flux.shape[axis_no]
        residue = residue - (
            lax.slice_in_dim(face_flux, 1, count_faces, axis=axis_no)
            - lax.slice_in_dim(face_flux, 0, count_faces - 1, axis=axis_no)
        )
        face_weight = face_diff + 0.5 * jnp.abs(face_speed)
        weight = (
            weight
            + lax.slice_in_dim(face_weight, 1, count_faces, axis=axis_no)
            + lax.slice_in_dim(face_weight, 0, count_faces - 1, axis=axis_no)
        )
    return center_val + RELAX_FACTOR * residue / weight


def wall_pad(temp_rim, wall_temp, live_plane):
    wall_cell = temp_rim[1:-1, 1:-1, 0]
    ghost_val = jnp.pad(wall_cell + live_plane * 2.0 * (wall_temp - wall_cell), 1)
    return jnp.concatenate(
        [ghost_val[:, :, None], temp_rim, jnp.zeros_like(ghost_val)[:, :, None]], axis=2
    )


def edge_pad(values_in):
    return jnp.pad(values_in, ((0, 0), (0, 0), (1, 1)), mode="edge")


def flow_pad(flow_rim):
    normal_speed = flow_rim[2]
    normal_pad = jnp.concatenate(
        [-normal_speed[:, :, :1], normal_speed, normal_speed[:, :, -1:]], axis=2
    )
    velo_pad = jnp.stack([edge_pad(flow_rim[0]), edge_pad(flow_rim[1]), normal_pad])
    return (velo_pad, edge_pad(flow_rim[3]))


def conduct(state_pad, cond_pad, diag_extra, rhs_field):
    center_val = state_pad[1:-1, 1:-1]
    center_cond = cond_pad[1:-1, 1:-1]
    state_z = jnp.pad(center_val, ((0, 0), (0, 0), (1, 1)))
    cond_z = jnp.pad(center_cond, ((0, 0), (0, 0), (1, 1)))
    neighbours = [
        (state_pad[2:, 1:-1], cond_pad[2:, 1:-1]),
        (state_pad[:-2, 1:-1], cond_pad[:-2, 1:-1]),
        (state_pad[1:-1, 2:], cond_pad[1:-1, 2:]),
        (state_pad[1:-1, :-2], cond_pad[1:-1, :-2]),
        (state_z[:, :, 2:], cond_z[:, :, 2:]),
        (state_z[:, :, :-2], cond_z[:, :, :-2]),
    ]
    applied = diag_extra * center_val
    diag_sum = diag_extra
    for near_val, near_cond in neighbours:
        summed = center_cond + near_cond
        conduct_face = 2.0 * center_cond * near_cond / jnp.where(summed > 0.0, summed, 1.0)
        applied = applied + conduct_face * (center_val - near_val)
        diag_sum = diag_sum + conduct_face
    return (rhs_field - applied) / jnp.where(diag_sum > 0.0, diag_sum, 1.0)


def cheby_coefficients(count_sweeps):
    center_eig = 0.5 * (EIG_HIGH + EIG_LOW)
    half_width = 0.5 * (EIG_HIGH - EIG_LOW)
    ratio_eig = center_eig / half_width
    damping = 1.0 / ratio_eig
    coefficients = [(0.0, 1.0 / center_eig)]
    for sweep_no in range(1, count_sweeps):
        damping_new = 1.0 / (2.0 * ratio_eig - damping)
        coefficients.append((damping_new * damping, 2.0 * damping_new / half_width))
        damping = damping_new
    return coefficients


def pick_groups(group_dirs, dir_code, near_groups):
    matched = group_dirs == dir_code
    group_rank = jnp.cumsum(matched.astype(jnp.int32)) - 1
    slot_ids = jnp.arange(near_groups, dtype=jnp.int32)
    return (matched[:, None] & (group_rank[:, None] == slot_ids[None, :])).astype(jnp.float32)


def move_span(payload, step_by):
    return from_behind(payload, "blk", step_by)


def move_chord(payload, step_by):
    return from_behind(payload, "sub", step_by)


def return_span(payload, step_by):
    return from_behind(payload, "blk", step_by)


def return_chord(payload, step_by):
    return from_behind(payload, "sub", step_by)


def on_device(
    fluid_temp,
    velocity,
    eddy_diff,
    wall_prev,
    row_count,
    owner_table,
    landing_cell,
    solid_temp,
    conductivity,
    sink,
    heat_source,
):
    cells_x, cells_y, cells_z = fluid_temp.shape
    row_total = cells_x * cells_y
    live_rows = (jnp.arange(row_total, dtype=jnp.int32) < row_count[0]).astype(jnp.float32)
    wall_temp = wall_prev.reshape(cells_x, cells_y)
    live_plane = live_rows.reshape(cells_x, cells_y)
    flow_stack = jnp.concatenate([velocity, eddy_diff[None]], axis=0)
    flow_rim = extended(flow_stack, (("blk", 1), ("sub", 2)), 1)
    velo_pad, alpha_pad = flow_pad(flow_rim)
    fluid_now = fluid_temp
    for sweep_no in range(FLUID_SWEEPS):
        temp_rim = extended(fluid_now, (("blk", 0), ("sub", 1)), 1)
        fluid_now = fluid_update(wall_pad(temp_rim, wall_temp, live_plane), velo_pad, alpha_pad)
    group_dirs = owner_table[0]
    group_total = group_dirs.shape[0]
    slot_cap = row_total // group_total
    near_groups = group_total // 8
    near_rows = near_groups * slot_cap
    dir_rows = jnp.repeat(group_dirs, slot_cap)
    self_mask = (dir_rows == 0).astype(jnp.float32)
    gas_temp = fluid_now[:, :, 0].reshape(-1)
    film_coeff = 2.0 * eddy_diff[:, :, 0].reshape(-1) * live_rows
    row_pair = jnp.stack([film_coeff, gas_temp]).reshape(2, group_total, slot_cap)
    selections = [pick_groups(group_dirs, dir_code, near_groups) for dir_code in (1, 2, 3, 4)]
    outbound = [
        jnp.einsum("cgk,gs->csk", row_pair, selection, precision=lax.Precision.HIGHEST).reshape(
            2, near_rows
        )
        for selection in selections
    ]
    arrived = [
        move_span(outbound[0], 1),
        move_span(outbound[1], -1),
        move_chord(outbound[2], 1),
        move_chord(outbound[3], -1),
    ]
    film_in = jnp.concatenate([film_coeff * self_mask] + [piece[0] for piece in arrived])
    gas_in = jnp.concatenate([gas_temp] + [piece[1] for piece in arrived])
    solid_x, solid_y, solid_z = solid_temp.shape
    landing = landing_cell[0]
    film_sum = jax.ops.segment_sum(film_in, landing, num_segments=solid_x * solid_y)
    film_gas = jax.ops.segment_sum(film_in * gas_in, landing, num_segments=solid_x * solid_y)
    surface_mask = (jnp.arange(solid_z, dtype=jnp.int32) == 0).astype(jnp.float32)
    diag_extra = sink + film_sum.reshape(solid_x, solid_y)[:, :, None] * surface_mask
    rhs_field = heat_source + film_gas.reshape(solid_x, solid_y)[:, :, None] * surface_mask
    coefficients = cheby_coefficients(SWEEPS)
    cond_pad = extended(conductivity, (("blk", 0), ("sub", 1)), 1)
    solid_now = solid_temp
    update = jnp.zeros_like(solid_temp)
    for decay, gain_term in coefficients:
        state_pad = extended(solid_now, (("blk", 0), ("sub", 1)), 1)
        scaled_res = conduct(state_pad, cond_pad, diag_extra, rhs_field)
        update = decay * update + gain_term * scaled_res
        solid_now = solid_now + update
    surface = solid_now[:, :, 0].reshape(-1)
    slot_values = surface[landing]
    band_values = [
        slot_values[row_total + dir_index * near_rows : row_total + (dir_index + 1) * near_rows]
        for dir_index in range(4)
    ]
    returned_bands = [
        return_span(band_values[0], -1),
        return_span(band_values[1], 1),
        return_chord(band_values[2], -1),
        return_chord(band_values[3], 1),
    ]
    wall_sum = self_mask * slot_values[:row_total]
    for dir_index in range(4):
        spread = jnp.einsum(
            "sk,gs->gk",
            returned_bands[dir_index].reshape(near_groups, slot_cap),
            selections[dir_index],
            precision=lax.Precision.HIGHEST,
        )
        wall_sum = wall_sum + spread.reshape(row_total)
    wall_new = wall_sum * live_rows
    return (fluid_now, solid_now, wall_new)


def solution(mesh):
    return jax.shard_map(
        on_device,
        mesh=mesh,
        in_specs=(
            P("blk", "sub", None),
            P(None, "blk", "sub", None),
            P("blk", "sub", None),
            P(("blk", "sub")),
            P(("blk", "sub")),
            P(("blk", "sub"), None),
            P(("blk", "sub"), None),
            P("blk", "sub", None),
            P("blk", "sub", None),
            P("blk", "sub", None),
            P("blk", "sub", None),
        ),
        out_specs=(P("blk", "sub", None), P("blk", "sub", None), P(("blk", "sub"))),
        check_vma=False,
    )
```

profile of v0, /device:TPU:5, one launch (start us, length us, event | category | flops | bytes accessed | tf_op | source)
XLA Modules:
  0.0 432.1 jit_solution(5681446776183647858)
XLA Ops:
  2.1 3.2 collective-permute-start.4
  5.3 6.6 %collective-permute-start.5 = (f32[1,32,512]{2,1,0:T(8,128)}, f32[1,32,512]{2,1,0:T(8,128)}, u32[]{:S(2)}, u32[]{:S(2)}) collective-permute-start(f32[1,32,512]{2,1,0:T(8,128)} %get-tuple-element.60), channel_id=1, source_target_pairs={{4,0},{8,4},{12,8},{16,12},{20,16},{24,20},{28,24},{32,28},{36,32}... | collective-permute-start | bytes 196616 | tf_op jit(solution)/shard_map/ppermute | solution.py:29
  14.1 3.3 collective-permute-start.1
  41.6 8.0 %collective-permute-start.17 = (f32[1,32,256]{2,1,0:T(8,128)}, f32[1,32,256]{2,1,0:T(8,128)S(1)}, u32[]{:S(2)}, u32[]{:S(2)}) collective-permute-start(f32[1,32,256]{2,1,0:T(8,128)} %get-tuple-element.96), channel_id=1, source_target_pairs={{4,0},{8,4},{12,8},{16,12},{20,16},{24,20},{28,24},{32,28},{36,32}... | collective-permute-start | bytes 98312 | tf_op jit(solution)/shard_map/ppermute | solution.py:29
  54.8 6.5 %collective-permute-done.18 = f32[1,32,256]{2,1,0:T(8,128)S(1)} collective-permute-done((f32[1,32,256]{2,1,0:T(8,128)S(1)}, f32[1,32,256]{2,1,0:T(8,128)S(1)}, u32[]{:S(2)}, u32[]{:S(2)}) %collective-permute-start.18) | collective-permute-done | bytes 32800 | tf_op jit(solution)/shard_map/ppermute | solution.py:26
  65.9 8.0 %collective-permute-start.23 = (f32[34,1,256]{2,1,0:T(1,128)}, f32[34,1,256]{2,1,0:T(1,128)}, u32[]{:S(2)}, u32[]{:S(2)}) collective-permute-start(f32[34,1,256]{2,1,0:T(1,128)} %get-tuple-element.79), channel_id=1, source_target_pairs={{0,1},{1,2},{2,3},{4,5},{5,6},{6,7},{8,9},{9,10},{10,11},{12,13},{... | collective-permute-start | bytes 104456 | tf_op jit(solution)/shard_map/ppermute | solution.py:26
  83.9 3.6 collective-permute-start.2
  92.0 4.2 collective-permute-start.6
  96.5 7.9 %pad_maximum_fusion = f32[4,34,34,512]{3,2,1,0:T(8,128)} fusion(f32[4,34,1,512]{3,2,1,0:T(1,128)S(1)} %copy.235, f32[4,1,32,512]{3,2,1,0:T(8,128)S(1)} %collective-permute-done.1, f32[1,32,32,512]{3,2,1,0:T(8,128)S(1)} %bitcast.98, f32[3,32,32,512]{3,2,1,0:T(8,128)S(1)} %bitcast.95, f32[4,1,32,512]{3,2,1,0:T(8,128)} %collective-permute-done, ...), kind=kLoop, calls=%fused_computation.3 | loop fusion | flops 11837440 | bytes 18939904 | tf_op jit(solution)/shard_map/concatenate | solution.py:30
  104.4 7.4 %slice_bitcast_fusion.3 = (f32[34,34,512]{2,1,0:T(8,128)}, f32[34,34,512]{2,1,0:T(8,128)S(1)}, f32[34,34,512]{2,1,0:T(8,128)S(1)}, f32[34,34,512]{2,1,0:T(8,128)S(1)}) fusion(f32[4,34,34,512]{3,2,1,0:T(8,128)} %pad_maximum_fusion), kind=kLoop, calls=%fused_computation.14 | loop fusion | bytes 18939904 | tf_op jit(solution)/shard_map/squeeze | solution.py:87
  115.7 4.0 multiply_add_fusion.2
  119.7 5.6 %multiply_add_fusion = f32[32,32,513]{2,1,0:T(8,128)S(1)} fusion(f32[34,34,1]{2,1,0:T(8,128)S(1)} %get-tuple-element.50, f32[34,34,512]{2,1,0:T(8,128)S(1)} %get-tuple-element.36, f32[34,34,1]{2,1,0:T(8,128)S(1)} %get-tuple-element.49, f32[34,34,1]{2,1,0:T(8,128)} %get-tuple-element.48, f32[34,34,512]{2,1,0:T(8,128)S(1)} %get-tuple-element.38, ...), kind=kLoop, calls=%fused_computation.60 | loop fusion | flops 5778432 | bytes 6854720 | tf_op jit(solution)/shard_map/add | solution.py:61
  125.4 3.8 multiply_subtract_fusion.2
  129.2 3.9 multiply_add_fusion.1
  133.1 6.5 %fusion.23 = (f32[32,32,512]{2,1,0:T(8,128)S(1)}, f32[32,32,512]{2,1,0:T(8,128)}) fusion(f32[32,32,512]{2,1,0:T(8,128)} %param.11, f32[32,32,513]{2,1,0:T(8,128)S(1)} %multiply_subtract_fusion.2, f32[32,33,512]{2,1,0:T(8,128)} %get-tuple-element.46, f32[33,32,512]{2,1,0:T(8,128)S(1)} %get-tuple-element.44, f32[32,32,513]{2,1,0:T(8,128)S(1)} %multiply_add_fusion, ...), kind=kLoop, calls=%fused_computation.91 | loop fusion | flops 7340032 | bytes 31457280 | tf_op jit(solution)/shard_map/add | solution.py:67
  141.3 8.5 %collective-permute-start.9 = (f32[1,32,512]{2,1,0:T(8,128)}, f32[1,32,512]{2,1,0:T(8,128)}, u32[]{:S(2)}, u32[]{:S(2)}) collective-permute-start(f32[1,32,512]{2,1,0:T(8,128)} %get-tuple-element.56), channel_id=1, source_target_pairs={{4,0},{8,4},{12,8},{16,12},{20,16},{24,20},{28,24},{32,28},{36,32}... | collective-permute-start | bytes 196616 | tf_op jit(solution)/shard_map/ppermute | solution.py:29
  154.3 5.5 %collective-permute-done.8 = f32[1,32,512]{2,1,0:T(8,128)} collective-permute-done((f32[1,32,512]{2,1,0:T(8,128)}, f32[1,32,512]{2,1,0:T(8,128)}, u32[]{:S(2)}, u32[]{:S(2)}) %collective-permute-start.8) | collective-permute-done | bytes 65568 | tf_op jit(solution)/shard_map/ppermute | solution.py:26
  163.3 3.5 collective-permute-start.10
  166.8 4.2 multiply_subtract_fusion.4
  176.2 6.8 %multiply_subtract_fusion = f32[32,32,513]{2,1,0:T(8,128)S(1)} fusion(f32[34,1,512]{2,1,0:T(1,128)S(1)} %collective-permute-done.11, f32[1,32,512]{2,1,0:T(8,128)} %collective-permute-done.9, f32[32,32,512]{2,1,0:T(8,128)S(1)} %copy-done.3, f32[1,32,512]{2,1,0:T(8,128)} %collective-permute-done.8, f32[34,1,512]{2,1,0:T(1,128)S(1)} %collective-permute-done.10, ...), kind=kLoop, calls=%fused_computation.58 | loop fusion | flops 16284672 | bytes 9226832 | tf_op jit(solution)/shard_map/sub | solution.py:52
  183.1 3.5 fusion.17
  191.6 5.9 %collective-permute-done.12 = f32[2,128]{1,0:T(2,128)S(1)} collective-permute-done((f32[2,128]{1,0:T(2,128)S(1)}, f32[2,128]{1,0:T(2,128)S(1)}, u32[]{:S(2)}, u32[]{:S(2)}) %collective-permute-start.12) | collective-permute-done | bytes 1056 | tf_op jit(solution)/shard_map/ppermute | solution.py:18
  201.9 4.2 collective-permute-start.14
  209.1 3.1 collective-permute-done.15
  212.2 11.3 %scatter_custom_fusion.1 = f32[1024]{0:T(1024)S(1)} fusion(s32[1536]{0:T(1024)} %reduce.1, f32[1536]{0:T(1024)S(1)} %get-tuple-element.107, f32[]{:T(128)} %constant.29.clone.1), kind=kCustom, calls=%fused_computation.474 | custom fusion | flops 1536 | bytes 4608 | tf_op jit(solution)/shard_map/scatter-add | solution.py:202
  223.6 11.5 %scatter_custom_fusion = f32[1024]{0:T(1024)S(1)} fusion(s32[1536]{0:T(1024)} %reduce.1, f32[1536]{0:T(1024)S(1)} %mul.580, f32[]{:T(128)} %constant.29.clone.1), kind=kCustom, calls=%fused_computation.476 | custom fusion | flops 1536 | bytes 4608 | tf_op jit(solution)/shard_map/scatter-add | solution.py:203
  235.2 7.9 %multiply_add_fusion.9 = (f32[32,32,256]{2,1,0:T(8,128)S(1)}, f32[32,32,256]{2,1,0:T(8,128)S(1)}, f32[32,32,256]{2,1,0:T(8,128)S(1)}, f32[32,32,256]{2,1,0:T(8,1...) fusion(f32[32,32,256]{2,1,0:T(8,128)} %param.18, f32[34,32,256]{2,1,0:T(8,128)} %copy-done.28, ...), kind=kLoop, calls=%fused_computation.359 | loop fusion | flops 19398656 | bytes 12993536 | tf_op jit(solution)/shard_map/add | solution.py:215
  243.1 6.8 %collective-permute-start.24 = (f32[1,32,256]{2,1,0:T(8,128)S(1)}, f32[1,32,256]{2,1,0:T(8,128)S(1)}, u32[]{:S(2)}, u32[]{:S(2)}) collective-permute-start(f32[1,32,256]{2,1,0:T(8,128)S(1)} %get-tuple-element.93), channel_id=1, source_target_pairs={{4,0},{8,4},{12,8},{16,12},{20,16},{24,20},{28,24},{32,28},{36,32}... | collective-permute-start | bytes 98312 | tf_op jit(solution)/shard_map/ppermute | solution.py:29
  251.8 7.2 %collective-permute-done.25 = f32[1,32,256]{2,1,0:T(8,128)S(1)} collective-permute-done((f32[1,32,256]{2,1,0:T(8,128)S(1)}, f32[1,32,256]{2,1,0:T(8,128)S(1)}, u32[]{:S(2)}, u32[]{:S(2)}) %collective-permute-start.25) | collective-permute-done | bytes 32800 | tf_op jit(solution)/shard_map/ppermute | solution.py:26
  259.1 2.8 collective-permute-start.27
  263.8 3.3 collective-permute-done.26
  267.1 3.6 fusion.196
  272.7 3.3 collective-permute-start.29
  276.1 5.8 %collective-permute-done.29 = f32[1,32,256]{2,1,0:T(8,128)S(1)} collective-permute-done((f32[1,32,256]{2,1,0:T(8,128)S(1)}, f32[1,32,256]{2,1,0:T(8,128)S(1)}, u32[]{:S(2)}, u32[]{:S(2)}) %collective-permute-start.29) | collective-permute-done | bytes 32800 | tf_op jit(solution)/shard_map/ppermute | solution.py:26
  281.9 3.0 collective-permute-start.31
  286.9 3.3 collective-permute-done.30
  290.2 3.4 fusion.254
  295.5 3.3 collective-permute-start.33
  298.9 5.8 %collective-permute-done.33 = f32[1,32,256]{2,1,0:T(8,128)S(1)} collective-permute-done((f32[1,32,256]{2,1,0:T(8,128)S(1)}, f32[1,32,256]{2,1,0:T(8,128)S(1)}, u32[]{:S(2)}, u32[]{:S(2)}) %collective-permute-start.33) | collective-permute-done | bytes 32800 | tf_op jit(solution)/shard_map/ppermute | solution.py:26
  304.8 3.0 collective-permute-start.35
  309.8 3.3 collective-permute-done.34
  313.1 3.4 fusion.253
  318.4 3.3 collective-permute-start.37
  321.8 5.8 %collective-permute-done.37 = f32[1,32,256]{2,1,0:T(8,128)S(1)} collective-permute-done((f32[1,32,256]{2,1,0:T(8,128)S(1)}, f32[1,32,256]{2,1,0:T(8,128)S(1)}, u32[]{:S(2)}, u32[]{:S(2)}) %collective-permute-start.37) | collective-permute-done | bytes 32800 | tf_op jit(solution)/shard_map/ppermute | solution.py:26
  327.6 3.0 collective-permute-start.39
  332.6 3.3 collective-permute-done.38
  335.9 3.4 fusion.252
  341.3 3.3 collective-permute-start.41
  344.6 5.8 %collective-permute-done.41 = f32[1,32,256]{2,1,0:T(8,128)S(1)} collective-permute-done((f32[1,32,256]{2,1,0:T(8,128)S(1)}, f32[1,32,256]{2,1,0:T(8,128)S(1)}, u32[]{:S(2)}, u32[]{:S(2)}) %collective-permute-start.41) | collective-permute-done | bytes 32800 | tf_op jit(solution)/shard_map/ppermute | solution.py:26
  350.5 3.0 collective-permute-start.43
  355.5 3.3 collective-permute-done.42
  358.8 3.4 fusion.251
  364.1 3.3 collective-permute-start.45
  367.5 5.8 %collective-permute-done.45 = f32[1,32,256]{2,1,0:T(8,128)S(1)} collective-permute-done((f32[1,32,256]{2,1,0:T(8,128)S(1)}, f32[1,32,256]{2,1,0:T(8,128)S(1)}, u32[]{:S(2)}, u32[]{:S(2)}) %collective-permute-start.45) | collective-permute-done | bytes 32800 | tf_op jit(solution)/shard_map/ppermute | solution.py:26
  373.3 3.0 collective-permute-start.47
  378.3 3.3 collective-permute-done.46
  381.6 3.4 fusion.250
  387.0 3.3 collective-permute-start.49
  390.4 5.8 %collective-permute-done.49 = f32[1,32,256]{2,1,0:T(8,128)S(1)} collective-permute-done((f32[1,32,256]{2,1,0:T(8,128)S(1)}, f32[1,32,256]{2,1,0:T(8,128)S(1)}, u32[]{:S(2)}, u32[]{:S(2)}) %collective-permute-start.49) | collective-permute-done | bytes 32800 | tf_op jit(solution)/shard_map/ppermute | solution.py:26
  396.2 3.0 collective-permute-start.51
  401.2 3.3 collective-permute-done.50
  404.5 3.6 add_add_fusion
  409.4 5.8 %gather_fusion = f32[1536]{0:T(1024)S(1)} fusion(f32[1024]{0:T(1024)S(1)} %reshape_squeeze.8, s32[2048]{0:T(1024)S(1)} %pad_clamp_fusion), kind=kCustom, calls=%fused_computation | custom fusion | bytes 18432 | tf_op jit(solution)/shard_map/gather | solution.py:217
  421.5 7.9 %collective-permute-start.52 = (f32[128]{0:T(128)S(1)}, f32[128]{0:T(128)S(1)}, u32[]{:S(2)}, u32[]{:S(2)}) collective-permute-start(f32[128]{0:T(128)S(1)} %get-tuple-element.102), channel_id=1, source_target_pairs={{4,0},{8,4},{12,8},{16,12},{20,16},{24,20},{28,24},{32,28},{36,32}... | collective-permute-start | bytes 1544 | tf_op jit(solution)/shard_map/ppermute | solution.py:18
  (288 shorter events, 119.5 us)
Async XLA Ops:
  2.1 72.5 %collective-permute-start.4 = (f32[1,32,512]{2,1,0:T(8,128)}, f32[1,32,512]{2,1,0:T(8,128)}, u32[]{:S(2)}, u32[]{:S(2)}) collective-permute-start(f32[1,32,512]{2,1,0:T(8,128)} %get-tuple-element.61), channel_id=1, source_target_pairs={{0,4},{4,8},{8,12},{12,16},{16,20},{20,24},{24,28},{28,32},{32,36}... | collective-permute-start | bytes 196616 | tf_op jit(solution)/shard_map/ppermute | solution.py:26
  5.3 78.6 %collective-permute-start.5 = (f32[1,32,512]{2,1,0:T(8,128)}, f32[1,32,512]{2,1,0:T(8,128)}, u32[]{:S(2)}, u32[]{:S(2)}) collective-permute-start(f32[1,32,512]{2,1,0:T(8,128)} %get-tuple-element.60), channel_id=1, source_target_pairs={{4,0},{8,4},{12,8},{16,12},{20,16},{24,20},{28,24},{32,28},{36,32}... | collective-permute-start | bytes 196616 | tf_op jit(solution)/shard_map/ppermute | solution.py:29
  14.1 64.3 %collective-permute-start.1 = (f32[4,1,32,512]{3,2,1,0:T(8,128)}, f32[4,1,32,512]{3,2,1,0:T(8,128)S(1)}, u32[]{:S(2)}, u32[]{:S(2)}) collective-permute-start(f32[4,1,32,512]{3,2,1,0:T(8,128)} %get-tuple-element.42), channel_id=1, source_target_pairs={{4,0},{8,4},{12,8},{16,12},{20,16},{24,20},{28,24},{32,28},{36,32}... | collective-permute-start | bytes 786440 | tf_op jit(solution)/shard_map/ppermute | solution.py:29
  17.5 62.9 %collective-permute-start = (f32[4,1,32,512]{3,2,1,0:T(8,128)}, f32[4,1,32,512]{3,2,1,0:T(8,128)}, u32[]{:S(2)}, u32[]{:S(2)}) collective-permute-start(f32[4,1,32,512]{3,2,1,0:T(8,128)} %get-tuple-element.41), channel_id=1, source_target_pairs={{0,4},{4,8},{8,12},{12,16},{16,20},{20,24},{24,28},{28,32},{32,36}... | collective-permute-start | bytes 786440 | tf_op jit(solution)/shard_map/ppermute | solution.py:26
  20.8 20.9 %collective-permute-start.19 = (f32[1,32,256]{2,1,0:T(8,128)}, f32[1,32,256]{2,1,0:T(8,128)}, u32[]{:S(2)}, u32[]{:S(2)}) collective-permute-start(f32[1,32,256]{2,1,0:T(8,128)} %get-tuple-element.97), channel_id=1, source_target_pairs={{0,4},{4,8},{8,12},{12,16},{16,20},{20,24},{24,28},{28,32},{32,36}... | collective-permute-start | bytes 98312 | tf_op jit(solution)/shard_map/ppermute | solution.py:26
  41.6 35.9 %copy-start.12 = (f32[32,32,512]{2,1,0:T(8,128)S(1)}, f32[32,32,512]{2,1,0:T(8,128)}, u32[]{:S(2)}) copy-start(f32[32,32,512]{2,1,0:T(8,128)} %param.11) | copy-start | bytes 6291460
  41.6 10.2 %collective-permute-start.17 = (f32[1,32,256]{2,1,0:T(8,128)}, f32[1,32,256]{2,1,0:T(8,128)S(1)}, u32[]{:S(2)}, u32[]{:S(2)}) collective-permute-start(f32[1,32,256]{2,1,0:T(8,128)} %get-tuple-element.96), channel_id=1, source_target_pairs={{4,0},{8,4},{12,8},{16,12},{20,16},{24,20},{28,24},{32,28},{36,32}... | collective-permute-start | bytes 98312 | tf_op jit(solution)/shard_map/ppermute | solution.py:29
  50.4 30.0 %slice-start = ((s8[6291456]{0:T(1024)(128)(4,1)}), s8[4194304]{0:T(1024)(128)(4,1)S(1)}, s32[]{:S(2)}) async-start(s8[6291456]{0:T(1024)(128)(4,1)} %bitcast.94), calls=%async_computation | async-start | bytes 8388608
  51.9 9.3 %collective-permute-start.18 = (f32[1,32,256]{2,1,0:T(8,128)S(1)}, f32[1,32,256]{2,1,0:T(8,128)S(1)}, u32[]{:S(2)}, u32[]{:S(2)}) collective-permute-start(f32[1,32,256]{2,1,0:T(8,128)S(1)} %copy-done.37), channel_id=1, source_target_pairs={{0,4},{4,8},{8,12},{12,16},{16,20},{20,24},{24,28},{28,32},{32,36}... | collective-permute-start | bytes 98312 | tf_op jit(solution)/shard_map/ppermute | solution.py:26
  61.2 4.6 %collective-permute-start.16 = (f32[1,32,256]{2,1,0:T(8,128)S(1)}, f32[1,32,256]{2,1,0:T(8,128)S(1)}, u32[]{:S(2)}, u32[]{:S(2)}) collective-permute-start(f32[1,32,256]{2,1,0:T(8,128)S(1)} %copy-done.36), channel_id=1, source_target_pairs={{4,0},{8,4},{12,8},{16,12},{20,16},{24,20},{28,24},{32,28},{36,32}... | collective-permute-start | bytes 98312 | tf_op jit(solution)/shard_map/ppermute | solution.py:29
  65.9 169.3 %collective-permute-start.23 = (f32[34,1,256]{2,1,0:T(1,128)}, f32[34,1,256]{2,1,0:T(1,128)}, u32[]{:S(2)}, u32[]{:S(2)}) collective-permute-start(f32[34,1,256]{2,1,0:T(1,128)} %get-tuple-element.79), channel_id=1, source_target_pairs={{0,1},{1,2},{2,3},{4,5},{5,6},{6,7},{8,9},{9,10},{10,11},{12,13},{... | collective-permute-start | bytes 104456 | tf_op jit(solution)/shard_map/ppermute | solution.py:26
  74.7 160.4 %collective-permute-start.21 = (f32[34,1,256]{2,1,0:T(1,128)}, f32[34,1,256]{2,1,0:T(1,128)}, u32[]{:S(2)}, u32[]{:S(2)}) collective-permute-start(f32[34,1,256]{2,1,0:T(1,128)} %get-tuple-element.78), channel_id=1, source_target_pairs={{1,0},{2,1},{3,2},{5,4},{6,5},{7,6},{9,8},{10,9},{11,10},{13,12},{... | collective-permute-start | bytes 104456 | tf_op jit(solution)/shard_map/ppermute | solution.py:29
  78.4 156.7 %collective-permute-start.20 = (f32[34,1,256]{2,1,0:T(1,128)}, f32[34,1,256]{2,1,0:T(1,128)}, u32[]{:S(2)}, u32[]{:S(2)}) collective-permute-start(f32[34,1,256]{2,1,0:T(1,128)} %get-tuple-element.77), channel_id=1, source_target_pairs={{1,0},{2,1},{3,2},{5,4},{6,5},{7,6},{9,8},{10,9},{11,10},{13,12},{... | collective-permute-start | bytes 104456 | tf_op jit(solution)/shard_map/ppermute | solution.py:29
  81.9 7.9 %collective-permute-start.3 = (f32[4,34,1,512]{3,0,2,1:T(4,128)S(1)}, f32[4,34,1,512]{3,0,2,1:T(4,128)S(1)}, u32[]{:S(2)}, u32[]{:S(2)}) collective-permute-start(f32[4,34,1,512]{3,0,2,1:T(4,128)S(1)} %copy.258), channel_id=1, source_target_pairs={{1,0},{2,1},{3,2},{5,4},{6,5},{7,6},{9,8},{10,9},{11,10},{13,12},{... | collective-permute-start | bytes 835592 | tf_op jit(solution)/shard_map/ppermute | solution.py:29
  83.9 8.1 %collective-permute-start.2 = (f32[4,34,1,512]{3,0,2,1:T(4,128)S(1)}, f32[4,34,1,512]{3,0,2,1:T(4,128)S(1)}, u32[]{:S(2)}, u32[]{:S(2)}) collective-permute-start(f32[4,34,1,512]{3,0,2,1:T(4,128)S(1)} %copy.257), channel_id=1, source_target_pairs={{0,1},{1,2},{2,3},{4,5},{5,6},{6,7},{8,9},{9,10},{10,11},{12,13},{... | collective-permute-start | bytes 835592 | tf_op jit(solution)/shard_map/ppermute | solution.py:26
  89.8 35.5 %collective-permute-start.7 = (f32[34,1,512]{2,1,0:T(1,128)}, f32[34,1,512]{2,1,0:T(1,128)S(1)}, u32[]{:S(2)}, u32[]{:S(2)}) collective-permute-start(f32[34,1,512]{2,1,0:T(1,128)} %get-tuple-element.54), channel_id=1, source_target_pairs={{1,0},{2,1},{3,2},{5,4},{6,5},{7,6},{9,8},{10,9},{11,10},{13,12},{... | collective-permute-start | bytes 208904 | tf_op jit(solution)/shard_map/ppermute | solution.py:29
  92.0 33.3 %collective-permute-start.6 = (f32[34,1,512]{2,1,0:T(1,128)}, f32[34,1,512]{2,1,0:T(1,128)S(1)}, u32[]{:S(2)}, u32[]{:S(2)}) collective-permute-start(f32[34,1,512]{2,1,0:T(1,128)} %get-tuple-element.53), channel_id=1, source_target_pairs={{0,1},{1,2},{2,3},{4,5},{5,6},{6,7},{8,9},{9,10},{10,11},{12,13},{... | collective-permute-start | bytes 208904 | tf_op jit(solution)/shard_map/ppermute | solution.py:26
  141.3 13.0 %collective-permute-start.9 = (f32[1,32,512]{2,1,0:T(8,128)}, f32[1,32,512]{2,1,0:T(8,128)}, u32[]{:S(2)}, u32[]{:S(2)}) collective-permute-start(f32[1,32,512]{2,1,0:T(8,128)} %get-tuple-element.56), channel_id=1, source_target_pairs={{4,0},{8,4},{12,8},{16,12},{20,16},{24,20},{28,24},{32,28},{36,32}... | collective-permute-start | bytes 196616 | tf_op jit(solution)/shard_map/ppermute | solution.py:29
  149.7 10.1 %collective-permute-start.8 = (f32[1,32,512]{2,1,0:T(8,128)}, f32[1,32,512]{2,1,0:T(8,128)}, u32[]{:S(2)}, u32[]{:S(2)}) collective-permute-start(f32[1,32,512]{2,1,0:T(8,128)} %get-tuple-element.55), channel_id=1, source_target_pairs={{0,4},{4,8},{8,12},{12,16},{16,20},{20,24},{24,28},{28,32},{32,36}... | collective-permute-start | bytes 196616 | tf_op jit(solution)/shard_map/ppermute | solution.py:26
  161.2 9.8 %collective-permute-start.11 = (f32[34,1,512]{2,1,0:T(1,128)S(1)}, f32[34,1,512]{2,1,0:T(1,128)S(1)}, u32[]{:S(2)}, u32[]{:S(2)}) collective-permute-start(f32[34,1,512]{2,1,0:T(1,128)S(1)} %get-tuple-element.52), channel_id=1, source_target_pairs={{1,0},{2,1},{3,2},{5,4},{6,5},{7,6},{9,8},{10,9},{11,10},{13,12},{... | collective-permute-start | bytes 208904 | tf_op jit(solution)/shard_map/ppermute | solution.py:29
  163.3 10.1 %collective-permute-start.10 = (f32[34,1,512]{2,1,0:T(1,128)S(1)}, f32[34,1,512]{2,1,0:T(1,128)S(1)}, u32[]{:S(2)}, u32[]{:S(2)}) collective-permute-start(f32[34,1,512]{2,1,0:T(1,128)S(1)} %get-tuple-element.51), channel_id=1, source_target_pairs={{0,1},{1,2},{2,3},{4,5},{5,6},{6,7},{8,9},{9,10},{10,11},{12,13},{... | collective-permute-start | bytes 208904 | tf_op jit(solution)/shard_map/ppermute | solution.py:26
  171.1 64.1 %collective-permute-start.22 = (f32[34,1,256]{2,1,0:T(1,128)}, f32[34,1,256]{2,1,0:T(1,128)}, u32[]{:S(2)}, u32[]{:S(2)}) collective-permute-start(f32[34,1,256]{2,1,0:T(1,128)} %get-tuple-element.76), channel_id=1, source_target_pairs={{0,1},{1,2},{2,3},{4,5},{5,6},{6,7},{8,9},{9,10},{10,11},{12,13},{... | collective-permute-start | bytes 104456 | tf_op jit(solution)/shard_map/ppermute | solution.py:26
  183.1 52.1 %copy-start.1 = (f32[32,32,256]{2,1,0:T(8,128)S(1)}, f32[32,32,256]{2,1,0:T(8,128)}, u32[]{:S(2)}) copy-start(f32[32,32,256]{2,1,0:T(8,128)} %param.19) | copy-start | bytes 3145732
  183.1 52.1 %copy-start.4 = (f32[32,32,256]{2,1,0:T(8,128)S(1)}, f32[32,32,256]{2,1,0:T(8,128)}, u32[]{:S(2)}) copy-start(f32[32,32,256]{2,1,0:T(8,128)} %param.20) | copy-start | bytes 3145732
  183.1 52.1 %copy-start.5 = (f32[32,32,256]{2,1,0:T(8,128)S(1)}, f32[32,32,256]{2,1,0:T(8,128)}, u32[]{:S(2)}) copy-start(f32[32,32,256]{2,1,0:T(8,128)} %param.21) | copy-start | bytes 3145732
  183.1 52.1 %copy-start.33 = (f32[1,32,256]{2,1,0:T(8,128)S(1)}, f32[1,32,256]{2,1,0:T(8,128)}, u32[]{:S(2)}) copy-start(f32[1,32,256]{2,1,0:T(8,128)} %copy-done.32) | copy-start | bytes 98308
  183.1 52.1 %copy-start.35 = (f32[256]{0:T(256)S(1)}, f32[256]{0:T(256)}, u32[]{:S(2)}) copy-start(f32[256]{0:T(256)} %compare_convert_fusion) | copy-start | bytes 3076
  188.7 8.8 %collective-permute-start.12 = (f32[2,128]{1,0:T(2,128)S(1)}, f32[2,128]{1,0:T(2,128)S(1)}, u32[]{:S(2)}, u32[]{:S(2)}) collective-permute-start(f32[2,128]{1,0:T(2,128)S(1)} %reshape.291), channel_id=1, source_target_pairs={{0,4},{4,8},{8,12},{12,16},{16,20},{20,24},{24,28},{28,32},{32,36}... | collective-permute-start | bytes 3080 | tf_op jit(solution)/shard_map/ppermute | solution.py:18
  197.6 4.3 collective-permute-start.13
  201.9 5.2 %collective-permute-start.14 = (f32[2,128]{1,0:T(2,128)S(1)}, f32[2,128]{1,0:T(2,128)S(1)}, u32[]{:S(2)}, u32[]{:S(2)}) collective-permute-start(f32[2,128]{1,0:T(2,128)S(1)} %reshape.293), channel_id=1, source_target_pairs={{0,1},{1,2},{2,3},{4,5},{5,6},{6,7},{8,9},{9,10},{10,11},{12,13},{... | collective-permute-start | bytes 3080 | tf_op jit(solution)/shard_map/ppermute | solution.py:18
  207.0 5.2 %collective-permute-start.15 = (f32[2,128]{1,0:T(2,128)S(1)}, f32[2,128]{1,0:T(2,128)S(1)}, u32[]{:S(2)}, u32[]{:S(2)}) collective-permute-start(f32[2,128]{1,0:T(2,128)S(1)} %reshape.294), channel_id=1, source_target_pairs={{1,0},{2,1},{3,2},{5,4},{6,5},{7,6},{9,8},{10,9},{11,10},{13,12},{... | collective-permute-start | bytes 3080 | tf_op jit(solution)/shard_map/ppermute | solution.py:18
  235.1 32.0 %copy-start.19 = (f32[32,32,256]{2,1,0:T(8,128)S(1)}, f32[32,32,256]{2,1,0:T(8,128)}, u32[]{:S(2)}) copy-start(f32[32,32,256]{2,1,0:T(8,128)} %param.18) | copy-start | bytes 3145732
  243.1 8.7 %collective-permute-start.24 = (f32[1,32,256]{2,1,0:T(8,128)S(1)}, f32[1,32,256]{2,1,0:T(8,128)S(1)}, u32[]{:S(2)}, u32[]{:S(2)}) collective-permute-start(f32[1,32,256]{2,1,0:T(8,128)S(1)} %get-tuple-element.93), channel_id=1, source_target_pairs={{4,0},{8,4},{12,8},{16,12},{20,16},{24,20},{28,24},{32,28},{36,32}... | collective-permute-start | bytes 98312 | tf_op jit(solution)/shard_map/ppermute | solution.py:29
  249.9 9.2 %collective-permute-start.25 = (f32[1,32,256]{2,1,0:T(8,128)S(1)}, f32[1,32,256]{2,1,0:T(8,128)S(1)}, u32[]{:S(2)}, u32[]{:S(2)}) collective-permute-start(f32[1,32,256]{2,1,0:T(8,128)S(1)} %get-tuple-element.92), channel_id=1, source_target_pairs={{0,4},{4,8},{8,12},{12,16},{16,20},{20,24},{24,28},{28,32},{32,36}... | collective-permute-start | bytes 98312 | tf_op jit(solution)/shard_map/ppermute | solution.py:26
  259.1 4.7 %collective-permute-start.27 = (f32[34,1,256]{2,1,0:T(1,128)S(1)}, f32[34,1,256]{2,1,0:T(1,128)S(1)}, u32[]{:S(2)}, u32[]{:S(2)}) collective-permute-start(f32[34,1,256]{2,1,0:T(1,128)S(1)} %get-tuple-element.75), channel_id=1, source_target_pairs={{0,1},{1,2},{2,3},{4,5},{5,6},{6,7},{8,9},{9,10},{10,11},{12,13},{... | collective-permute-start | bytes 104456 | tf_op jit(solution)/shard_map/ppermute | solution.py:26
  261.9 5.3 %collective-permute-start.26 = (f32[34,1,256]{2,1,0:T(1,128)S(1)}, f32[34,1,256]{2,1,0:T(1,128)S(1)}, u32[]{:S(2)}, u32[]{:S(2)}) collective-permute-start(f32[34,1,256]{2,1,0:T(1,128)S(1)} %get-tuple-element.74), channel_id=1, source_target_pairs={{1,0},{2,1},{3,2},{5,4},{6,5},{7,6},{9,8},{10,9},{11,10},{13,12},{... | collective-permute-start | bytes 104456 | tf_op jit(solution)/shard_map/ppermute | solution.py:29
  270.7 5.3 %collective-permute-start.28 = (f32[1,32,256]{2,1,0:T(8,128)S(1)}, f32[1,32,256]{2,1,0:T(8,128)S(1)}, u32[]{:S(2)}, u32[]{:S(2)}) collective-permute-start(f32[1,32,256]{2,1,0:T(8,128)S(1)} %get-tuple-element.91), channel_id=1, source_target_pairs={{4,0},{8,4},{12,8},{16,12},{20,16},{24,20},{28,24},{32,28},{36,32}... | collective-permute-start | bytes 98312 | tf_op jit(solution)/shard_map/ppermute | solution.py:29
  272.7 9.2 %collective-permute-start.29 = (f32[1,32,256]{2,1,0:T(8,128)S(1)}, f32[1,32,256]{2,1,0:T(8,128)S(1)}, u32[]{:S(2)}, u32[]{:S(2)}) collective-permute-start(f32[1,32,256]{2,1,0:T(8,128)S(1)} %get-tuple-element.90), channel_id=1, source_target_pairs={{0,4},{4,8},{8,12},{12,16},{16,20},{20,24},{24,28},{28,32},{32,36}... | collective-permute-start | bytes 98312 | tf_op jit(solution)/shard_map/ppermute | solution.py:26
  281.9 5.0 %collective-permute-start.31 = (f32[34,1,256]{2,1,0:T(1,128)S(1)}, f32[34,1,256]{2,1,0:T(1,128)S(1)}, u32[]{:S(2)}, u32[]{:S(2)}) collective-permute-start(f32[34,1,256]{2,1,0:T(1,128)S(1)} %get-tuple-element.73), channel_id=1, source_target_pairs={{0,1},{1,2},{2,3},{4,5},{5,6},{6,7},{8,9},{9,10},{10,11},{12,13},{... | collective-permute-start | bytes 104456 | tf_op jit(solution)/shard_map/ppermute | solution.py:26
  285.0 5.3 %collective-permute-start.30 = (f32[34,1,256]{2,1,0:T(1,128)S(1)}, f32[34,1,256]{2,1,0:T(1,128)S(1)}, u32[]{:S(2)}, u32[]{:S(2)}) collective-permute-start(f32[34,1,256]{2,1,0:T(1,128)S(1)} %get-tuple-element.72), channel_id=1, source_target_pairs={{1,0},{2,1},{3,2},{5,4},{6,5},{7,6},{9,8},{10,9},{11,10},{13,12},{... | collective-permute-start | bytes 104456 | tf_op jit(solution)/shard_map/ppermute | solution.py:29
  293.6 5.3 %collective-permute-start.32 = (f32[1,32,256]{2,1,0:T(8,128)S(1)}, f32[1,32,256]{2,1,0:T(8,128)S(1)}, u32[]{:S(2)}, u32[]{:S(2)}) collective-permute-start(f32[1,32,256]{2,1,0:T(8,128)S(1)} %get-tuple-element.89), channel_id=1, source_target_pairs={{4,0},{8,4},{12,8},{16,12},{20,16},{24,20},{28,24},{32,28},{36,32}... | collective-permute-start | bytes 98312 | tf_op jit(solution)/shard_map/ppermute | solution.py:29
  295.5 9.2 %collective-permute-start.33 = (f32[1,32,256]{2,1,0:T(8,128)S(1)}, f32[1,32,256]{2,1,0:T(8,128)S(1)}, u32[]{:S(2)}, u32[]{:S(2)}) collective-permute-start(f32[1,32,256]{2,1,0:T(8,128)S(1)} %get-tuple-element.88), channel_id=1, source_target_pairs={{0,4},{4,8},{8,12},{12,16},{16,20},{20,24},{24,28},{28,32},{32,36}... | collective-permute-start | bytes 98312 | tf_op jit(solution)/shard_map/ppermute | solution.py:26
  304.8 5.0 %collective-permute-start.35 = (f32[34,1,256]{2,1,0:T(1,128)S(1)}, f32[34,1,256]{2,1,0:T(1,128)S(1)}, u32[]{:S(2)}, u32[]{:S(2)}) collective-permute-start(f32[34,1,256]{2,1,0:T(1,128)S(1)} %get-tuple-element.71), channel_id=1, source_target_pairs={{0,1},{1,2},{2,3},{4,5},{5,6},{6,7},{8,9},{9,10},{10,11},{12,13},{... | collective-permute-start | bytes 104456 | tf_op jit(solution)/shard_map/ppermute | solution.py:26
  307.8 5.3 %collective-permute-start.34 = (f32[34,1,256]{2,1,0:T(1,128)S(1)}, f32[34,1,256]{2,1,0:T(1,128)S(1)}, u32[]{:S(2)}, u32[]{:S(2)}) collective-permute-start(f32[34,1,256]{2,1,0:T(1,128)S(1)} %get-tuple-element.70), channel_id=1, source_target_pairs={{1,0},{2,1},{3,2},{5,4},{6,5},{7,6},{9,8},{10,9},{11,10},{13,12},{... | collective-permute-start | bytes 104456 | tf_op jit(solution)/shard_map/ppermute | solution.py:29
  316.5 5.3 %collective-permute-start.36 = (f32[1,32,256]{2,1,0:T(8,128)S(1)}, f32[1,32,256]{2,1,0:T(8,128)S(1)}, u32[]{:S(2)}, u32[]{:S(2)}) collective-permute-start(f32[1,32,256]{2,1,0:T(8,128)S(1)} %get-tuple-element.87), channel_id=1, source_target_pairs={{4,0},{8,4},{12,8},{16,12},{20,16},{24,20},{28,24},{32,28},{36,32}... | collective-permute-start | bytes 98312 | tf_op jit(solution)/shard_map/ppermute | solution.py:29
  318.4 9.2 %collective-permute-start.37 = (f32[1,32,256]{2,1,0:T(8,128)S(1)}, f32[1,32,256]{2,1,0:T(8,128)S(1)}, u32[]{:S(2)}, u32[]{:S(2)}) collective-permute-start(f32[1,32,256]{2,1,0:T(8,128)S(1)} %get-tuple-element.86), channel_id=1, source_target_pairs={{0,4},{4,8},{8,12},{12,16},{16,20},{20,24},{24,28},{28,32},{32,36}... | collective-permute-start | bytes 98312 | tf_op jit(solution)/shard_map/ppermute | solution.py:26
  327.6 5.0 %collective-permute-start.39 = (f32[34,1,256]{2,1,0:T(1,128)S(1)}, f32[34,1,256]{2,1,0:T(1,128)S(1)}, u32[]{:S(2)}, u32[]{:S(2)}) collective-permute-start(f32[34,1,256]{2,1,0:T(1,128)S(1)} %get-tuple-element.69), channel_id=1, source_target_pairs={{0,1},{1,2},{2,3},{4,5},{5,6},{6,7},{8,9},{9,10},{10,11},{12,13},{... | collective-permute-start | bytes 104456 | tf_op jit(solution)/shard_map/ppermute | solution.py:26
  330.7 5.3 %collective-permute-start.38 = (f32[34,1,256]{2,1,0:T(1,128)S(1)}, f32[34,1,256]{2,1,0:T(1,128)S(1)}, u32[]{:S(2)}, u32[]{:S(2)}) collective-permute-start(f32[34,1,256]{2,1,0:T(1,128)S(1)} %get-tuple-element.68), channel_id=1, source_target_pairs={{1,0},{2,1},{3,2},{5,4},{6,5},{7,6},{9,8},{10,9},{11,10},{13,12},{... | collective-permute-start | bytes 104456 | tf_op jit(solution)/shard_map/ppermute | solution.py:29
  339.3 5.3 %collective-permute-start.40 = (f32[1,32,256]{2,1,0:T(8,128)S(1)}, f32[1,32,256]{2,1,0:T(8,128)S(1)}, u32[]{:S(2)}, u32[]{:S(2)}) collective-permute-start(f32[1,32,256]{2,1,0:T(8,128)S(1)} %get-tuple-element.85), channel_id=1, source_target_pairs={{4,0},{8,4},{12,8},{16,12},{20,16},{24,20},{28,24},{32,28},{36,32}... | collective-permute-start | bytes 98312 | tf_op jit(solution)/shard_map/ppermute | solution.py:29
  341.3 9.2 %collective-permute-start.41 = (f32[1,32,256]{2,1,0:T(8,128)S(1)}, f32[1,32,256]{2,1,0:T(8,128)S(1)}, u32[]{:S(2)}, u32[]{:S(2)}) collective-permute-start(f32[1,32,256]{2,1,0:T(8,128)S(1)} %get-tuple-element.84), channel_id=1, source_target_pairs={{0,4},{4,8},{8,12},{12,16},{16,20},{20,24},{24,28},{28,32},{32,36}... | collective-permute-start | bytes 98312 | tf_op jit(solution)/shard_map/ppermute | solution.py:26
  350.5 5.0 %collective-permute-start.43 = (f32[34,1,256]{2,1,0:T(1,128)S(1)}, f32[34,1,256]{2,1,0:T(1,128)S(1)}, u32[]{:S(2)}, u32[]{:S(2)}) collective-permute-start(f32[34,1,256]{2,1,0:T(1,128)S(1)} %get-tuple-element.67), channel_id=1, source_target_pairs={{0,1},{1,2},{2,3},{4,5},{5,6},{6,7},{8,9},{9,10},{10,11},{12,13},{... | collective-permute-start | bytes 104456 | tf_op jit(solution)/shard_map/ppermute | solution.py:26
  353.5 5.3 %collective-permute-start.42 = (f32[34,1,256]{2,1,0:T(1,128)S(1)}, f32[34,1,256]{2,1,0:T(1,128)S(1)}, u32[]{:S(2)}, u32[]{:S(2)}) collective-permute-start(f32[34,1,256]{2,1,0:T(1,128)S(1)} %get-tuple-element.66), channel_id=1, source_target_pairs={{1,0},{2,1},{3,2},{5,4},{6,5},{7,6},{9,8},{10,9},{11,10},{13,12},{... | collective-permute-start | bytes 104456 | tf_op jit(solution)/shard_map/ppermute | solution.py:29
  362.2 5.3 %collective-permute-start.44 = (f32[1,32,256]{2,1,0:T(8,128)S(1)}, f32[1,32,256]{2,1,0:T(8,128)S(1)}, u32[]{:S(2)}, u32[]{:S(2)}) collective-permute-start(f32[1,32,256]{2,1,0:T(8,128)S(1)} %get-tuple-element.83), channel_id=1, source_target_pairs={{4,0},{8,4},{12,8},{16,12},{20,16},{24,20},{28,24},{32,28},{36,32}... | collective-permute-start | bytes 98312 | tf_op jit(solution)/shard_map/ppermute | solution.py:29
  364.1 9.2 %collective-permute-start.45 = (f32[1,32,256]{2,1,0:T(8,128)S(1)}, f32[1,32,256]{2,1,0:T(8,128)S(1)}, u32[]{:S(2)}, u32[]{:S(2)}) collective-permute-start(f32[1,32,256]{2,1,0:T(8,128)S(1)} %get-tuple-element.82), channel_id=1, source_target_pairs={{0,4},{4,8},{8,12},{12,16},{16,20},{20,24},{24,28},{28,32},{32,36}... | collective-permute-start | bytes 98312 | tf_op jit(solution)/shard_map/ppermute | solution.py:26
  373.3 5.0 %collective-permute-start.47 = (f32[34,1,256]{2,1,0:T(1,128)S(1)}, f32[34,1,256]{2,1,0:T(1,128)S(1)}, u32[]{:S(2)}, u32[]{:S(2)}) collective-permute-start(f32[34,1,256]{2,1,0:T(1,128)S(1)} %get-tuple-element.65), channel_id=1, source_target_pairs={{0,1},{1,2},{2,3},{4,5},{5,6},{6,7},{8,9},{9,10},{10,11},{12,13},{... | collective-permute-start | bytes 104456 | tf_op jit(solution)/shard_map/ppermute | solution.py:26
  376.4 5.3 %collective-permute-start.46 = (f32[34,1,256]{2,1,0:T(1,128)S(1)}, f32[34,1,256]{2,1,0:T(1,128)S(1)}, u32[]{:S(2)}, u32[]{:S(2)}) collective-permute-start(f32[34,1,256]{2,1,0:T(1,128)S(1)} %get-tuple-element.64), channel_id=1, source_target_pairs={{1,0},{2,1},{3,2},{5,4},{6,5},{7,6},{9,8},{10,9},{11,10},{13,12},{... | collective-permute-start | bytes 104456 | tf_op jit(solution)/shard_map/ppermute | solution.py:29
  385.0 5.3 %collective-permute-start.48 = (f32[1,32,256]{2,1,0:T(8,128)S(1)}, f32[1,32,256]{2,1,0:T(8,128)S(1)}, u32[]{:S(2)}, u32[]{:S(2)}) collective-permute-start(f32[1,32,256]{2,1,0:T(8,128)S(1)} %get-tuple-element.81), channel_id=1, source_target_pairs={{4,0},{8,4},{12,8},{16,12},{20,16},{24,20},{28,24},{32,28},{36,32}... | collective-permute-start | bytes 98312 | tf_op jit(solution)/shard_map/ppermute | solution.py:29
  387.0 9.2 %collective-permute-start.49 = (f32[1,32,256]{2,1,0:T(8,128)S(1)}, f32[1,32,256]{2,1,0:T(8,128)S(1)}, u32[]{:S(2)}, u32[]{:S(2)}) collective-permute-start(f32[1,32,256]{2,1,0:T(8,128)S(1)} %get-tuple-element.80), channel_id=1, source_target_pairs={{0,4},{4,8},{8,12},{12,16},{16,20},{20,24},{24,28},{28,32},{32,36}... | collective-permute-start | bytes 98312 | tf_op jit(solution)/shard_map/ppermute | solution.py:26
  396.2 5.0 %collective-permute-start.51 = (f32[34,1,256]{2,1,0:T(1,128)S(1)}, f32[34,1,256]{2,1,0:T(1,128)S(1)}, u32[]{:S(2)}, u32[]{:S(2)}) collective-permute-start(f32[34,1,256]{2,1,0:T(1,128)S(1)} %get-tuple-element.63), channel_id=1, source_target_pairs={{0,1},{1,2},{2,3},{4,5},{5,6},{6,7},{8,9},{9,10},{10,11},{12,13},{... | collective-permute-start | bytes 104456 | tf_op jit(solution)/shard_map/ppermute | solution.py:26
  399.3 5.3 %collective-permute-start.50 = (f32[34,1,256]{2,1,0:T(1,128)S(1)}, f32[34,1,256]{2,1,0:T(1,128)S(1)}, u32[]{:S(2)}, u32[]{:S(2)}) collective-permute-start(f32[34,1,256]{2,1,0:T(1,128)S(1)} %get-tuple-element.62), channel_id=1, source_target_pairs={{1,0},{2,1},{3,2},{5,4},{6,5},{7,6},{9,8},{10,9},{11,10},{13,12},{... | collective-permute-start | bytes 104456 | tf_op jit(solution)/shard_map/ppermute | solution.py:29
  415.2 14.2 %collective-permute-start.55 = (f32[128]{0:T(128)S(1)}, f32[128]{0:T(128)S(1)}, u32[]{:S(2)}, u32[]{:S(2)}) collective-permute-start(f32[128]{0:T(128)S(1)} %get-tuple-element.105), channel_id=1, source_target_pairs={{0,1},{1,2},{2,3},{4,5},{5,6},{6,7},{8,9},{9,10},{10,11},{12,13},{... | collective-permute-start | bytes 1544 | tf_op jit(solution)/shard_map/ppermute | solution.py:18
  417.1 12.6 %collective-permute-start.54 = (f32[128]{0:T(128)S(1)}, f32[128]{0:T(128)S(1)}, u32[]{:S(2)}, u32[]{:S(2)}) collective-permute-start(f32[128]{0:T(128)S(1)} %get-tuple-element.103), channel_id=1, source_target_pairs={{1,0},{2,1},{3,2},{5,4},{6,5},{7,6},{9,8},{10,9},{11,10},{13,12},{... | collective-permute-start | bytes 1544 | tf_op jit(solution)/shard_map/ppermute | solution.py:18
  419.6 10.5 %collective-permute-start.53 = (f32[128]{0:T(128)S(1)}, f32[128]{0:T(128)S(1)}, u32[]{:S(2)}, u32[]{:S(2)}) collective-permute-start(f32[128]{0:T(128)S(1)} %get-tuple-element.104), channel_id=1, source_target_pairs={{0,4},{4,8},{8,12},{12,16},{16,20},{20,24},{24,28},{28,32},{32,36}... | collective-permute-start | bytes 1544 | tf_op jit(solution)/shard_map/ppermute | solution.py:18
  421.5 9.2 %collective-permute-start.52 = (f32[128]{0:T(128)S(1)}, f32[128]{0:T(128)S(1)}, u32[]{:S(2)}, u32[]{:S(2)}) collective-permute-start(f32[128]{0:T(128)S(1)} %get-tuple-element.102), channel_id=1, source_target_pairs={{4,0},{8,4},{12,8},{16,12},{20,16},{24,20},{28,24},{32,28},{36,32}... | collective-permute-start | bytes 1544 | tf_op jit(solution)/shard_map/ppermute | solution.py:18
  (44 other events, 401.2 us)
where the time goes:
time: 439 us; the launch traced here: 432 us
  starting transfers between devices  170 us (39%)
  other arithmetic  117 us (27%)
  waiting for transfers between devices  92.1 us (21%)
  local copies, waits for them, and re-layouts  47.7 us (11%)
    ppermute x24, starting transfers between devices, extended(): lax.ppermute(lax.slice_in_dim(block, block.shape[dim] - width, None, axis...  75.6 us
    ppermute x24, starting transfers between devices, extended(): lax.ppermute(lax.slice_in_dim(block, 0, width, axis=dim), axis, backward)  70.6 us
    ppermute x24, waiting for transfers between devices, extended(): lax.ppermute(lax.slice_in_dim(block, block.shape[dim] - width, None, axis...  54.1 us
    add x8, other arithmetic, on_device(): solid_now = solid_now + update  31.8 us
    ppermute x24, waiting for transfers between devices, extended(): lax.ppermute(lax.slice_in_dim(block, 0, width, axis=dim), axis, backward)  25.7 us
    ppermute x8, starting transfers between devices, from_behind(): lax.ppermute(value, axis, [(source, source + steps) for source in range(i...  24.3 us
    sub x4, other arithmetic, fluid_update(): jnp.maximum(face_speed, 0.0) * lower_val  17.6 us
    add x3, other arithmetic, fluid_update(): face_weight = face_diff + 0.5 * jnp.abs(face_speed)  13.5 us
  transfers between devices with their start and end apart: 56, of which 22 were waited for; matrix products, arithmetic and copies ran while one was open for 28% of the time, Pallas kernels for 0%

commit v1 on v0

v1 whole, which is shorter than its diff:
```python
import functools

import jax
import jax.numpy as jnp
from jax import lax
from jax.experimental import pallas as pl
from jax.experimental.pallas import tpu as pltpu
from jax.sharding import PartitionSpec as P

MESH = pl.DeviceIdType.MESH
SWEEPS = 8
HALO = 8
DEEP = 16
EIG_LOW = 0.02
EIG_HIGH = 2.0
HIGHEST = lax.Precision.HIGHEST
DIRS = ((1, 0), (-1, 0), (0, 1), (0, -1), (1, 1), (1, -1), (-1, 1), (-1, -1))


def cheby_coefficients(count_sweeps):
    center_eig = 0.5 * (EIG_HIGH + EIG_LOW)
    half_width = 0.5 * (EIG_HIGH - EIG_LOW)
    ratio_eig = center_eig / half_width
    damping = 1.0 / ratio_eig
    coefficients = [(0.0, 1.0 / center_eig)]
    for _ in range(1, count_sweeps):
        damping_new = 1.0 / (2.0 * ratio_eig - damping)
        coefficients.append((damping_new * damping, 2.0 * damping_new / half_width))
        damping = damping_new
    return coefficients


def iota(shape, dim):
    return lax.broadcasted_iota(jnp.int32, shape, dim)


def shift_rows(v, low, high):
    n = v.shape[0]
    row = iota(v.shape, 0)
    below = jnp.where(row == 0, low, pltpu.roll(v, 1, axis=0))
    above = jnp.where(row == n - 1, high, pltpu.roll(v, n - 1, axis=0))
    return below, above


def roll_lanes(v):
    n = v.shape[1]
    return pltpu.roll(v, 1, axis=1), pltpu.roll(v, n - 1, axis=1)


def face(u, un, a, an):
    total_u, total_a = u + un, a + an
    return total_a + jnp.maximum(total_u, 0.0), total_a - jnp.minimum(total_u, 0.0)


def conductance(k, kn):
    total = k + kn
    return 2.0 * k * kn / jnp.where(total > 0.0, total, 1.0)


def kernel(
    n_blk, n_sub,
    count_ref, t_hbm, vel_hbm, a_hbm, x_hbm, k_hbm, e_hbm, q_hbm, wall_ref, owner_ref, land_ref,
    t_out, x_out, wedge_out, wall_out,
    t0, t1, t2, ux, uy, uz, al, cf, sf,
    hxf, hyf, ysf, hxt, hyt, yst,
    xa, xb, kc, ec, qc, cs, pc, hxs, hys, yss, hxk, hyk, ysk,
    nb, fb, wk, wcf, wxa, wxb, wp, wd,
    rows_s, rows_r, wall_s, wall_r, hot_x, hot_y, slots,
    load_sem, send_sem, recv_sem,
):
    b, s = lax.axis_index("blk"), lax.axis_index("sub")
    nx, ny, nz = t0.shape
    nsz = xa.shape[2]
    coefficients = cheby_coefficients(SWEEPS)

    def inside(db, ds):
        ok = None
        for delta, at, count in ((db, b, n_blk), (ds, s, n_sub)):
            if delta:
                this = (at < count - 1) if delta > 0 else (at > 0)
                ok = this if ok is None else ok & this
        return ok

    counter = [0]
    pending = []

    class Message:
        def __init__(self, src, dst, d):
            db, ds = DIRS[d]
            self.n = counter[0]
            counter[0] += 1
            self.make = lambda: pltpu.make_async_remote_copy(
                src_ref=src, dst_ref=dst, send_sem=send_sem.at[self.n], recv_sem=recv_sem.at[self.n],
                device_id=(b + db, s + ds), device_id_type=MESH)
            self.goes, self.comes = inside(db, ds), inside(-db, -ds)

        def start(self):
            @pl.when(self.goes)
            def _():
                self.make().start()
            pending.append(self)

        def sent(self):
            @pl.when(self.goes)
            def _():
                self.make().wait_send()
            pending.remove(self)

        def arrived(self):
            @pl.when(self.comes)
            def _():
                self.make().wait_recv()

    loads = {}
    for n, (name, src, dst) in enumerate((
        ("k", k_hbm, kc), ("x", x_hbm, xa), ("e", e_hbm, ec), ("q", q_hbm, qc),
        ("a", a_hbm, al), ("uy", vel_hbm.at[1], uy), ("t", t_hbm, t0), ("ux", vel_hbm.at[0], ux), ("uz", vel_hbm.at[2], uz),
    )):
        loads[name] = pltpu.make_async_copy(src, dst, load_sem.at[n])
        loads[name].start()

    barrier = pltpu.get_barrier_semaphore()
    for db, ds in DIRS:
        @pl.when(inside(db, ds))
        def _(db=db, ds=ds):
            pl.semaphore_signal(barrier, inc=1, device_id=(b + db, s + ds), device_id_type=MESH)

    for d in range(2):
        @pl.when(jnp.logical_not(inside(-DIRS[d][0], 0)))
        def _(d=d):
            for ref in (hxf.at[d], hxt.at[d], hxk.at[d]):
                ref[...] = jnp.zeros(ref.shape, jnp.float32)
            for n in range(SWEEPS - 1):
                hxs[n, d] = jnp.zeros(hxs.shape[2:], jnp.float32)

        @pl.when(jnp.logical_not(inside(0, -DIRS[2 + d][1])))
        def _(d=d):
            for ref in (hyf.at[d], hyt.at[d], hyk.at[d]):
                ref[...] = jnp.zeros(ref.shape, jnp.float32)
            for n in range(SWEEPS - 1):
                hys[n, d] = jnp.zeros(hys.shape[2:], jnp.float32)
    for d in range(4):
        @pl.when(jnp.logical_not(inside(-DIRS[d][0], -DIRS[d][1])))
        def _(d=d):
            rows_r[d] = jnp.zeros(rows_r.shape[1:], jnp.float32)
            wall_r[d] = jnp.zeros(wall_r.shape[1:], jnp.float32)

    def near_slot(d):
        db, ds = DIRS[d]
        column = {1: 0, 0: 1, -1: 2}[ds]
        if db == 0:
            return column, slice(HALO, HALO + nx), slice(HALO, HALO + nx)
        if db > 0:
            return column, slice(nx, HALO + nx), slice(0, HALO)
        return column, slice(HALO, 2 * HALO), slice(HALO + nx, 2 * HALO + nx)

    for d in range(8):
        @pl.when(jnp.logical_not(inside(-DIRS[d][0], -DIRS[d][1])))
        def _(d=d):
            column, _, rows = near_slot(d)
            height = rows.stop - rows.start
            nb[column, :, rows, :] = jnp.zeros((DEEP, height, 128), jnp.float32)
            fb[column, rows, :] = jnp.zeros((height, 128), jnp.float32)

    near = (b > 0).astype(jnp.int32) + (b < n_blk - 1).astype(jnp.int32)
    side = (s > 0).astype(jnp.int32) + (s < n_sub - 1).astype(jnp.int32)
    pl.semaphore_wait(barrier, near + side + near * side)

    edge = (nx - 1, 0)
    solid_x = [[Message(k_hbm.at[edge[d]], hxk.at[d, 0], d), Message(x_hbm.at[edge[d]], hxk.at[d, 1], d)] for d in range(2)]
    for pair in solid_x:
        for m in pair:
            m.start()
    fluid_x = [[Message(a_hbm.at[edge[d]], hxf.at[d, 0], d), Message(vel_hbm.at[0, edge[d]], hxf.at[d, 1], d),
                Message(t_hbm.at[edge[d]], hxf.at[d, 2], d)] for d in range(2)]
    for trio in fluid_x:
        for m in trio:
            m.start()

    def pack(refs, dst):
        def body(x, _):
            for f, ref in enumerate(refs):
                dst[0, f, pl.ds(x, 1), :] = ref[x, ny - 1:ny, :]
                dst[1, f, pl.ds(x, 1), :] = ref[x, 0:1, :]
            return 0
        lax.fori_loop(0, nx, body, 0)

    loads["k"].wait()
    loads["x"].wait()
    pack((kc, xa), ysk)
    solid_y = [Message(ysk.at[d], hyk.at[d], 2 + d) for d in range(2)]
    for m in solid_y:
        m.start()
    loads["a"].wait()
    loads["uy"].wait()
    loads["t"].wait()
    pack((al, uy, t0), ysf)
    fluid_y = [Message(ysf.at[d], hyf.at[d], 2 + d) for d in range(2)]
    for m in fluid_y:
        m.start()

    loads["e"].wait()
    loads["q"].wait()

    def turn(x, _):
        tile = jnp.concatenate([ref[x, :, 0:128] for ref in (xa, kc, ec, qc)], axis=0)
        nb[1, :, pl.ds(HALO + x, 1), :] = jnp.transpose(tile)[0:DEEP].reshape(DEEP, 1, 128)
        return 0

    lax.fori_loop(0, nx, turn, 0)
    near_msgs = []
    for d in range(8):
        column, out_rows, rows = near_slot(d)
        near_msgs.append(Message(nb.at[1, :, out_rows, :], nb.at[column, :, rows, :], d))
        near_msgs[-1].start()

    lane_s = iota((ny, nsz), 1)

    def solid_coef(x, km, kp):
        k = kc[x]
        ym, yp = shift_rows(k, hyk[0, 0, pl.ds(x, 1), :], hyk[1, 0, pl.ds(x, 1), :])
        zm, zp = roll_lanes(k)
        zm, zp = jnp.where(lane_s == 0, 0.0, zm), jnp.where(lane_s == nsz - 1, 0.0, zp)
        g = [conductance(k, kn) for kn in (km, kp, ym, yp, zm, zp)]
        inverse = 1.0 / (((g[0] + g[1]) + (g[2] + g[3])) + ((g[4] + g[5]) + ec[x]))
        for n in range(6):
            cs[n, x] = g[n] * inverse
        cs[6, x] = qc[x] * inverse

    def solid_plane(n, src, dst, x, xm, xp, low, high):
        decay, gain = coefficients[n]
        v = src[x]
        ym, yp = shift_rows(v, low, high)
        zm, zp = roll_lanes(v)
        r = (cs[6, x] - v) + cs[0, x] * xm + cs[1, x] * xp + cs[2, x] * ym + cs[3, x] * yp + cs[4, x] * zm + cs[5, x] * zp
        p = gain * r if n == 0 else decay * pc[x] + gain * r
        if n < SWEEPS - 1:
            pc[x] = p
        new = v + p
        dst[x] = new
        if n < SWEEPS - 1:
            yss[n, 0, pl.ds(x, 1), :] = new[ny - 1:ny, :]
            yss[n, 1, pl.ds(x, 1), :] = new[0:1, :]

    solid_msgs = {}

    def solid_sweep(n):
        src, dst = (xa, xb) if n % 2 == 0 else (xb, xa)
        if n == 0:
            low, high = hyk.at[0, 1], hyk.at[1, 1]
            xlow, xhigh = hxk.at[0, 1], hxk.at[1, 1]
        else:
            low, high = hys.at[n - 1, 0], hys.at[n - 1, 1]
            xlow, xhigh = hxs.at[n - 1, 0], hxs.at[n - 1, 1]
            for m in solid_msgs[n - 1]:
                m.arrived()
        if n >= 2:
            for m in solid_msgs[n - 2][:2]:
                m.sent()

        def plane(x, xm, xp):
            solid_plane(n, src, dst, x, xm, xp, low[pl.ds(x, 1), :], high[pl.ds(x, 1), :])

        plane(0, xlow[...], src[1])
        plane(nx - 1, src[nx - 2], xhigh[...])
        if n < SWEEPS - 1:
            msgs = [Message(dst.at[edge[d]], hxs.at[n, d], d) for d in range(2)]
            for m in msgs:
                m.start()

        def body(x, _):
            plane(x, src[x - 1], src[x + 1])
            return 0
        lax.fori_loop(1, nx - 1, body, 0)
        if n < SWEEPS - 1:
            more = [Message(yss.at[n, d], hys.at[n, d], 2 + d) for d in range(2)]
            for m in more:
                m.start()
            solid_msgs[n] = msgs + more

    for m in solid_y:
        m.arrived()

    def body(x, _):
        solid_coef(x, kc[x - 1], kc[x + 1])
        return 0
    lax.fori_loop(1, nx - 1, body, 0)
    for pair in solid_x:
        for m in pair:
            m.arrived()
    solid_coef(0, hxk[0, 0], kc[1])
    solid_coef(nx - 1, kc[nx - 2], hxk[1, 0])
    solid_sweep(0)

    lane8, sub8 = iota((8, 128), 1), iota((8, 128), 0)
    live = jnp.where(lane8 * 8 + sub8 < count_ref[0], 1.0, 0.0)
    owner = jnp.broadcast_to(owner_ref[...], (8, 128))
    self_mask = jnp.where(owner == 0, 1.0, 0.0)
    match = jnp.where((owner == sub8 + 1) & (sub8 < 4), 1.0, 0.0)
    before = jnp.where(iota((128, 128), 0) < iota((128, 128), 1), 1.0, 0.0)
    rank = lax.dot_general(match, before, (((1,), (0,)), ((), ())), precision=HIGHEST, preferred_element_type=jnp.float32)
    place = jnp.sum(match * (rank + (sub8 * 16 + 1).astype(jnp.float32)), axis=0, keepdims=True) - 1.0
    select = jnp.where(iota((128, 128), 0).astype(jnp.float32) == place, 1.0, 0.0)
    row32 = iota((32, 256), 0)
    for n in range(8):
        cell = land_ref[n:n + 1, :]
        hot_x[:, 256 * n:256 * n + 256] = jnp.where((cell >> 5) == row32, 1.0, 0.0)
        hot_y[:, 256 * n:256 * n + 256] = jnp.where(((cell & 31) == row32) & (cell >= 0), 1.0, 0.0)

    lane_f = iota((ny, nz), 1)
    lane_t = iota((ny, 128), 1)
    mirror = 1.0 - 2.0 * live
    source = 2.0 * live * wall_ref[...]

    def columns(v, x):
        return jnp.concatenate([pltpu.roll(v, lax.rem(128 - (x * 4 + j), 128), axis=1) for j in range(4)], axis=0)

    def rows_of(v, x, into):
        for j in range(4):
            into = jnp.where(lane8 == x * 4 + j, jnp.broadcast_to(v[8 * j:8 * j + 8, 0:1], (8, 128)), into)
        return into

    def fluid_coef(x, am, ap, um, up, film):
        a, u = al[x], ux[x]
        p_xm, q_xm = face(u, um, a, am)
        p_xp, q_xp = face(u, up, a, ap)
        ym, yp = shift_rows(a, hyf[0, 0, pl.ds(x, 1), :], hyf[1, 0, pl.ds(x, 1), :])
        u = uy[x]
        vm, vp = shift_rows(u, hyf[0, 1, pl.ds(x, 1), :], hyf[1, 1, pl.ds(x, 1), :])
        p_ym, q_ym = face(u, vm, a, ym)
        p_yp, q_yp = face(u, vp, a, yp)
        zm, zp = roll_lanes(a)
        u = uz[x]
        vm, vp = roll_lanes(u)
        low, high = lane_f == 0, lane_f == nz - 1
        p_zm, q_zm = face(u, jnp.where(low, -u, vm), a, jnp.where(low, a, zm))
        p_zp, q_zp = face(u, jnp.where(high, u, vp), a, jnp.where(high, a, zp))
        away = ((q_xm + p_xp) + (q_ym + p_yp)) + (q_zm + p_zp)
        toward = ((p_xm + q_xp) + (p_ym + q_yp)) + (p_zm + q_zp)
        scale = 1.6 / (away + toward)
        cf[0, x] = p_xm * scale
        cf[1, x] = q_xp * scale
        cf[2, x] = p_ym * scale
        cf[3, x] = q_yp * scale
        below = p_zm * scale
        cf[4, x] = jnp.where(low, 0.0, below)
        cf[5, x] = jnp.where(high, 0.0, q_zp * scale)
        centre = 1.0 - away * scale
        first = lane_t == 0
        wall = jnp.where(first, below[:, 0:128], 0.0)
        sf[x] = wall * columns(source, x)
        cf[6, x] = centre
        cf[6, x, :, 0:128] = centre[:, 0:128] + wall * columns(mirror, x)
        return rows_of(a, x, film)

    def fluid_plane(src, dst, x, tm, tp, low, high):
        t = src[x]
        ym, yp = shift_rows(t, low, high)
        zm, zp = roll_lanes(t)
        new = cf[6, x] * t + cf[0, x] * tm + cf[1, x] * tp + cf[2, x] * ym + cf[3, x] * yp + cf[4, x] * zm + cf[5, x] * zp
        first = new[:, 0:128] + sf[x]
        new = jnp.concatenate([first, new[:, 128:]], axis=1) if nz > 128 else first
        dst[x] = new
        return new

    for name in ("ux", "uz"):
        loads[name].wait()
    for m in fluid_y:
        m.arrived()

    def body(x, film):
        return fluid_coef(x, al[x - 1], al[x + 1], ux[x - 1], ux[x + 1], film)
    film = lax.fori_loop(1, nx - 1, body, jnp.zeros((8, 128), jnp.float32))
    for trio in fluid_x:
        for m in trio:
            m.arrived()
    film = fluid_coef(0, hxf[0, 0], al[1], hxf[0, 1], ux[1], film)
    film = fluid_coef(nx - 1, al[nx - 2], hxf[1, 0], ux[nx - 2], hxf[1, 1], film)
    film = 2.0 * film * live

    def first_plane(x, tm, tp):
        new = fluid_plane(t0, t1, x, tm, tp, hyf[0, 2, pl.ds(x, 1), :], hyf[1, 2, pl.ds(x, 1), :])
        for d, at in ((0, ny - 1), (1, 0)):
            yst[d, pl.ds(x, 1), :] = new[at:at + 1, :]

    first_plane(0, hxf[0, 2], t0[1])
    first_plane(nx - 1, t0[nx - 2], hxf[1, 2])
    t_msgs = [Message(t1.at[edge[d]], hxt.at[d], d) for d in range(2)]
    for m in t_msgs:
        m.start()

    def body(x, _):
        first_plane(x, t0[x - 1], t0[x + 1])
        return 0
    lax.fori_loop(1, nx - 1, body, 0)
    more = [Message(yst.at[d], hyt.at[d], 2 + d) for d in range(2)]
    for m in more:
        m.start()
    t_msgs += more

    solid_sweep(1)

    for m in t_msgs:
        m.arrived()

    def second_plane(x, tm, tp, gas):
        new = fluid_plane(t1, t2, x, tm, tp, hyt[0, pl.ds(x, 1), :], hyt[1, pl.ds(x, 1), :])
        return rows_of(new[:, 0:128], x, gas)

    gas = second_plane(0, hxt[0], t1[1], jnp.zeros((8, 128), jnp.float32))
    gas = second_plane(nx - 1, t1[nx - 2], hxt[1], gas)
    gas = lax.fori_loop(1, nx - 1, lambda x, g: second_plane(x, t1[x - 1], t1[x + 1], g), gas)
    t_store = pltpu.make_async_copy(t2, t_out, load_sem.at[9])
    t_store.start()

    def take(v):
        return lax.dot_general(v, select, (((1,), (1,)), ((), ())), precision=HIGHEST, preferred_element_type=jnp.float32)

    rows_s[...] = take(jnp.concatenate([film, gas], axis=0))
    row_msgs = [Message(rows_s, rows_r.at[d], d) for d in range(4)]
    for m in row_msgs:
        m.start()

    solid_sweep(2)

    for m in near_msgs:
        m.arrived()
    lane_w = iota((nx + 2 * HALO, 128), 1)

    def widen(left, mid, right, f):
        left = pltpu.roll(left, (128 - 32 * f - 24) % 128, axis=1)
        mid = pltpu.roll(mid, (128 + HALO - 32 * f) % 128, axis=1)
        right = pltpu.roll(right, (128 + 40 - 32 * f) % 128, axis=1)
        return jnp.where(lane_w < HALO, left, jnp.where(lane_w < HALO + ny, mid, jnp.where(lane_w < 2 * HALO + ny, right, 0.0)))

    def near_field(z, f):
        return widen(nb[0, z], nb[1, z], nb[2, z], f)

    def body(z, _):
        wk[z] = near_field(z, 1)
        wxa[z] = near_field(z, 0)
        return 0
    lax.fori_loop(0, DEEP, body, 0)

    def shift_all(v):
        n = v.shape[0]
        return [pltpu.roll(v, 1, axis=0), pltpu.roll(v, n - 1, axis=0), pltpu.roll(v, 1, axis=1), pltpu.roll(v, 127, axis=1)]

    def body(z, _):
        k = wk[z]
        under = wk[jnp.maximum(z - 1, 0)] * (z > 0).astype(jnp.float32)
        over = wk[jnp.minimum(z + 1, DEEP - 1)] * (z < DEEP - 1).astype(jnp.float32)
        g = [conductance(k, kn) for kn in shift_all(k) + [under, over]]
        diag = ((g[0] + g[1]) + (g[2] + g[3])) + ((g[4] + g[5]) + near_field(z, 2))
        diag = jnp.where(diag > 0.0, diag, 1.0)
        inverse = 1.0 / diag
        for n in range(6):
            wcf[n, z] = g[n] * inverse
        wcf[6, z] = near_field(z, 3) * inverse

        @pl.when(z == 0)
        def _():
            wd[...] = diag
        return 0
    lax.fori_loop(0, DEEP, body, 0)

    for m in row_msgs:
        m.arrived()

    def bands(refs):
        total = None
        for band, ref in enumerate(refs):
            v = ref[...]
            lane = iota(v.shape, 1)
            v = jnp.where((lane >= 16 * band) & (lane < 16 * band + 16), v, 0.0)
            total = v if total is None else total + v
        return total

    came = bands([rows_r.at[d] for d in range(4)])
    film_in = jnp.concatenate([film * self_mask, came[0:8]], axis=1)
    heat_in = film_in * jnp.concatenate([gas, came[8:16]], axis=1)
    weighed = jnp.concatenate(
        [jnp.concatenate([hot_y[:, 256 * n:256 * n + 256] * v[n:n + 1, :] for n in range(8)], axis=1) for v in (film_in, heat_in)]
        + [jnp.zeros((64, 2048), jnp.float32)], axis=0)
    fb[1, HALO:HALO + nx, :] = lax.dot_general(
        hot_x[...], weighed, (((1,), (1,)), ((), ())), precision=HIGHEST, preferred_element_type=jnp.float32)
    film_msgs = []
    for d in range(8):
        column, out_rows, rows = near_slot(d)
        film_msgs.append(Message(fb.at[1, out_rows, :], fb.at[column, rows, :], d))
        film_msgs[-1].start()

    solid_sweep(3)

    for m in film_msgs:
        m.arrived()
    wide = [widen(fb[0], fb[1], fb[2], f) for f in range(2)]
    diag = wd[...]
    inverse = 1.0 / (diag + wide[0])
    wcf[6, 0] = (wcf[6, 0] * diag + wide[1]) * inverse
    for n in range(6):
        wcf[n, 0] = wcf[n, 0] * diag * inverse

    for n in range(SWEEPS):
        decay, gain = coefficients[n]
        src, dst = (wxa, wxb) if n % 2 == 0 else (wxb, wxa)

        def body(z, _, n=n, decay=decay, gain=gain, src=src, dst=dst):
            v = src[z]
            near_v = shift_all(v) + [src[jnp.maximum(z - 1, 0)], src[z + 1]]
            r = wcf[6, z] - v
            for i in range(6):
                r = r + wcf[i, z] * near_v[i]
            p = gain * r if n == 0 else decay * wp[z] + gain * r
            wp[z] = p
            dst[z] = v + p
            return 0
        lax.fori_loop(0, DEEP - 1 - n, body, 0)

    solved = wxa if SWEEPS % 2 == 0 else wxb
    for z in range(HALO):
        wedge_out[z] = pltpu.roll(solved[z, HALO:HALO + nx, :], 128 - HALO, axis=1)

    surface = wedge_out[0][:, 0:32]
    picked = lax.dot_general(surface, hot_y[...], (((1,), (0,)), ((), ())), precision=HIGHEST, preferred_element_type=jnp.float32)
    picked = jnp.sum(picked * hot_x[...], axis=0, keepdims=True)
    for n in range(8):
        slots[n:n + 1, :] = picked[:, 256 * n:256 * n + 256]
    wall_s[...] = slots[:, 128:256]
    wall_msgs = [Message(wall_s, wall_r.at[d], d) for d in range(4)]
    for m in wall_msgs:
        m.start()

    solid_sweep(4)

    for m in wall_msgs:
        m.arrived()
    back = bands([wall_r.at[d] for d in (1, 0, 3, 2)])
    spread = lax.dot_general(back, select, (((1,), (0,)), ((), ())), precision=HIGHEST, preferred_element_type=jnp.float32)
    wall_out[...] = (self_mask * slots[:, 0:128] + spread) * live

    for n in range(5, SWEEPS):
        solid_sweep(n)
    x_store = pltpu.make_async_copy(xa, x_out, load_sem.at[10])
    x_store.start()
    t_store.wait()
    x_store.wait()
    for m in list(pending):
        m.sent()


N_MESSAGES = 4 + 6 + 2 + 2 + 8 + 4 * (SWEEPS - 1) + 4 + 4 + 8 + 4


def on_device(n_blk, n_sub, fluid_temp, velocity, eddy_diff, wall_prev, row_count, owner_table, landing_cell, solid_temp, conductivity, sink, heat_source):
    nx, ny, nz = fluid_temp.shape
    nsz = solid_temp.shape[2]
    f32 = jnp.float32
    wall_rows = wall_prev.reshape(128, 8).T
    landing = jnp.pad(landing_cell.reshape(192, 8).T, ((0, 0), (0, 64)), constant_values=-1)
    any_space = pl.BlockSpec(memory_space=pl.ANY)
    vmem_space = pl.BlockSpec(memory_space=pltpu.VMEM)

    def vmem(*shape):
        return pltpu.VMEM(shape, f32)

    wide = nx + 2 * HALO
    fluid_new, solid_bulk, wedge, wall_rows_new = pl.pallas_call(
        functools.partial(kernel, n_blk, n_sub),
        out_shape=(
            jax.ShapeDtypeStruct((nx, ny, nz), f32),
            jax.ShapeDtypeStruct((nx, ny, nsz), f32),
            jax.ShapeDtypeStruct((HALO, nx, 128), f32),
            jax.ShapeDtypeStruct((8, 128), f32),
        ),
        in_specs=[pl.BlockSpec(memory_space=pltpu.SMEM)] + [any_space] * 7 + [vmem_space] * 3,
        out_specs=(any_space, any_space, vmem_space, vmem_space),
        scratch_shapes=[
            vmem(nx, ny, nz), vmem(nx, ny, nz), vmem(nx, ny, nz),
            vmem(nx, ny, nz), vmem(nx, ny, nz), vmem(nx, ny, nz), vmem(nx, ny, nz),
            vmem(7, nx, ny, nz), vmem(nx, ny, 128),
            vmem(2, 3, ny, nz), vmem(2, 3, nx, nz), vmem(2, 3, nx, nz),
            vmem(2, ny, nz), vmem(2, nx, nz), vmem(2, nx, nz),
            vmem(nx, ny, nsz), vmem(nx, ny, nsz), vmem(nx, ny, nsz), vmem(nx, ny, nsz), vmem(nx, ny, nsz),
            vmem(7, nx, ny, nsz), vmem(nx, ny, nsz),
            vmem(SWEEPS - 1, 2, ny, nsz), vmem(SWEEPS - 1, 2, nx, nsz), vmem(SWEEPS - 1, 2, nx, nsz),
            vmem(2, 2, ny, nsz), vmem(2, 2, nx, nsz), vmem(2, 2, nx, nsz),
            vmem(3, DEEP, wide, 128), vmem(3, wide, 128),
            vmem(DEEP, wide, 128), vmem(7, DEEP, wide, 128),
            vmem(DEEP, wide, 128), vmem(DEEP, wide, 128), vmem(DEEP, wide, 128), vmem(wide, 128),
            vmem(16, 128), vmem(4, 16, 128), vmem(8, 128), vmem(4, 8, 128),
            vmem(32, 2048), vmem(32, 2048), vmem(8, 256),
            pltpu.SemaphoreType.DMA((11,)),
            pltpu.SemaphoreType.DMA((N_MESSAGES,)),
            pltpu.SemaphoreType.DMA((N_MESSAGES,)),
        ],
        compiler_params=pltpu.CompilerParams(
            collective_id=0, has_side_effects=True, vmem_limit_bytes=60 * 1024 * 1024
        ),
    )(row_count, fluid_temp, velocity, eddy_diff, solid_temp, conductivity, sink, heat_source, wall_rows, owner_table, landing)
    near_wall = jnp.pad(wedge[:, :, 0:ny].transpose(1, 2, 0), ((0, 0), (0, 0), (0, nsz - HALO)))
    depth = lax.broadcasted_iota(jnp.int32, solid_bulk.shape, 2)
    solid_new = jnp.where(depth < HALO, near_wall, solid_bulk)
    return fluid_new, solid_new, wall_rows_new.T.reshape(-1)


def solution(mesh):
    return jax.shard_map(
        functools.partial(on_device, mesh.shape["blk"], mesh.shape["sub"]),
        mesh=mesh,
        in_specs=(
            P("blk", "sub", None),
            P(None, "blk", "sub", None),
            P("blk", "sub", None),
            P(("blk", "sub")),
            P(("blk", "sub")),
            P(("blk", "sub"), None),
            P(("blk", "sub"), None),
            P("blk", "sub", None),
            P("blk", "sub", None),
            P("blk", "sub", None),
            P("blk", "sub", None),
        ),
        out_specs=(P("blk", "sub", None), P("blk", "sub", None), P(("blk", "sub"))),
        check_vma=False,
    )
```

time: 439 us -> 110 us (0.25); the launches traced: 432 us -> 109 us
  starting transfers between devices: 170 us -> 0 us
  other arithmetic: 117 us -> 4.74 us
  waiting for transfers between devices: 92.1 us -> 0 us
  Pallas kernels: 0 us -> 88.8 us
  local copies, waits for them, and re-layouts: 47.7 us -> 14.2 us
    ppermute x56 -> x0, starting transfers between devices: 170 us -> none  [the longest x24 75.6 us: extended(): lax.ppermute(lax.slice_in_dim(block, block.shape[dim] - width, None, axis...]
    ppermute x56 -> x0, waiting for transfers between devices: 92.1 us -> none  [the longest x24 54.1 us: extended(): lax.ppermute(lax.slice_in_dim(block, block.shape[dim] - width, None, axis...]
    pallas_call x0 -> x1, Pallas kernels: none -> 88.8 us  [on_device(): pl.pallas_call(functools.partial(kernel, n_blk, n_sub), out_shape=(jax.Sh...]
    add x15 -> x0, other arithmetic: 55.3 us -> none  [the longest x8 31.8 us: on_device(): solid_now = solid_now + update]
    scatter-add x2 -> x0, other arithmetic: 22.8 us -> none  [the longest x1 11.5 us: on_device(): jax.ops.segment_sum(film_in * gas_in, landing, num_segments=solid_x * sol...]
    sub x8 -> x0, other arithmetic: 20.2 us -> none  [the longest x4 17.6 us: fluid_update(): jnp.maximum(face_speed, 0.0) * lower_val]
    slice x20 -> x0, local copies, waits for them, and re-layouts: 10.3 us -> none  [the longest x4 4.31 us: extended(): lax.slice_in_dim(block, 0, width, axis=dim)]
    concatenate x1 -> x0, other arithmetic: 7.94 us -> none  [extended(): block = jnp.concatenate([low, block, high], axis=dim)]
  transfers between devices with their start and end apart: 56 -> 0, of which waited for: 22 -> 0; matrix products, arithmetic and copies ran while one was open for 28% -> 0% of each run, Pallas kernels for 0% -> 0%
where the time goes in v1:
time: 110 us; the launch traced here: 109 us
  Pallas kernels  88.8 us (81%)
  local copies, waits for them, and re-layouts  14.2 us (13%)
  other arithmetic  4.74 us (4%)
  between operations  1.33 us (1%)
    pallas_call x1, Pallas kernels, on_device(): pl.pallas_call(functools.partial(kernel, n_blk, n_sub), out_shape=(jax.Sh...  88.8 us
    unnamed x8, local copies, waits for them, and re-layouts  5.85 us
    pallas_call x1, local copies, waits for them, and re-layouts, on_device(): pl.pallas_call(functools.partial(kernel, n_blk, n_sub), out_shape=(jax.Sh...  5.37 us
    select_n x1, other arithmetic, on_device(): solid_new = jnp.where(depth < HALO, near_wall, solid_bulk)  4.02 us

profile of v1, /device:TPU:5, one launch (start us, length us, event | category | flops | bytes accessed | tf_op | source)
XLA Modules:
  0.0 109.1 jit_solution(17370635950016243645)
XLA Ops:
  0.6 0.7 reduce
  1.3 0.1 reshape.16
  1.5 0.1 copy.17
  1.5 0.6 pad.8.land_ref
  2.1 0.8 reshape.15
  2.9 0.7 copy.16
  4.2 88.8 %shard_map.130 = (f32[32,32,512]{2,1,0:T(8,128)}, f32[32,32,256]{2,1,0:T(8,128)}, f32[8,32,128]{2,1,0:T(8,128)}, f32[8,128]{1,0:T(8,128)}) custom-call(s32[1]{0:T(128)S(6)} %copy.22.count_ref, f32[32,32,512]{2,1,0:T(8,128)} %t_hbm.1, f32[3,32,32,512]{3,2,1,0:T(8,128)} %vel_hbm.1, f32[32,32,512]{2,1,0:T(8,128)} %a_hbm.1, f32[32,32,256]{2,1,0:T(8,128)} %x_hbm.1, ...), custom_call_target="tpu_custom_call" | custom-call | tf_op jit(solution)/shard_map/pallas_call | solution.py:568
  93.0 0.0 copy-start.1
  93.0 5.4 %copy.18 = f32[32,32,256]{1,0,2:T(8,128)} copy(f32[32,32,256]{2,1,0:T(8,128)} %get-tuple-element.9) | data formatting | bytes 2097152 | tf_op jit(solution)/shard_map/pallas_call | solution.py:568
  98.4 0.0 copy-done.1
  98.4 4.0 %pad_select_fusion = f32[32,32,256]{1,0,2:T(8,128)} fusion(f32[32,32,256]{1,0,2:T(8,128)} %copy.18, f32[32,32,8]{1,0,2:T(8,128)S(1)} %slice_bitcast_fusion, pred[256]{0:T(512)(128)(4,1)S(1)} %iota_compare_fusion), kind=kLoop, calls=%fused_computation | loop fusion | flops 262144 | bytes 2130176 | tf_op jit(solution)/shard_map/jit(_where)/select_n | solution.py:603
  102.4 0.0 copy-start.2
  102.4 0.0 copy-start
  102.4 4.5 %copy.20 = f32[32,32,256]{2,1,0:T(8,128)} copy(f32[32,32,256]{1,0,2:T(8,128)} %pad_select_fusion) | data formatting | bytes 2097152
  107.0 0.0 copy-done.2
  107.0 0.1 copy.19
  107.1 0.7 reshape.17
  107.7 0.0 copy-done
  107.7 1.3 %copy.23 = f32[32,32,512]{2,1,0:T(8,128)} copy(f32[32,32,512]{2,1,0:T(8,128)S(1)} %copy-done) | data formatting | bytes 4194304
  (2 shorter events, 0.0 us)
Async XLA Ops:
  93.0 5.4 %copy-start.1 = (f32[8,32,128]{2,1,0:T(8,128)S(1)}, f32[8,32,128]{2,1,0:T(8,128)}, u32[]{:S(2)}) copy-start(f32[8,32,128]{2,1,0:T(8,128)} %get-tuple-element.8) | copy-start | bytes 393220
  102.4 4.5 %copy-start.2 = (f32[8,128]{1,0:T(8,128)S(1)}, f32[8,128]{1,0:T(8,128)}, u32[]{:S(2)}) copy-start(f32[8,128]{1,0:T(8,128)} %get-tuple-element.10) | copy-start | bytes 12292
  102.4 5.3 %copy-start = (f32[32,32,512]{2,1,0:T(8,128)S(1)}, f32[32,32,512]{2,1,0:T(8,128)}, u32[]{:S(2)}) copy-start(f32[32,32,512]{2,1,0:T(8,128)} %get-tuple-element.20) | copy-start | bytes 6291460

commit v2 on v1

v2 whole, which is shorter than its diff:
```python
import functools

import jax
import jax.numpy as jnp
from jax import lax
from jax.experimental import pallas as pl
from jax.experimental.pallas import tpu as pltpu
from jax.sharding import PartitionSpec as P

MESH = pl.DeviceIdType.MESH
SWEEPS = 8
HALO = 8
DEEP = 16
TOP = 8
EIG_LOW = 0.02
EIG_HIGH = 2.0
HIGHEST = lax.Precision.HIGHEST
DIRS = ((1, 0), (-1, 0), (0, 1), (0, -1), (1, 1), (1, -1), (-1, 1), (-1, -1))


def cheby_coefficients(count_sweeps):
    center_eig = 0.5 * (EIG_HIGH + EIG_LOW)
    half_width = 0.5 * (EIG_HIGH - EIG_LOW)
    ratio_eig = center_eig / half_width
    damping = 1.0 / ratio_eig
    coefficients = [(0.0, 1.0 / center_eig)]
    for _ in range(1, count_sweeps):
        damping_new = 1.0 / (2.0 * ratio_eig - damping)
        coefficients.append((damping_new * damping, 2.0 * damping_new / half_width))
        damping = damping_new
    return coefficients


def iota(shape, dim):
    return lax.broadcasted_iota(jnp.int32, shape, dim)


def lane_shifts(v):
    lane = iota(v[0].shape, 1)
    low, high = [pltpu.roll(c, 1, axis=1) for c in v], [pltpu.roll(c, 127, axis=1) for c in v]
    below = [low[0]] + [jnp.where(lane == 0, low[c - 1], low[c]) for c in range(1, len(v))]
    above = [jnp.where(lane == 127, high[c + 1], high[c]) for c in range(len(v) - 1)] + [high[-1]]
    return below, above


def face(u, un, a, an):
    total_u, total_a = u + un, a + an
    return total_a + jnp.maximum(total_u, 0.0), total_a - jnp.minimum(total_u, 0.0)


def within(k, kn):
    return 2.0 * k * kn / (k + kn)


def conductance(k, kn):
    total = k + kn
    return 2.0 * k * kn / jnp.where(total > 0.0, total, 1.0)


def kernel(
    n_blk, n_sub,
    count_ref, t_hbm, vel_hbm, a_hbm, x_hbm, k_hbm, e_hbm, q_hbm, wall_ref, owner_ref, land_ref,
    t_out, x_out, wall_out,
    t0, t1, t2, ux, uy, uz, al, cf, sf,
    xa, xb, kc, ec, qc, cs,
    nb, fb, wk, wcf, wxa, wxb, wp, wd, wz,
    rows_s, rows_r, wall_s, wall_r, hot_x, hot_y, slots,
    load_sem, send_sem, recv_sem,
):
    b, s = lax.axis_index("blk"), lax.axis_index("sub")
    nx, ny, _ = t_hbm.shape
    fluid_chunks, solid_chunks = t0.shape[0], xa.shape[0]
    end = TOP + ny
    own_rows, own_planes = slice(TOP, end), slice(1, 1 + nx)
    coefficients = cheby_coefficients(SWEEPS)

    def inside(db, ds):
        ok = None
        for delta, at, count in ((db, b, n_blk), (ds, s, n_sub)):
            if delta:
                this = (at < count - 1) if delta > 0 else (at > 0)
                ok = this if ok is None else ok & this
        return ok

    counter = [0]
    pending = []

    class Message:
        def __init__(self, src, dst, d):
            db, ds = DIRS[d]
            self.n = counter[0]
            counter[0] += 1
            self.make = lambda: pltpu.make_async_remote_copy(
                src_ref=src, dst_ref=dst, send_sem=send_sem.at[self.n], recv_sem=recv_sem.at[self.n],
                device_id=(b + db, s + ds), device_id_type=MESH)
            self.goes, self.comes = inside(db, ds), inside(-db, -ds)

        def start(self):
            @pl.when(self.goes)
            def _():
                self.make().start()
            pending.append(self)
            return self

        def sent(self):
            @pl.when(self.goes)
            def _():
                self.make().wait_send()
            pending.remove(self)

        def arrived(self):
            @pl.when(self.comes)
            def _():
                self.make().wait_recv()

    def send_planes(ref):
        return [Message(ref.at[:, nx if d == 0 else 1, own_rows, :], ref.at[:, 0 if d == 0 else nx + 1, own_rows, :], d).start()
                for d in range(2)]

    def send_rows(ref):
        return [Message(ref.at[:, own_planes, end - 1:end, :], ref.at[:, own_planes, TOP - 1:TOP, :], 2).start(),
                Message(ref.at[:, own_planes, TOP:TOP + 1, :], ref.at[:, own_planes, end:end + 1, :], 3).start()]

    def arrived(messages):
        for m in messages:
            m.arrived()

    loads = {}
    for name, src, dst in (
        ("k", k_hbm, kc), ("x", x_hbm, xa), ("a", a_hbm, al), ("ux", vel_hbm.at[0], ux), ("t", t_hbm, t0), ("uy", vel_hbm.at[1], uy),
        ("e", e_hbm, ec), ("q", q_hbm, qc), ("uz", vel_hbm.at[2], uz),
    ):
        planes = own_planes if dst.shape[1] > nx else slice(0, nx)
        rows = own_rows if dst.shape[2] > ny else slice(0, ny)
        loads[name] = []
        for c in range(dst.shape[0]):
            n = sum(len(v) for v in loads.values())
            copy = pltpu.make_async_copy(src.at[:, :, 128 * c:128 * c + 128], dst.at[c, planes, rows, :], load_sem.at[n])
            copy.start()
            loads[name].append(copy)

    def loaded(*names):
        for name in names:
            for copy in loads[name]:
                copy.wait()

    barrier = pltpu.get_barrier_semaphore()
    for db, ds in DIRS:
        @pl.when(inside(db, ds))
        def _(db=db, ds=ds):
            pl.semaphore_signal(barrier, inc=1, device_id=(b + db, s + ds), device_id_type=MESH)

    def clear(ref, *where):
        ref[where] = jnp.zeros(ref.at[where].shape, jnp.float32)

    for d in range(2):
        @pl.when(jnp.logical_not(inside(-DIRS[d][0], 0)))
        def _(d=d):
            for ref in (t0, t1, al, ux, xa, xb, kc):
                rows = own_rows if ref.shape[2] > ny else slice(0, ny)
                for c in range(ref.shape[0]):
                    clear(ref, c, 0 if d == 0 else nx + 1, rows, slice(None))

        @pl.when(jnp.logical_not(inside(0, -DIRS[2 + d][1])))
        def _(d=d):
            row = TOP - 1 if d == 0 else end

            def body(x, _):
                for ref in (t0, t1, al, uy, xa, xb, kc):
                    for c in range(ref.shape[0]):
                        clear(ref, c, x + (1 if ref.shape[1] > nx else 0), slice(row, row + 1), slice(None))
                return 0
            lax.fori_loop(0, nx, body, 0)
    for d in range(4):
        @pl.when(jnp.logical_not(inside(-DIRS[d][0], -DIRS[d][1])))
        def _(d=d):
            rows_r[d] = jnp.zeros(rows_r.shape[1:], jnp.float32)
            wall_r[d] = jnp.zeros(wall_r.shape[1:], jnp.float32)

    def near_slot(d):
        db, ds = DIRS[d]
        column = {1: 0, 0: 1, -1: 2}[ds]
        if db == 0:
            return column, slice(HALO, HALO + nx), slice(HALO, HALO + nx)
        if db > 0:
            return column, slice(nx, HALO + nx), slice(0, HALO)
        return column, slice(HALO, 2 * HALO), slice(HALO + nx, 2 * HALO + nx)

    for d in range(8):
        @pl.when(jnp.logical_not(inside(-DIRS[d][0], -DIRS[d][1])))
        def _(d=d):
            column, _, rows = near_slot(d)
            height = rows.stop - rows.start
            nb[column, :, rows, :] = jnp.zeros((DEEP, height, 128), jnp.float32)
            fb[column, rows, :] = jnp.zeros((height, 128), jnp.float32)

    near = (b > 0).astype(jnp.int32) + (b < n_blk - 1).astype(jnp.int32)
    side = (s > 0).astype(jnp.int32) + (s < n_sub - 1).astype(jnp.int32)
    pl.semaphore_wait(barrier, near + side + near * side)

    loaded("k", "x")
    k_x, x_x = send_planes(kc), send_planes(xa)
    k_y, x_y = send_rows(kc), send_rows(xa)
    loaded("a", "ux", "t")
    a_x = send_planes(al)
    u_x = [Message(ux.at[:, nx if d == 0 else 1], ux.at[:, 0 if d == 0 else nx + 1], d).start() for d in range(2)]
    t_x = send_planes(t0)
    loaded("uy")
    a_y, t_y = send_rows(al), send_rows(t0)
    u_y = [Message(uy.at[:, :, end - 1:end, :], uy.at[:, :, TOP - 1:TOP, :], 2).start(),
           Message(uy.at[:, :, TOP:TOP + 1, :], uy.at[:, :, end:end + 1, :], 3).start()]

    loaded("e", "q")

    def turn(x, _):
        tile = jnp.concatenate([xa[0, x + 1, own_rows, :], kc[0, x + 1, own_rows, :], ec[0, x], qc[0, x]], axis=0)
        nb[1, :, pl.ds(HALO + x, 1), :] = jnp.transpose(tile)[0:DEEP].reshape(DEEP, 1, 128)
        return 0

    lax.fori_loop(0, nx, turn, 0, unroll=2)
    near_msgs = []
    for d in range(8):
        column, out_rows, rows = near_slot(d)
        near_msgs.append(Message(nb.at[1, :, out_rows, :], nb.at[column, :, rows, :], d).start())

    lane = iota((ny, 128), 1)

    def solid_coef(x, count):
        k = [[kc[c, x + i, own_rows, :] for c in range(solid_chunks)] for i in range(count + 2)]
        out = []
        for i in range(count):
            here, under, over = k[i + 1], k[i], k[i + 2]
            zm, _ = lane_shifts(here)
            gz = [within(here[c], zm[c]) for c in range(solid_chunks)]
            gz[0] = jnp.where(lane == 0, 0.0, gz[0])
            _, gz_up = lane_shifts(gz)
            gz_up[-1] = jnp.where(lane == 127, 0.0, gz_up[-1])
            for c in range(solid_chunks):
                g = [within(here[c], under[c]), within(here[c], over[c]),
                     within(here[c], kc[c, x + i + 1, TOP - 1:end - 1, :]), within(here[c], kc[c, x + i + 1, TOP + 1:end + 1, :]),
                     gz[c], gz_up[c]]
                inverse = 1.0 / (((g[0] + g[1]) + (g[2] + g[3])) + ((g[4] + g[5]) + ec[c, x + i]))
                out.append((c, x + i, [v * inverse for v in g] + [qc[c, x + i] * inverse]))
        for c, at, values in out:
            for n in range(7):
                cs[n, c, at] = values[n]

    def solid_planes(n, src, dst, x, count):
        decay, gain = coefficients[n]
        v = [[src[c, x + i, own_rows, :] for c in range(solid_chunks)] for i in range(count + 2)]
        out = []
        for i in range(count):
            zm, zp = lane_shifts(v[i + 1])
            for c in range(solid_chunks):
                at = x + i
                r = ((cs[0, c, at] * v[i][c] + cs[1, c, at] * v[i + 2][c])
                     + (cs[2, c, at] * src[c, at + 1, TOP - 1:end - 1, :] + cs[3, c, at] * src[c, at + 1, TOP + 1:end + 1, :]))
                r = r + (cs[4, c, at] * zm[c] + cs[5, c, at] * zp[c]) + cs[6, c, at]
                new = (1.0 + decay - gain) * v[i + 1][c] + gain * r
                if n > 0:
                    new = new - decay * dst[c, at + 1, own_rows, :]
                if n == SWEEPS - 1 and c == 0:
                    new = jnp.where(lane < HALO, wz[at], new)
                out.append((c, at, new))
        for c, at, new in out:
            dst[c, at + 1, own_rows, :] = new

    pairs = (nx - 2) // 2

    def solid_sweep(n, waits):
        src, dst = (xa, xb) if n % 2 == 0 else (xb, xa)
        arrived(waits)
        for m in list(solid_sends):
            if m[0] <= n - 2:
                m[1].sent()
                solid_sends.remove(m)
        solid_planes(n, src, dst, 0, 1)
        solid_planes(n, src, dst, nx - 1, 1)
        msgs = send_planes(dst) if n < SWEEPS - 1 else []

        def body(i, _):
            solid_planes(n, src, dst, 1 + 2 * i, 2)
            return 0
        lax.fori_loop(0, pairs, body, 0)
        if n < SWEEPS - 1:
            msgs += send_rows(dst)
        solid_sends.extend((n, m) for m in msgs)
        return msgs

    solid_sends = [(-1, m) for m in x_x + x_y]

    arrived(k_y)

    def body(i, _):
        solid_coef(1 + 2 * i, 2)
        return 0
    lax.fori_loop(0, pairs, body, 0)
    arrived(k_x)
    solid_coef(0, 1)
    solid_coef(nx - 1, 1)
    solid_msgs = solid_sweep(0, x_x + x_y)

    lane8, sub8 = iota((8, 128), 1), iota((8, 128), 0)
    live = jnp.where(lane8 * 8 + sub8 < count_ref[0], 1.0, 0.0)
    owner = jnp.broadcast_to(owner_ref[...], (8, 128))
    self_mask = jnp.where(owner == 0, 1.0, 0.0)
    match = jnp.where((owner == sub8 + 1) & (sub8 < 4), 1.0, 0.0)
    before = jnp.where(iota((128, 128), 0) < iota((128, 128), 1), 1.0, 0.0)
    rank = lax.dot_general(match, before, (((1,), (0,)), ((), ())), precision=HIGHEST, preferred_element_type=jnp.float32)
    place = jnp.sum(match * (rank + (sub8 * 16 + 1).astype(jnp.float32)), axis=0, keepdims=True) - 1.0
    select = jnp.where(iota((128, 128), 0).astype(jnp.float32) == place, 1.0, 0.0)
    row32 = iota((32, 256), 0)
    for n in range(8):
        cell = land_ref[n:n + 1, :]
        hot_x[:, 256 * n:256 * n + 256] = jnp.where((cell >> 5) == row32, 1.0, 0.0)
        hot_y[:, 256 * n:256 * n + 256] = jnp.where(((cell & 31) == row32) & (cell >= 0), 1.0, 0.0)

    mirror = 1.0 - 2.0 * live
    source = 2.0 * live * wall_ref[...]

    def columns(v, x):
        return jnp.concatenate([pltpu.roll(v, lax.rem(128 - (x * 4 + j), 128), axis=1) for j in range(4)], axis=0)

    def rows_of(plane):
        def body(i, parts):
            parts = list(parts)
            for k in range(4):
                v = plane(4 * i + k)
                for j in range(4):
                    parts[j] = jnp.where(lane8 == (4 * i + k) * 4 + j, jnp.broadcast_to(v[8 * j:8 * j + 8, 0:1], (8, 128)), parts[j])
            return tuple(parts)
        parts = lax.fori_loop(0, nx // 4, body, (jnp.zeros((8, 128), jnp.float32),) * 4)
        return (parts[0] + parts[1]) + (parts[2] + parts[3])

    top = fluid_chunks - 1

    def fluid_coef(x):
        a = [al[c, x + 1, own_rows, :] for c in range(fluid_chunks)]
        u = [uz[c, x] for c in range(fluid_chunks)]
        am, _ = lane_shifts(a)
        um, _ = lane_shifts(u)
        am[0] = jnp.where(lane == 0, a[0], am[0])
        um[0] = jnp.where(lane == 0, -u[0], um[0])
        z = [face(u[c], um[c], a[c], am[c]) for c in range(fluid_chunks)]
        _, pz = lane_shifts([v[0] for v in z])
        _, qz = lane_shifts([v[1] for v in z])
        last = face(u[top], u[top], a[top], a[top])
        pz[top] = jnp.where(lane == 127, last[0], pz[top])
        qz[top] = jnp.where(lane == 127, last[1], qz[top])
        for c in range(fluid_chunks):
            v = ux[c, x + 1]
            p_xm, q_xm = face(v, ux[c, x], a[c], al[c, x, own_rows, :])
            p_xp, q_xp = face(v, ux[c, x + 2], a[c], al[c, x + 2, own_rows, :])
            v = uy[c, x, own_rows, :]
            p_ym, q_ym = face(v, uy[c, x, TOP - 1:end - 1, :], a[c], al[c, x + 1, TOP - 1:end - 1, :])
            p_yp, q_yp = face(v, uy[c, x, TOP + 1:end + 1, :], a[c], al[c, x + 1, TOP + 1:end + 1, :])
            p_zm, q_zm = z[c]
            away = ((q_xm + p_xp) + (q_ym + p_yp)) + (q_zm + pz[c])
            toward = ((p_xm + q_xp) + (p_ym + q_yp)) + (p_zm + qz[c])
            scale = 1.6 / (away + toward)
            cf[0, c, x] = p_xm * scale
            cf[1, c, x] = q_xp * scale
            cf[2, c, x] = p_ym * scale
            cf[3, c, x] = q_yp * scale
            below, above, centre = p_zm * scale, qz[c] * scale, 1.0 - away * scale
            if c == 0:
                first = lane == 0
                wall = jnp.where(first, below, 0.0)
                sf[x] = wall * columns(source, x)
                centre = centre + wall * columns(mirror, x)
                below = jnp.where(first, 0.0, below)
            if c == top:
                above = jnp.where(lane == 127, 0.0, above)
            cf[4, c, x] = below
            cf[5, c, x] = above
            cf[6, c, x] = centre

    def fluid_plane(src, x):
        t = [src[c, x + 1, own_rows, :] for c in range(fluid_chunks)]
        zm, zp = lane_shifts(t)
        out = []
        for c in range(fluid_chunks):
            new = ((cf[0, c, x] * src[c, x, own_rows, :] + cf[1, c, x] * src[c, x + 2, own_rows, :])
                   + (cf[2, c, x] * src[c, x + 1, TOP - 1:end - 1, :] + cf[3, c, x] * src[c, x + 1, TOP + 1:end + 1, :]))
            new = new + (cf[4, c, x] * zm[c] + cf[5, c, x] * zp[c]) + cf[6, c, x] * t[c]
            out.append(new + sf[x] if c == 0 else new)
        return out

    loaded("uz")
    film = 2.0 * live * rows_of(lambda x: al[0, x + 1, own_rows, :])
    arrived(a_y + u_y)

    def body(x, _):
        fluid_coef(x)
        return 0
    lax.fori_loop(1, nx - 1, body, 0)
    arrived(a_x + u_x)
    fluid_coef(0)
    fluid_coef(nx - 1)

    def first_plane(x):
        for c, new in enumerate(fluid_plane(t0, x)):
            t1[c, x + 1, own_rows, :] = new

    arrived(t_x + t_y)
    first_plane(0)
    first_plane(nx - 1)
    t_msgs = send_planes(t1)

    def body(x, _):
        first_plane(x)
        return 0
    lax.fori_loop(1, nx - 1, body, 0)
    t_msgs += send_rows(t1)

    solid_msgs = solid_sweep(1, solid_msgs)

    arrived(t_msgs)

    def body(x, _):
        for c, new in enumerate(fluid_plane(t1, x)):
            t2[c, x] = new
        return 0
    lax.fori_loop(0, nx, body, 0)
    gas = rows_of(lambda x: t2[0, x])

    stores = []

    def store(src, dst):
        for c in range(src.shape[0]):
            n = sum(len(v) for v in loads.values()) + len(stores)
            stores.append(pltpu.make_async_copy(src.at[c], dst.at[:, :, 128 * c:128 * c + 128], load_sem.at[n]))
            stores[-1].start()

    store(t2, t_out)

    def take(v):
        return lax.dot_general(v, select, (((1,), (1,)), ((), ())), precision=HIGHEST, preferred_element_type=jnp.float32)

    rows_s[...] = take(jnp.concatenate([film, gas], axis=0))
    row_msgs = [Message(rows_s, rows_r.at[d], d) for d in range(4)]
    for m in row_msgs:
        m.start()

    solid_msgs = solid_sweep(2, solid_msgs)

    for m in near_msgs:
        m.arrived()
    lane_w = iota((nx + 2 * HALO, 128), 1)

    def widen(left, mid, right, f):
        left = pltpu.roll(left, (128 - 32 * f - 24) % 128, axis=1)
        mid = pltpu.roll(mid, (128 + HALO - 32 * f) % 128, axis=1)
        right = pltpu.roll(right, (128 + 40 - 32 * f) % 128, axis=1)
        return jnp.where(lane_w < HALO, left, jnp.where(lane_w < HALO + ny, mid, jnp.where(lane_w < 2 * HALO + ny, right, 0.0)))

    def near_field(z, f):
        return widen(nb[0, z], nb[1, z], nb[2, z], f)

    def body(z, _):
        wk[z] = near_field(z, 1)
        wxa[z] = near_field(z, 0)
        return 0
    lax.fori_loop(0, DEEP, body, 0)

    def shift_all(v):
        n = v.shape[0]
        return [pltpu.roll(v, 1, axis=0), pltpu.roll(v, n - 1, axis=0), pltpu.roll(v, 1, axis=1), pltpu.roll(v, 127, axis=1)]

    def body(z, _):
        k = wk[z]
        under = wk[jnp.maximum(z - 1, 0)] * (z > 0).astype(jnp.float32)
        over = wk[jnp.minimum(z + 1, DEEP - 1)] * (z < DEEP - 1).astype(jnp.float32)
        g = [conductance(k, kn) for kn in shift_all(k) + [under, over]]
        diag = ((g[0] + g[1]) + (g[2] + g[3])) + ((g[4] + g[5]) + near_field(z, 2))
        diag = jnp.where(diag > 0.0, diag, 1.0)
        inverse = 1.0 / diag
        for n in range(6):
            wcf[n, z] = g[n] * inverse
        wcf[6, z] = near_field(z, 3) * inverse

        @pl.when(z == 0)
        def _():
            wd[...] = diag
        return 0
    lax.fori_loop(0, DEEP, body, 0)

    for m in row_msgs:
        m.arrived()

    def bands(refs):
        total = None
        for band, ref in enumerate(refs):
            v = ref[...]
            lane = iota(v.shape, 1)
            v = jnp.where((lane >= 16 * band) & (lane < 16 * band + 16), v, 0.0)
            total = v if total is None else total + v
        return total

    came = bands([rows_r.at[d] for d in range(4)])
    film_in = jnp.concatenate([film * self_mask, came[0:8]], axis=1)
    heat_in = film_in * jnp.concatenate([gas, came[8:16]], axis=1)
    weighed = jnp.concatenate(
        [jnp.concatenate([hot_y[:, 256 * n:256 * n + 256] * v[n:n + 1, :] for n in range(8)], axis=1) for v in (film_in, heat_in)]
        + [jnp.zeros((64, 2048), jnp.float32)], axis=0)
    fb[1, HALO:HALO + nx, :] = lax.dot_general(
        hot_x[...], weighed, (((1,), (1,)), ((), ())), precision=HIGHEST, preferred_element_type=jnp.float32)
    film_msgs = []
    for d in range(8):
        column, out_rows, rows = near_slot(d)
        film_msgs.append(Message(fb.at[1, out_rows, :], fb.at[column, rows, :], d))
        film_msgs[-1].start()

    solid_msgs = solid_sweep(3, solid_msgs)

    for m in film_msgs:
        m.arrived()
    wide = [widen(fb[0], fb[1], fb[2], f) for f in range(2)]
    diag = wd[...]
    inverse = 1.0 / (diag + wide[0])
    wcf[6, 0] = (wcf[6, 0] * diag + wide[1]) * inverse
    for n in range(6):
        wcf[n, 0] = wcf[n, 0] * diag * inverse

    for n in range(SWEEPS):
        decay, gain = coefficients[n]
        src, dst = (wxa, wxb) if n % 2 == 0 else (wxb, wxa)

        def level(z, n=n, decay=decay, gain=gain, src=src):
            v = src[z]
            near_v = shift_all(v) + [src[jnp.maximum(z - 1, 0)], src[z + 1]]
            r = (wcf[0, z] * near_v[0] + wcf[1, z] * near_v[1]) + (wcf[2, z] * near_v[2] + wcf[3, z] * near_v[3])
            r = r + (wcf[4, z] * near_v[4] + wcf[5, z] * near_v[5]) + wcf[6, z]
            new = (1.0 + decay - gain) * v + gain * r
            return new if n == 0 else new - decay * dst[z]

        count = DEEP - 1 - n

        def body(i, _, dst=dst, level=level):
            news = [level(2 * i), level(2 * i + 1)]
            for k in range(2):
                dst[2 * i + k] = news[k]
            return 0
        lax.fori_loop(0, count // 2, body, 0)
        if count % 2:
            dst[count - 1] = level(count - 1)

    solved = wxa if SWEEPS % 2 == 0 else wxb
    surface = pltpu.roll(solved[0, HALO:HALO + nx, :], 128 - HALO, axis=1)[:, 0:32]
    picked = lax.dot_general(surface, hot_y[...], (((1,), (0,)), ((), ())), precision=HIGHEST, preferred_element_type=jnp.float32)
    picked = jnp.sum(picked * hot_x[...], axis=0, keepdims=True)
    for n in range(8):
        slots[n:n + 1, :] = picked[:, 256 * n:256 * n + 256]
    wall_s[...] = slots[:, 128:256]
    wall_msgs = [Message(wall_s, wall_r.at[d], d) for d in range(4)]
    for m in wall_msgs:
        m.start()

    def body(x, _):
        cells = jnp.concatenate([solved[0:HALO, pl.ds(HALO + x, 1), :].reshape(HALO, 128), jnp.zeros((128 - HALO, 128), jnp.float32)], axis=0)
        wz[x] = jnp.transpose(cells)[HALO:HALO + ny]
        return 0
    lax.fori_loop(0, nx, body, 0)

    solid_msgs = solid_sweep(4, solid_msgs)

    for m in wall_msgs:
        m.arrived()
    back = bands([wall_r.at[d] for d in (1, 0, 3, 2)])
    spread = lax.dot_general(back, select, (((1,), (0,)), ((), ())), precision=HIGHEST, preferred_element_type=jnp.float32)
    wall_out[...] = (self_mask * slots[:, 0:128] + spread) * live

    for n in range(5, SWEEPS):
        solid_msgs = solid_sweep(n, solid_msgs)
    store(xa.at[:, own_planes, own_rows, :], x_out)
    for copy in stores:
        copy.wait()
    for m in list(pending):
        m.sent()


N_MESSAGES = 8 + 12 + 8 + 4 * (SWEEPS - 1) + 4 + 4 + 8 + 4


def on_device(n_blk, n_sub, fluid_temp, velocity, eddy_diff, wall_prev, row_count, owner_table, landing_cell, solid_temp, conductivity, sink, heat_source):
    nx, ny, nz = fluid_temp.shape
    nsz = solid_temp.shape[2]
    f32 = jnp.float32
    wall_rows = wall_prev.reshape(128, 8).T
    landing = jnp.pad(landing_cell.reshape(192, 8).T, ((0, 0), (0, 64)), constant_values=-1)
    any_space = pl.BlockSpec(memory_space=pl.ANY)
    vmem_space = pl.BlockSpec(memory_space=pltpu.VMEM)

    def vmem(*shape):
        return pltpu.VMEM(shape, f32)

    def haloed(depth):
        return vmem(depth // 128, nx + 2, ny + 2 * TOP, 128)

    wide = nx + 2 * HALO
    fluid_new, solid_new, wall_rows_new = pl.pallas_call(
        functools.partial(kernel, n_blk, n_sub),
        out_shape=(
            jax.ShapeDtypeStruct((nx, ny, nz), f32),
            jax.ShapeDtypeStruct((nx, ny, nsz), f32),
            jax.ShapeDtypeStruct((8, 128), f32),
        ),
        in_specs=[pl.BlockSpec(memory_space=pltpu.SMEM)] + [any_space] * 7 + [vmem_space] * 3,
        out_specs=(any_space, any_space, vmem_space),
        scratch_shapes=[
            haloed(nz), haloed(nz), vmem(nz // 128, nx, ny, 128),
            vmem(nz // 128, nx + 2, ny, 128), vmem(nz // 128, nx, ny + 2 * TOP, 128), vmem(nz // 128, nx, ny, 128),
            haloed(nz), vmem(7, nz // 128, nx, ny, 128), vmem(nx, ny, 128),
            haloed(nsz), haloed(nsz), haloed(nsz), vmem(nsz // 128, nx, ny, 128), vmem(nsz // 128, nx, ny, 128),
            vmem(7, nsz // 128, nx, ny, 128),
            vmem(3, DEEP, wide, 128), vmem(3, wide, 128),
            vmem(DEEP, wide, 128), vmem(7, DEEP, wide, 128),
            vmem(DEEP, wide, 128), vmem(DEEP, wide, 128), vmem(DEEP, wide, 128), vmem(wide, 128), vmem(nx, ny, 128),
            vmem(16, 128), vmem(4, 16, 128), vmem(8, 128), vmem(4, 8, 128),
            vmem(32, 2048), vmem(32, 2048), vmem(8, 256),
            pltpu.SemaphoreType.DMA((6 * nz // 128 + 5 * nsz // 128,)),
            pltpu.SemaphoreType.DMA((N_MESSAGES,)),
            pltpu.SemaphoreType.DMA((N_MESSAGES,)),
        ],
        compiler_params=pltpu.CompilerParams(
            collective_id=0, has_side_effects=True, vmem_limit_bytes=60 * 1024 * 1024
        ),
    )(row_count, fluid_temp, velocity, eddy_diff, solid_temp, conductivity, sink, heat_source, wall_rows, owner_table, landing)
    return fluid_new, solid_new, wall_rows_new.T.reshape(-1)


def solution(mesh):
    return jax.shard_map(
        functools.partial(on_device, mesh.shape["blk"], mesh.shape["sub"]),
        mesh=mesh,
        in_specs=(
            P("blk", "sub", None),
            P(None, "blk", "sub", None),
            P("blk", "sub", None),
            P(("blk", "sub")),
            P(("blk", "sub")),
            P(("blk", "sub"), None),
            P(("blk", "sub"), None),
            P("blk", "sub", None),
            P("blk", "sub", None),
            P("blk", "sub", None),
            P("blk", "sub", None),
        ),
        out_specs=(P("blk", "sub", None), P("blk", "sub", None), P(("blk", "sub"))),
        check_vma=False,
    )
```

time: 110 us -> 93.6 us (0.85)
  local copies, waits for them, and re-layouts: 14.2 us -> 7.92 us
  Pallas kernels: 88.8 us -> 83.2 us
  other arithmetic: 4.74 us -> 0.71 us
    pallas_call x1, Pallas kernels: 88.8 us -> 83.2 us  [on_device(): pl.pallas_call(functools.partial(kernel, n_blk, n_sub), out_shape=(jax.Sh...]
    pallas_call x1 -> x0, local copies, waits for them, and re-layouts: 5.37 us -> none  [on_device(): pl.pallas_call(functools.partial(kernel, n_blk, n_sub), out_shape=(jax.Sh...]
    select_n x1 -> x0, other arithmetic: 4.02 us -> none  [on_device(): solid_new = jnp.where(depth < HALO, near_wall, solid_bulk)]
    unnamed x8 -> x4, local copies, waits for them, and re-layouts: 5.85 us -> 4.25 us
where the time goes in v2:
time: 93.6 us; the launch traced here: 93.2 us
  Pallas kernels  83.2 us (89%)
  local copies, waits for them, and re-layouts  7.92 us (8%)
  between operations  1.31 us (1%)
    pallas_call x1, Pallas kernels, on_device(): pl.pallas_call(functools.partial(kernel, n_blk, n_sub), out_shape=(jax.Sh...  83.2 us
    unnamed x4, local copies, waits for them, and re-layouts  4.25 us

profile of v2, /device:TPU:5, one launch (start us, length us, event | category | flops | bytes accessed | tf_op | source)
XLA Modules:
  0.0 93.2 jit_solution(1293267123965094755)
XLA Ops:
  1.3 0.7 reduce
  2.0 0.8 reshape.15
  2.8 0.7 copy.14
  3.4 0.1 reshape.16
  3.5 0.1 copy.15
  3.6 0.6 pad.4.land_ref
  4.2 83.2 %shard_map.130 = (f32[32,32,512]{2,1,0:T(8,128)}, f32[32,32,256]{2,1,0:T(8,128)}, f32[8,128]{1,0:T(8,128)}) custom-call(s32[1]{0:T(128)S(6)} %copy.19.count_ref, f32[32,32,512]{2,1,0:T(8,128)} %t_hbm.1, f32[3,32,32,512]{3,2,1,0:T(8,128)} %vel_hbm.1, f32[32,32,512]{2,1,0:T(8,128)} %a_hbm.1, f32[32,32,256]{2,1,0:T(8,128)} %x_hbm.1, f32[32,32,256]{2,1,0:T(8,128)} %k_hbm.1, ...), custom_call_target="tpu_custom_call" | custom-call | tf_op jit(solution)/shard_map/pallas_call | solution.py:601
  87.5 0.8 copy.16
  88.2 0.7 reshape.17
  88.9 0.0 copy-start
  88.9 3.3 %copy.20 = f32[32,32,512]{2,1,0:T(8,128)} copy(f32[32,32,512]{2,1,0:T(8,128)} %get-tuple-element.12) | data formatting | bytes 4194304
  92.2 0.0 copy-done
  92.2 1.0 %copy.21 = f32[32,32,256]{2,1,0:T(8,128)} copy(f32[32,32,256]{2,1,0:T(8,128)S(1)} %copy-done) | data formatting | bytes 2097152
Async XLA Ops:
  88.9 3.3 %copy-start = (f32[32,32,256]{2,1,0:T(8,128)S(1)}, f32[32,32,256]{2,1,0:T(8,128)}, u32[]{:S(2)}) copy-start(f32[32,32,256]{2,1,0:T(8,128)} %get-tuple-element.13) | copy-start | bytes 3145732

commit v3 on v2

--- a/solution.py
+++ b/solution.py
@@ -12,6 +12,9 @@
 HALO = 8
 DEEP = 16
 TOP = 8
+SOLID_STEP = 5
+WEDGE_SPLIT = 4
+FLUID_STEP = 2
 EIG_LOW = 0.02
 EIG_HIGH = 2.0
 HIGHEST = lax.Precision.HIGHEST
@@ -61,7 +64,7 @@
     n_blk, n_sub,
     count_ref, t_hbm, vel_hbm, a_hbm, x_hbm, k_hbm, e_hbm, q_hbm, wall_ref, owner_ref, land_ref,
     t_out, x_out, wall_out,
-    t0, t1, t2, ux, uy, uz, al, cf, sf,
+    t0, t1, ux, uy, uz, al, cf, sf,
     xa, xb, kc, ec, qc, cs,
     nb, fb, wk, wcf, wxa, wxb, wp, wd, wz,
     rows_s, rows_r, wall_s, wall_r, hot_x, hot_y, slots,
@@ -194,6 +197,39 @@
             nb[column, :, rows, :] = jnp.zeros((DEEP, height, 128), jnp.float32)
             fb[column, rows, :] = jnp.zeros((height, 128), jnp.float32)
 
+    def product(x, y, dims):
+        return lax.dot_general(x, y, (dims, ((), ())), precision=HIGHEST, preferred_element_type=jnp.float32)
+
+    lane, lane8, sub8 = iota((ny, 128), 1), iota((8, 128), 1), iota((8, 128), 0)
+    keep = (lane8 & 7) == sub8
+    compress = jnp.where((iota((128, 128), 0) >> 3) == iota((128, 128), 1), 1.0, 0.0)
+    flat = [wall_ref[n:n + 1, :] for n in range(8)] + [land_ref[0:1, 128 * n:128 * n + 128].astype(jnp.float32) for n in range(12)]
+    packed = product(jnp.concatenate([jnp.where(keep, jnp.broadcast_to(v, (8, 128)), 0.0) for v in flat], axis=0), compress, ((1,), (0,)))
+
+    def gather_rows(first, count):
+        total = packed[8 * first:8 * first + 8]
+        for n in range(1, count):
+            total = total + pltpu.roll(packed[8 * (first + n):8 * (first + n) + 8], 16 * n, axis=1)
+        return total
+
+    wall = gather_rows(0, 8)
+    land = jnp.concatenate([gather_rows(8, 8), jnp.where(lane8 < 64, gather_rows(16, 4), -1.0)], axis=1).astype(jnp.int32)
+    live = jnp.where(lane8 * 8 + sub8 < count_ref[0], 1.0, 0.0)
+    owner = jnp.broadcast_to(owner_ref[...], (8, 128))
+    self_mask = jnp.where(owner == 0, 1.0, 0.0)
+    match = jnp.where((owner == sub8 + 1) & (sub8 < 4), 1.0, 0.0)
+    before = jnp.where(iota((128, 128), 0) < iota((128, 128), 1), 1.0, 0.0)
+    rank = product(match, before, ((1,), (0,)))
+    place = jnp.sum(match * (rank + (sub8 * 16 + 1).astype(jnp.float32)), axis=0, keepdims=True) - 1.0
+    row32 = iota((32, 256), 0)
+    for n in range(8):
+        cell = land[n:n + 1, :]
+        hot_x[:, 256 * n:256 * n + 256] = jnp.where((cell >> 5) == row32, 1.0, 0.0)
+        hot_y[:, 256 * n:256 * n + 256] = jnp.where(((cell & 31) == row32) & (cell >= 0), 1.0, 0.0)
+
+    def select():
+        return jnp.where(iota((128, 128), 0).astype(jnp.float32) == place, 1.0, 0.0)
+
     near = (b > 0).astype(jnp.int32) + (b < n_blk - 1).astype(jnp.int32)
     side = (s > 0).astype(jnp.int32) + (s < n_sub - 1).astype(jnp.int32)
     pl.semaphore_wait(barrier, near + side + near * side)
@@ -210,20 +246,17 @@
     u_y = [Message(uy.at[:, :, end - 1:end, :], uy.at[:, :, TOP - 1:TOP, :], 2).start(),
            Message(uy.at[:, :, TOP:TOP + 1, :], uy.at[:, :, end:end + 1, :], 3).start()]
 
-    loaded("e", "q")
-
     def turn(x, _):
         tile = jnp.concatenate([xa[0, x + 1, own_rows, :], kc[0, x + 1, own_rows, :], ec[0, x], qc[0, x]], axis=0)
         nb[1, :, pl.ds(HALO + x, 1), :] = jnp.transpose(tile)[0:DEEP].reshape(DEEP, 1, 128)
         return 0
 
-    lax.fori_loop(0, nx, turn, 0, unroll=2)
-    near_msgs = []
-    for d in range(8):
-        column, out_rows, rows = near_slot(d)
-        near_msgs.append(Message(nb.at[1, :, out_rows, :], nb.at[column, :, rows, :], d).start())
-
-    lane = iota((ny, 128), 1)
+    def send_near(column_ref, part):
+        messages = []
+        for d in range(8):
+            column, out_rows, rows = near_slot(d)
+            messages.append(Message(part(column_ref, 1, out_rows), part(column_ref, column, rows), d).start())
+        return messages
 
     def solid_coef(x, count):
         k = [[kc[c, x + i, own_rows, :] for c in range(solid_chunks)] for i in range(count + 2)]
@@ -245,78 +278,57 @@
             for n in range(7):
                 cs[n, c, at] = values[n]
 
-    def solid_planes(n, src, dst, x, count):
+    def solid_planes(n, src, dst, runs):
         decay, gain = coefficients[n]
-        v = [[src[c, x + i, own_rows, :] for c in range(solid_chunks)] for i in range(count + 2)]
         out = []
-        for i in range(count):
-            zm, zp = lane_shifts(v[i + 1])
-            for c in range(solid_chunks):
-                at = x + i
-                r = ((cs[0, c, at] * v[i][c] + cs[1, c, at] * v[i + 2][c])
-                     + (cs[2, c, at] * src[c, at + 1, TOP - 1:end - 1, :] + cs[3, c, at] * src[c, at + 1, TOP + 1:end + 1, :]))
-                r = r + (cs[4, c, at] * zm[c] + cs[5, c, at] * zp[c]) + cs[6, c, at]
-                new = (1.0 + decay - gain) * v[i + 1][c] + gain * r
-                if n > 0:
-                    new = new - decay * dst[c, at + 1, own_rows, :]
-                if n == SWEEPS - 1 and c == 0:
-                    new = jnp.where(lane < HALO, wz[at], new)
-                out.append((c, at, new))
+        for x, count in runs:
+            v = [[src[c, x + i, own_rows, :] for c in range(solid_chunks)] for i in range(count + 2)]
+            for i in range(count):
+                zm, zp = lane_shifts(v[i + 1])
+                for c in range(solid_chunks):
+                    at = x + i
+                    r = ((cs[0, c, at] * v[i][c] + cs[1, c, at] * v[i + 2][c])
+                         + (cs[2, c, at] * src[c, at + 1, TOP - 1:end - 1, :] + cs[3, c, at] * src[c, at + 1, TOP + 1:end + 1, :]))
+                    r = r + (cs[4, c, at] * zm[c] + cs[5, c, at] * zp[c]) + cs[6, c, at]
+                    new = (1.0 + decay - gain) * v[i + 1][c] + gain * r
+                    if n > 0:
+                        new = new - decay * dst[c, at + 1, own_rows, :]
+                    if n == SWEEPS - 1 and c == 0:
+                        new = jnp.where(lane < HALO, wz[at], new)
+                    out.append((c, at, new))
         for c, at, new in out:
-            dst[c, at + 1, own_rows, :] = new
-
-    pairs = (nx - 2) // 2
-
-    def solid_sweep(n, waits):
+            if n == SWEEPS - 1:
+                x_out[at, :, 128 * c:128 * c + 128] = new
+            else:
+                dst[c, at + 1, own_rows, :] = new
+
+    solid_sends = [(-1, m) for m in x_x + x_y]
+    solid_waits = [x_x + x_y]
+    interior = nx - 2
+
+    def loop(count, step, work):
+        def body(i, _):
+            work(i * step)
+            return 0
+        lax.fori_loop(0, count // step, body, 0)
+
+    def solid_sweep(n):
         src, dst = (xa, xb) if n % 2 == 0 else (xb, xa)
-        arrived(waits)
+        arrived(solid_waits.pop())
         for m in list(solid_sends):
             if m[0] <= n - 2:
                 m[1].sent()
                 solid_sends.remove(m)
-        solid_planes(n, src, dst, 0, 1)
-        solid_planes(n, src, dst, nx - 1, 1)
+        solid_planes(n, src, dst, [(0, 1), (nx - 1, 1)])
         msgs = send_planes(dst) if n < SWEEPS - 1 else []
-
-        def body(i, _):
-            solid_planes(n, src, dst, 1 + 2 * i, 2)
-            return 0
-        lax.fori_loop(0, pairs, body, 0)
+        loop(interior, SOLID_STEP, lambda x: solid_planes(n, src, dst, [(1 + x, SOLID_STEP)]))
         if n < SWEEPS - 1:
             msgs += send_rows(dst)
         solid_sends.extend((n, m) for m in msgs)
-        return msgs
-
-    solid_sends = [(-1, m) for m in x_x + x_y]
-
-    arrived(k_y)
-
-    def body(i, _):
-        solid_coef(1 + 2 * i, 2)
-        return 0
-    lax.fori_loop(0, pairs, body, 0)
-    arrived(k_x)
-    solid_coef(0, 1)
-    solid_coef(nx - 1, 1)
-    solid_msgs = solid_sweep(0, x_x + x_y)
-
-    lane8, sub8 = iota((8, 128), 1), iota((8, 128), 0)
-    live = jnp.where(lane8 * 8 + sub8 < count_ref[0], 1.0, 0.0)
-    owner = jnp.broadcast_to(owner_ref[...], (8, 128))
-    self_mask = jnp.where(owner == 0, 1.0, 0.0)
-    match = jnp.where((owner == sub8 + 1) & (sub8 < 4), 1.0, 0.0)
-    before = jnp.where(iota((128, 128), 0) < iota((128, 128), 1), 1.0, 0.0)
-    rank = lax.dot_general(match, before, (((1,), (0,)), ((), ())), precision=HIGHEST, preferred_element_type=jnp.float32)
-    place = jnp.sum(match * (rank + (sub8 * 16 + 1).astype(jnp.float32)), axis=0, keepdims=True) - 1.0
-    select = jnp.where(iota((128, 128), 0).astype(jnp.float32) == place, 1.0, 0.0)
-    row32 = iota((32, 256), 0)
-    for n in range(8):
-        cell = land_ref[n:n + 1, :]
-        hot_x[:, 256 * n:256 * n + 256] = jnp.where((cell >> 5) == row32, 1.0, 0.0)
-        hot_y[:, 256 * n:256 * n + 256] = jnp.where(((cell & 31) == row32) & (cell >= 0), 1.0, 0.0)
+        solid_waits.append(msgs)
 
     mirror = 1.0 - 2.0 * live
-    source = 2.0 * live * wall_ref[...]
+    source = 2.0 * live * wall
 
     def columns(v, x):
         return jnp.concatenate([pltpu.roll(v, lax.rem(128 - (x * 4 + j), 128), axis=1) for j in range(4)], axis=0)
@@ -365,9 +377,9 @@
             below, above, centre = p_zm * scale, qz[c] * scale, 1.0 - away * scale
             if c == 0:
                 first = lane == 0
-                wall = jnp.where(first, below, 0.0)
-                sf[x] = wall * columns(source, x)
-                centre = centre + wall * columns(mirror, x)
+                at_wall = jnp.where(first, below, 0.0)
+                sf[x] = at_wall * columns(source, x)
+                centre = centre + at_wall * columns(mirror, x)
                 below = jnp.where(first, 0.0, below)
             if c == top:
                 above = jnp.where(lane == 127, 0.0, above)
@@ -375,77 +387,32 @@
             cf[5, c, x] = above
             cf[6, c, x] = centre
 
-    def fluid_plane(src, x):
-        t = [src[c, x + 1, own_rows, :] for c in range(fluid_chunks)]
-        zm, zp = lane_shifts(t)
+    def fluid_planes(src, xs, chunks, put):
         out = []
-        for c in range(fluid_chunks):
-            new = ((cf[0, c, x] * src[c, x, own_rows, :] + cf[1, c, x] * src[c, x + 2, own_rows, :])
-                   + (cf[2, c, x] * src[c, x + 1, TOP - 1:end - 1, :] + cf[3, c, x] * src[c, x + 1, TOP + 1:end + 1, :]))
-            new = new + (cf[4, c, x] * zm[c] + cf[5, c, x] * zp[c]) + cf[6, c, x] * t[c]
-            out.append(new + sf[x] if c == 0 else new)
-        return out
-
-    loaded("uz")
-    film = 2.0 * live * rows_of(lambda x: al[0, x + 1, own_rows, :])
-    arrived(a_y + u_y)
-
-    def body(x, _):
-        fluid_coef(x)
-        return 0
-    lax.fori_loop(1, nx - 1, body, 0)
-    arrived(a_x + u_x)
-    fluid_coef(0)
-    fluid_coef(nx - 1)
-
-    def first_plane(x):
-        for c, new in enumerate(fluid_plane(t0, x)):
-            t1[c, x + 1, own_rows, :] = new
-
-    arrived(t_x + t_y)
-    first_plane(0)
-    first_plane(nx - 1)
-    t_msgs = send_planes(t1)
-
-    def body(x, _):
-        first_plane(x)
-        return 0
-    lax.fori_loop(1, nx - 1, body, 0)
-    t_msgs += send_rows(t1)
-
-    solid_msgs = solid_sweep(1, solid_msgs)
-
-    arrived(t_msgs)
-
-    def body(x, _):
-        for c, new in enumerate(fluid_plane(t1, x)):
-            t2[c, x] = new
-        return 0
-    lax.fori_loop(0, nx, body, 0)
-    gas = rows_of(lambda x: t2[0, x])
-
-    stores = []
-
-    def store(src, dst):
-        for c in range(src.shape[0]):
-            n = sum(len(v) for v in loads.values()) + len(stores)
-            stores.append(pltpu.make_async_copy(src.at[c], dst.at[:, :, 128 * c:128 * c + 128], load_sem.at[n]))
-            stores[-1].start()
-
-    store(t2, t_out)
-
-    def take(v):
-        return lax.dot_general(v, select, (((1,), (1,)), ((), ())), precision=HIGHEST, preferred_element_type=jnp.float32)
-
-    rows_s[...] = take(jnp.concatenate([film, gas], axis=0))
-    row_msgs = [Message(rows_s, rows_r.at[d], d) for d in range(4)]
-    for m in row_msgs:
-        m.start()
-
-    solid_msgs = solid_sweep(2, solid_msgs)
-
-    for m in near_msgs:
-        m.arrived()
+        for x in xs:
+            held = {}
+
+            def rolled(c, shift, held=held, x=x):
+                if (c, shift) not in held:
+                    held[c, shift] = pltpu.roll(src[c, x + 1, own_rows, :], shift, axis=1)
+                return held[c, shift]
+
+            for c in chunks:
+                zm = rolled(c, 1) if c == 0 else jnp.where(lane == 0, rolled(c - 1, 1), rolled(c, 1))
+                zp = rolled(c, 127) if c == top else jnp.where(lane == 127, rolled(c + 1, 127), rolled(c, 127))
+                new = ((cf[0, c, x] * src[c, x, own_rows, :] + cf[1, c, x] * src[c, x + 2, own_rows, :])
+                       + (cf[2, c, x] * src[c, x + 1, TOP - 1:end - 1, :] + cf[3, c, x] * src[c, x + 1, TOP + 1:end + 1, :]))
+                new = new + (cf[4, c, x] * zm + cf[5, c, x] * zp) + cf[6, c, x] * src[c, x + 1, own_rows, :]
+                out.append((c, x, new + sf[x] if c == 0 else new))
+        for item in out:
+            put(*item)
+
+    def put_first(c, x, new):
+        t1[c, x + 1, own_rows, :] = new
+
+    def put_second(c, x, new):
+        t_out[x, :, 128 * c:128 * c + 128] = new
+
     lane_w = iota((nx + 2 * HALO, 128), 1)
 
     def widen(left, mid, right, f):
@@ -457,17 +424,15 @@
     def near_field(z, f):
         return widen(nb[0, z], nb[1, z], nb[2, z], f)
 
-    def body(z, _):
-        wk[z] = near_field(z, 1)
-        wxa[z] = near_field(z, 0)
-        return 0
-    lax.fori_loop(0, DEEP, body, 0)
-
     def shift_all(v):
         n = v.shape[0]
         return [pltpu.roll(v, 1, axis=0), pltpu.roll(v, n - 1, axis=0), pltpu.roll(v, 1, axis=1), pltpu.roll(v, 127, axis=1)]
 
-    def body(z, _):
+    def spread_near(z):
+        wk[z] = near_field(z, 1)
+        wxa[z] = near_field(z, 0)
+
+    def wedge_coef(z):
         k = wk[z]
         under = wk[jnp.maximum(z - 1, 0)] * (z > 0).astype(jnp.float32)
         over = wk[jnp.minimum(z + 1, DEEP - 1)] * (z < DEEP - 1).astype(jnp.float32)
@@ -482,99 +447,131 @@
         @pl.when(z == 0)
         def _():
             wd[...] = diag
-        return 0
-    lax.fori_loop(0, DEEP, body, 0)
-
-    for m in row_msgs:
-        m.arrived()
+
+    def wedge_sweep(n):
+        decay, gain = coefficients[n]
+        src, dst = (wxa, wxb) if n % 2 == 0 else (wxb, wxa)
+
+        def level(z):
+            v = src[z]
+            near_v = shift_all(v) + [src[jnp.maximum(z - 1, 0)], src[z + 1]]
+            r = (wcf[0, z] * near_v[0] + wcf[1, z] * near_v[1]) + (wcf[2, z] * near_v[2] + wcf[3, z] * near_v[3])
+            r = r + (wcf[4, z] * near_v[4] + wcf[5, z] * near_v[5]) + wcf[6, z]
+            new = (1.0 + decay - gain) * v + gain * r
+            return new if n == 0 else new - decay * dst[z]
+
+        def levels(z, step):
+            for k, new in enumerate([level(z + k) for k in range(step)]):
+                dst[z + k] = new
+
+        count = DEEP - 1 - n
+        step = 3 if count % 3 == 0 else 2
+        loop(count - count % step, step, lambda z: levels(z, step))
+        if count % step:
+            levels(count - count % step, count % step)
 
     def bands(refs):
         total = None
         for band, ref in enumerate(refs):
             v = ref[...]
-            lane = iota(v.shape, 1)
-            v = jnp.where((lane >= 16 * band) & (lane < 16 * band + 16), v, 0.0)
+            at = iota(v.shape, 1)
+            v = jnp.where((at >= 16 * band) & (at < 16 * band + 16), v, 0.0)
             total = v if total is None else total + v
         return total
 
+    all_chunks = range(fluid_chunks)
+    loaded("e", "q")
+    lax.fori_loop(0, nx, turn, 0, unroll=2)
+    film = 2.0 * live * rows_of(lambda x: al[0, x + 1, own_rows, :])
+    arrived(k_y)
+    loop(interior, 2, lambda x: solid_coef(1 + x, 2))
+    arrived(k_x)
+    solid_coef(0, 1)
+    solid_coef(nx - 1, 1)
+    solid_sweep(0)
+    near_msgs = send_near(nb, lambda ref, column, rows: ref.at[column, :, rows, :])
+
+    loaded("uz")
+    arrived(a_y + u_y)
+    half = interior // 2
+    loop(half, 1, lambda x: fluid_coef(1 + x))
+    solid_sweep(1)
+    loop(interior - half, 1, lambda x: fluid_coef(1 + half + x))
+    arrived(a_x + u_x)
+    fluid_coef(0)
+    fluid_coef(nx - 1)
+
+    arrived(t_x + t_y)
+    fluid_planes(t0, (0, nx - 1), all_chunks, put_first)
+    t_msgs = send_planes(t1)
+    loop(interior, FLUID_STEP, lambda x: fluid_planes(t0, [1 + x + i for i in range(FLUID_STEP)], all_chunks, put_first))
+    t_msgs += send_rows(t1)
+    solid_sweep(2)
+
+    arrived(near_msgs)
+    loop(DEEP, 1, spread_near)
+    loop(DEEP, 1, wedge_coef)
+    solid_sweep(3)
+
+    arrived(t_msgs)
+    loop(nx, 4, lambda x: fluid_planes(t1, [x + i for i in range(4)], (0,), put_second))
+    gas = rows_of(lambda x: t_out[x, :, 0:128])
+    rows_s[...] = product(jnp.concatenate([film, gas], axis=0), select(), ((1,), (1,)))
+    row_msgs = [Message(rows_s, rows_r.at[d], d).start() for d in range(4)]
+
+    if fluid_chunks > 1:
+        loop(nx, FLUID_STEP, lambda x: fluid_planes(t1, [x + i for i in range(FLUID_STEP)], all_chunks[1:], put_second))
+    solid_sweep(4)
+
+    arrived(row_msgs)
     came = bands([rows_r.at[d] for d in range(4)])
     film_in = jnp.concatenate([film * self_mask, came[0:8]], axis=1)
     heat_in = film_in * jnp.concatenate([gas, came[8:16]], axis=1)
     weighed = jnp.concatenate(
         [jnp.concatenate([hot_y[:, 256 * n:256 * n + 256] * v[n:n + 1, :] for n in range(8)], axis=1) for v in (film_in, heat_in)]
         + [jnp.zeros((64, 2048), jnp.float32)], axis=0)
-    fb[1, HALO:HALO + nx, :] = lax.dot_general(
-        hot_x[...], weighed, (((1,), (1,)), ((), ())), precision=HIGHEST, preferred_element_type=jnp.float32)
-    film_msgs = []
-    for d in range(8):
-        column, out_rows, rows = near_slot(d)
-        film_msgs.append(Message(fb.at[1, out_rows, :], fb.at[column, rows, :], d))
-        film_msgs[-1].start()
-
-    solid_msgs = solid_sweep(3, solid_msgs)
-
-    for m in film_msgs:
-        m.arrived()
+    fb[1, HALO:HALO + nx, :] = product(hot_x[...], weighed, ((1,), (1,)))
+    film_msgs = send_near(fb, lambda ref, column, rows: ref.at[column, rows, :])
+
+    solid_sweep(5)
+
+    arrived(film_msgs)
     wide = [widen(fb[0], fb[1], fb[2], f) for f in range(2)]
     diag = wd[...]
     inverse = 1.0 / (diag + wide[0])
     wcf[6, 0] = (wcf[6, 0] * diag + wide[1]) * inverse
     for n in range(6):
         wcf[n, 0] = wcf[n, 0] * diag * inverse
-
-    for n in range(SWEEPS):
-        decay, gain = coefficients[n]
-        src, dst = (wxa, wxb) if n % 2 == 0 else (wxb, wxa)
-
-        def level(z, n=n, decay=decay, gain=gain, src=src):
-            v = src[z]
-            near_v = shift_all(v) + [src[jnp.maximum(z - 1, 0)], src[z + 1]]
-            r = (wcf[0, z] * near_v[0] + wcf[1, z] * near_v[1]) + (wcf[2, z] * near_v[2] + wcf[3, z] * near_v[3])
-            r = r + (wcf[4, z] * near_v[4] + wcf[5, z] * near_v[5]) + wcf[6, z]
-            new = (1.0 + decay - gain) * v + gain * r
-            return new if n == 0 else new - decay * dst[z]
-
-        count = DEEP - 1 - n
-
-        def body(i, _, dst=dst, level=level):
-            news = [level(2 * i), level(2 * i + 1)]
-            for k in range(2):
-                dst[2 * i + k] = news[k]
-            return 0
-        lax.fori_loop(0, count // 2, body, 0)
-        if count % 2:
-            dst[count - 1] = level(count - 1)
-
+    for n in range(WEDGE_SPLIT):
+        wedge_sweep(n)
+    solid_sweep(6)
+    for n in range(WEDGE_SPLIT, SWEEPS):
+        wedge_sweep(n)
     solved = wxa if SWEEPS % 2 == 0 else wxb
+
     surface = pltpu.roll(solved[0, HALO:HALO + nx, :], 128 - HALO, axis=1)[:, 0:32]
-    picked = lax.dot_general(surface, hot_y[...], (((1,), (0,)), ((), ())), precision=HIGHEST, preferred_element_type=jnp.float32)
+    picked = product(surface, hot_y[...], ((1,), (0,)))
     picked = jnp.sum(picked * hot_x[...], axis=0, keepdims=True)
     for n in range(8):
         slots[n:n + 1, :] = picked[:, 256 * n:256 * n + 256]
     wall_s[...] = slots[:, 128:256]
-    wall_msgs = [Message(wall_s, wall_r.at[d], d) for d in range(4)]
-    for m in wall_msgs:
-        m.start()
-
-    def body(x, _):
+    wall_msgs = [Message(wall_s, wall_r.at[d], d).start() for d in range(4)]
+
+    def turn_back(x, _):
         cells = jnp.concatenate([solved[0:HALO, pl.ds(HALO + x, 1), :].reshape(HALO, 128), jnp.zeros((128 - HALO, 128), jnp.float32)], axis=0)
         wz[x] = jnp.transpose(cells)[HALO:HALO + ny]
         return 0
-    lax.fori_loop(0, nx, body, 0)
-
-    solid_msgs = solid_sweep(4, solid_msgs)
-
-    for m in wall_msgs:
-        m.arrived()
+    lax.fori_loop(0, nx, turn_back, 0, unroll=2)
+
+    solid_sweep(7)
+
+    arrived(wall_msgs)
     back = bands([wall_r.at[d] for d in (1, 0, 3, 2)])
-    spread = lax.dot_general(back, select, (((1,), (0,)), ((), ())), precision=HIGHEST, preferred_element_type=jnp.float32)
-    wall_out[...] = (self_mask * slots[:, 0:128] + spread) * live
-
-    for n in range(5, SWEEPS):
-        solid_msgs = solid_sweep(n, solid_msgs)
-    store(xa.at[:, own_planes, own_rows, :], x_out)
-    for copy in stores:
-        copy.wait()
+    rows = (self_mask * slots[:, 0:128] + product(back, select(), ((1,), (0,)))) * live
+    rows = jnp.concatenate([jnp.where(lane8 < 16, pltpu.roll(rows, (128 - 16 * n) % 128, axis=1), 0.0) for n in range(8)], axis=0)
+    rows = product(rows, compress, ((1,), (1,)))
+    for n in range(8):
+        wall_out[n:n + 1, :] = jnp.sum(jnp.where(keep, rows[8 * n:8 * n + 8], 0.0), axis=0, keepdims=True)
     for m in list(pending):
         m.sent()
 
@@ -586,8 +583,6 @@
     nx, ny, nz = fluid_temp.shape
     nsz = solid_temp.shape[2]
     f32 = jnp.float32
-    wall_rows = wall_prev.reshape(128, 8).T
-    landing = jnp.pad(landing_cell.reshape(192, 8).T, ((0, 0), (0, 64)), constant_values=-1)
     any_space = pl.BlockSpec(memory_space=pl.ANY)
     vmem_space = pl.BlockSpec(memory_space=pltpu.VMEM)
 
@@ -598,17 +593,17 @@
         return vmem(depth // 128, nx + 2, ny + 2 * TOP, 128)
 
     wide = nx + 2 * HALO
-    fluid_new, solid_new, wall_rows_new = pl.pallas_call(
+    fluid_new, solid_new, wall_new = pl.pallas_call(
         functools.partial(kernel, n_blk, n_sub),
         out_shape=(
-            jax.ShapeDtypeStruct((nx, ny, nz), f32),
-            jax.ShapeDtypeStruct((nx, ny, nsz), f32),
+            vmem(nx, ny, nz),
+            vmem(nx, ny, nsz),
             jax.ShapeDtypeStruct((8, 128), f32),
         ),
         in_specs=[pl.BlockSpec(memory_space=pltpu.SMEM)] + [any_space] * 7 + [vmem_space] * 3,
-        out_specs=(any_space, any_space, vmem_space),
+        out_specs=(vmem_space,) * 3,
         scratch_shapes=[
-            haloed(nz), haloed(nz), vmem(nz // 128, nx, ny, 128),
+            haloed(nz), haloed(nz),
             vmem(nz // 128, nx + 2, ny, 128), vmem(nz // 128, nx, ny + 2 * TOP, 128), vmem(nz // 128, nx, ny, 128),
             haloed(nz), vmem(7, nz // 128, nx, ny, 128), vmem(nx, ny, 128),
             haloed(nsz), haloed(nsz), haloed(nsz), vmem(nsz // 128, nx, ny, 128), vmem(nsz // 128, nx, ny, 128),
@@ -625,8 +620,8 @@
         compiler_params=pltpu.CompilerParams(
             collective_id=0, has_side_effects=True, vmem_limit_bytes=60 * 1024 * 1024
         ),
-    )(row_count, fluid_temp, velocity, eddy_diff, solid_temp, conductivity, sink, heat_source, wall_rows, owner_table, landing)
-    return fluid_new, solid_new, wall_rows_new.T.reshape(-1)
+    )(row_count, fluid_temp, velocity, eddy_diff, solid_temp, conductivity, sink, heat_source, wall_prev.reshape(8, 128), owner_table, landing_cell)
+    return fluid_new, solid_new, wall_new.reshape(-1)
 
 
 def solution(mesh):

time: 93.6 us -> 70.5 us (0.75)
  Pallas kernels: 83.2 us -> 65.4 us
  local copies, waits for them, and re-layouts: 7.92 us -> 2.89 us
    pallas_call x1, Pallas kernels: 83.2 us -> 65.4 us  [on_device(): pl.pallas_call(functools.partial(kernel, n_blk, n_sub), out_shape=(vmem(n...]
    reshape x5 -> x0, local copies, waits for them, and re-layouts: 2.27 us -> none  [the longest x2 1.43 us: on_device(): wall_rows = wall_prev.reshape(128, 8).T]
    unnamed x4 -> x5, local copies, waits for them, and re-layouts: 4.25 us -> 2.89 us
where the time goes in v3:
time: 70.5 us; the launch traced here: 69.5 us
  Pallas kernels  65.4 us (93%)
  local copies, waits for them, and re-layouts  2.89 us (4%)
  between operations  1.29 us (2%)
    pallas_call x1, Pallas kernels, on_device(): pl.pallas_call(functools.partial(kernel, n_blk, n_sub), out_shape=(vmem(n...  65.4 us
    unnamed x5, local copies, waits for them, and re-layouts  2.89 us

profile of v3, /device:TPU:5, one launch (start us, length us, event | category | flops | bytes accessed | tf_op | source)
XLA Modules:
  0.0 69.5 jit_solution(435276383733040243)
XLA Ops:
  1.3 65.4 %shard_map.130 = (f32[32,32,512]{2,1,0:T(8,128)S(1)}, f32[32,32,256]{2,1,0:T(8,128)S(1)}, f32[8,128]{1,0:T(8,128)}) custom-call(s32[1]{0:T(128)S(6)} %copy.19.count_ref, f32[32,32,512]{2,1,0:T(8,128)} %t_hbm.1, f32[3,32,32,512]{3,2,1,0:T(8,128)} %vel_hbm.1, f32[32,32,512]{2,1,0:T(8,128)} %a_hbm.1, f32[32,32,256]{2,1,0:T(8,128)} %x_hbm.1, ...), custom_call_target="tpu_custom_call" | custom-call | tf_op jit(solution)/shard_map/pallas_call | solution.py:596
  66.6 1.3 %copy.17 = f32[32,32,512]{2,1,0:T(8,128)} copy(f32[32,32,512]{2,1,0:T(8,128)S(1)} %get-tuple-element.9) | data formatting | bytes 4194304
  68.0 0.0 copy-start
  68.0 1.0 %copy.18 = f32[32,32,256]{2,1,0:T(8,128)} copy(f32[32,32,256]{2,1,0:T(8,128)S(1)} %get-tuple-element.10) | data formatting | bytes 2097152
  68.9 0.0 copy-done
  68.9 0.6 copy.20
Async XLA Ops:
  68.0 1.0 %copy-start = (f32[8,128]{1,0:T(8,128)S(1)}, f32[8,128]{1,0:T(8,128)}, u32[]{:S(2)}) copy-start(f32[8,128]{1,0:T(8,128)} %get-tuple-element.8) | copy-start | bytes 12292

commit v4 on v3

--- a/solution.py
+++ b/solution.py
@@ -66,8 +66,8 @@
     t_out, x_out, wall_out,
     t0, t1, ux, uy, uz, al, cf, sf,
     xa, xb, kc, ec, qc, cs,
-    nb, fb, wk, wcf, wxa, wxb, wp, wd, wz,
-    rows_s, rows_r, wall_s, wall_r, hot_x, hot_y, slots,
+    nb, fb, wk, wcf, wxa, wxb, wd, wz,
+    rows_s, rows_r, wall_s, wall_r, hot_x, hot_y, hot_x16, hot_y16, slots,
     load_sem, send_sem, recv_sem,
 ):
     b, s = lax.axis_index("blk"), lax.axis_index("sub")
@@ -200,6 +200,16 @@
     def product(x, y, dims):
         return lax.dot_general(x, y, (dims, ((), ())), precision=HIGHEST, preferred_element_type=jnp.float32)
 
+    def pieces(v):
+        out = []
+        for _ in range(3):
+            out.append(v.astype(jnp.bfloat16))
+            v = v - out[-1].astype(jnp.float32)
+        return out
+
+    def product16(x, y, dims):
+        return lax.dot_general(x, y, (dims, ((), ())), preferred_element_type=jnp.float32)
+
     lane, lane8, sub8 = iota((ny, 128), 1), iota((8, 128), 1), iota((8, 128), 0)
     keep = (lane8 & 7) == sub8
     compress = jnp.where((iota((128, 128), 0) >> 3) == iota((128, 128), 1), 1.0, 0.0)
@@ -224,8 +234,11 @@
     row32 = iota((32, 256), 0)
     for n in range(8):
         cell = land[n:n + 1, :]
-        hot_x[:, 256 * n:256 * n + 256] = jnp.where((cell >> 5) == row32, 1.0, 0.0)
-        hot_y[:, 256 * n:256 * n + 256] = jnp.where(((cell & 31) == row32) & (cell >= 0), 1.0, 0.0)
+        at = slice(256 * n, 256 * n + 256)
+        hot_x[:, at] = jnp.where((cell >> 5) == row32, 1.0, 0.0)
+        hot_y[:, at] = jnp.where(((cell & 31) == row32) & (cell >= 0), 1.0, 0.0)
+        hot_x16[:, at] = hot_x[:, at].astype(jnp.bfloat16)
+        hot_y16[:, at] = hot_y[:, at].astype(jnp.bfloat16)
 
     def select():
         return jnp.where(iota((128, 128), 0).astype(jnp.float32) == place, 1.0, 0.0)
@@ -239,8 +252,6 @@
     k_y, x_y = send_rows(kc), send_rows(xa)
     loaded("a", "ux", "t")
     a_x = send_planes(al)
-    u_x = [Message(ux.at[:, nx if d == 0 else 1], ux.at[:, 0 if d == 0 else nx + 1], d).start() for d in range(2)]
-    t_x = send_planes(t0)
     loaded("uy")
     a_y, t_y = send_rows(al), send_rows(t0)
     u_y = [Message(uy.at[:, :, end - 1:end, :], uy.at[:, :, TOP - 1:TOP, :], 2).start(),
@@ -443,10 +454,7 @@
         for n in range(6):
             wcf[n, z] = g[n] * inverse
         wcf[6, z] = near_field(z, 3) * inverse
-
-        @pl.when(z == 0)
-        def _():
-            wd[...] = diag
+        wd[z] = diag
 
     def wedge_sweep(n):
         decay, gain = coefficients[n]
@@ -478,6 +486,13 @@
             v = jnp.where((at >= 16 * band) & (at < 16 * band + 16), v, 0.0)
             total = v if total is None else total + v
         return total
+
+    def drain():
+        recent = [m for n, m in solid_sends if n >= 0]
+        for m in [m for m in pending if m not in recent and m not in held_back]:
+            m.sent()
+
+    held_back = []
 
     all_chunks = range(fluid_chunks)
     loaded("e", "q")
@@ -489,13 +504,15 @@
     solid_coef(0, 1)
     solid_coef(nx - 1, 1)
     solid_sweep(0)
-    near_msgs = send_near(nb, lambda ref, column, rows: ref.at[column, :, rows, :])
+    u_x = [Message(ux.at[:, nx if d == 0 else 1], ux.at[:, 0 if d == 0 else nx + 1], d).start() for d in range(2)]
+    t_x = send_planes(t0)
 
     loaded("uz")
     arrived(a_y + u_y)
     half = interior // 2
     loop(half, 1, lambda x: fluid_coef(1 + x))
     solid_sweep(1)
+    near_msgs = send_near(nb, lambda ref, column, rows: ref.at[column, :, rows, :])
     loop(interior - half, 1, lambda x: fluid_coef(1 + half + x))
     arrived(a_x + u_x)
     fluid_coef(0)
@@ -509,8 +526,8 @@
     solid_sweep(2)
 
     arrived(near_msgs)
-    loop(DEEP, 1, spread_near)
-    loop(DEEP, 1, wedge_coef)
+    loop(DEEP, 2, lambda z: [spread_near(z), spread_near(z + 1)])
+    loop(DEEP, 2, lambda z: [wedge_coef(z), wedge_coef(z + 1)])
     solid_sweep(3)
 
     arrived(t_msgs)
@@ -523,21 +540,30 @@
         loop(nx, FLUID_STEP, lambda x: fluid_planes(t1, [x + i for i in range(FLUID_STEP)], all_chunks[1:], put_second))
     solid_sweep(4)
 
+    solid_sends[:] = [item for item in solid_sends if item[0] >= 0]
+    held_back.extend(row_msgs)
+    drain()
     arrived(row_msgs)
     came = bands([rows_r.at[d] for d in range(4)])
     film_in = jnp.concatenate([film * self_mask, came[0:8]], axis=1)
     heat_in = film_in * jnp.concatenate([gas, came[8:16]], axis=1)
-    weighed = jnp.concatenate(
-        [jnp.concatenate([hot_y[:, 256 * n:256 * n + 256] * v[n:n + 1, :] for n in range(8)], axis=1) for v in (film_in, heat_in)]
-        + [jnp.zeros((64, 2048), jnp.float32)], axis=0)
-    fb[1, HALO:HALO + nx, :] = product(hot_x[...], weighed, ((1,), (1,)))
+    sums = None
+    for film_piece, heat_piece in zip(pieces(film_in), pieces(heat_in)):
+        weighed = jnp.concatenate(
+            [jnp.concatenate([hot_y[:, 256 * n:256 * n + 256] * v[n:n + 1, :] for n in range(8)], axis=1)
+             for v in (film_piece.astype(jnp.float32), heat_piece.astype(jnp.float32))], axis=0).astype(jnp.bfloat16)
+        part = product16(hot_x16[...], weighed, ((1,), (1,)))
+        sums = part if sums is None else sums + part
+    fb[1, HALO:HALO + nx, :] = jnp.concatenate([sums, jnp.zeros((nx, 64), jnp.float32)], axis=1)
     film_msgs = send_near(fb, lambda ref, column, rows: ref.at[column, rows, :])
 
     solid_sweep(5)
 
+    held_back[:] = film_msgs
+    drain()
     arrived(film_msgs)
     wide = [widen(fb[0], fb[1], fb[2], f) for f in range(2)]
-    diag = wd[...]
+    diag = wd[0]
     inverse = 1.0 / (diag + wide[0])
     wcf[6, 0] = (wcf[6, 0] * diag + wide[1]) * inverse
     for n in range(6):
@@ -550,7 +576,8 @@
     solved = wxa if SWEEPS % 2 == 0 else wxb
 
     surface = pltpu.roll(solved[0, HALO:HALO + nx, :], 128 - HALO, axis=1)[:, 0:32]
-    picked = product(surface, hot_y[...], ((1,), (0,)))
+    picked = product16(jnp.concatenate(pieces(surface), axis=0), hot_y16[...], ((1,), (0,)))
+    picked = (picked[0:nx] + picked[nx:2 * nx]) + picked[2 * nx:3 * nx]
     picked = jnp.sum(picked * hot_x[...], axis=0, keepdims=True)
     for n in range(8):
         slots[n:n + 1, :] = picked[:, 256 * n:256 * n + 256]
@@ -610,9 +637,10 @@
             vmem(7, nsz // 128, nx, ny, 128),
             vmem(3, DEEP, wide, 128), vmem(3, wide, 128),
             vmem(DEEP, wide, 128), vmem(7, DEEP, wide, 128),
-            vmem(DEEP, wide, 128), vmem(DEEP, wide, 128), vmem(DEEP, wide, 128), vmem(wide, 128), vmem(nx, ny, 128),
+            vmem(DEEP, wide, 128), vmem(DEEP, wide, 128), vmem(DEEP, wide, 128), vmem(nx, ny, 128),
             vmem(16, 128), vmem(4, 16, 128), vmem(8, 128), vmem(4, 8, 128),
-            vmem(32, 2048), vmem(32, 2048), vmem(8, 256),
+            vmem(32, 2048), vmem(32, 2048),
+            pltpu.VMEM((32, 2048), jnp.bfloat16), pltpu.VMEM((32, 2048), jnp.bfloat16), vmem(8, 256),
             pltpu.SemaphoreType.DMA((6 * nz // 128 + 5 * nsz // 128,)),
             pltpu.SemaphoreType.DMA((N_MESSAGES,)),
             pltpu.SemaphoreType.DMA((N_MESSAGES,)),

time: 70.5 us -> 64.6 us (0.916); the launches traced: 69.5 us -> 64.3 us
  Pallas kernels: 65.4 us -> 60.2 us
    pallas_call x1, Pallas kernels: 65.4 us -> 60.2 us  [on_device(): pl.pallas_call(functools.partial(kernel, n_blk, n_sub), out_shape=(vmem(n...]
where the time goes in v4:
time: 64.6 us; the launch traced here: 64.3 us
  Pallas kernels  60.2 us (93%)
  local copies, waits for them, and re-layouts  2.89 us (4%)
  between operations  1.29 us (2%)
    pallas_call x1, Pallas kernels, on_device(): pl.pallas_call(functools.partial(kernel, n_blk, n_sub), out_shape=(vmem(n...  60.2 us
    unnamed x5, local copies, waits for them, and re-layouts  2.89 us

profile of v4, /device:TPU:5, one launch (start us, length us, event | category | flops | bytes accessed | tf_op | source)
XLA Modules:
  0.0 64.3 jit_solution(17549536940049879544)
XLA Ops:
  1.3 60.2 %shard_map.130 = (f32[32,32,512]{2,1,0:T(8,128)S(1)}, f32[32,32,256]{2,1,0:T(8,128)S(1)}, f32[8,128]{1,0:T(8,128)}) custom-call(s32[1]{0:T(128)S(6)} %copy.19.count_ref, f32[32,32,512]{2,1,0:T(8,128)} %t_hbm.1, f32[3,32,32,512]{3,2,1,0:T(8,128)} %vel_hbm.1, f32[32,32,512]{2,1,0:T(8,128)} %a_hbm.1, f32[32,32,256]{2,1,0:T(8,128)} %x_hbm.1, ...), custom_call_target="tpu_custom_call" | custom-call | tf_op jit(solution)/shard_map/pallas_call | solution.py:623
  61.5 1.3 %copy.17 = f32[32,32,512]{2,1,0:T(8,128)} copy(f32[32,32,512]{2,1,0:T(8,128)S(1)} %get-tuple-element.9) | data formatting | bytes 4194304
  62.8 0.0 copy-start
  62.8 1.0 %copy.18 = f32[32,32,256]{2,1,0:T(8,128)} copy(f32[32,32,256]{2,1,0:T(8,128)S(1)} %get-tuple-element.10) | data formatting | bytes 2097152
  63.7 0.0 copy-done
  63.8 0.6 copy.20
Async XLA Ops:
  62.8 1.0 %copy-start = (f32[8,128]{1,0:T(8,128)S(1)}, f32[8,128]{1,0:T(8,128)}, u32[]{:S(2)}) copy-start(f32[8,128]{1,0:T(8,128)} %get-tuple-element.8) | copy-start | bytes 12292

commit v5 on v4

--- a/solution.py
+++ b/solution.py
@@ -12,9 +12,11 @@
 HALO = 8
 DEEP = 16
 TOP = 8
-SOLID_STEP = 5
-WEDGE_SPLIT = 4
-FLUID_STEP = 2
+SOLID_STEP = 10
+WEDGE_SPLIT = 5
+COEF_CUTS = (0, 14, 26, 30)
+FLUID_STEP = 5
+COEF_STEP = 2
 EIG_LOW = 0.02
 EIG_HIGH = 2.0
 HIGHEST = lax.Precision.HIGHEST
@@ -456,13 +458,13 @@
         wcf[6, z] = near_field(z, 3) * inverse
         wd[z] = diag
 
-    def wedge_sweep(n):
+    def wedge_sweep(n, first=0, last=None):
         decay, gain = coefficients[n]
         src, dst = (wxa, wxb) if n % 2 == 0 else (wxb, wxa)
 
         def level(z):
             v = src[z]
-            near_v = shift_all(v) + [src[jnp.maximum(z - 1, 0)], src[z + 1]]
+            near_v = shift_all(v) + [src[jnp.maximum(z - 1, 0) if not isinstance(z, int) else max(z - 1, 0)], src[z + 1]]
             r = (wcf[0, z] * near_v[0] + wcf[1, z] * near_v[1]) + (wcf[2, z] * near_v[2] + wcf[3, z] * near_v[3])
             r = r + (wcf[4, z] * near_v[4] + wcf[5, z] * near_v[5]) + wcf[6, z]
             new = (1.0 + decay - gain) * v + gain * r
@@ -472,11 +474,16 @@
             for k, new in enumerate([level(z + k) for k in range(step)]):
                 dst[z + k] = new
 
-        count = DEEP - 1 - n
+        if last is None:
+            last = DEEP - 1 - n
+        count = last - first
         step = 3 if count % 3 == 0 else 2
-        loop(count - count % step, step, lambda z: levels(z, step))
-        if count % step:
-            levels(count - count % step, count % step)
+        if count > step:
+            loop(count - count % step, step, lambda z: levels(first + z, step))
+            if count % step:
+                levels(last - count % step, count % step)
+        else:
+            levels(first, count)
 
     def bands(refs):
         total = None
@@ -509,11 +516,18 @@
 
     loaded("uz")
     arrived(a_y + u_y)
-    half = interior // 2
-    loop(half, 1, lambda x: fluid_coef(1 + x))
+    cuts = [interior * n // (30 * COEF_STEP) * COEF_STEP for n in COEF_CUTS]
+
+    def coef_part(n):
+        first = 1 + cuts[n]
+        loop(cuts[n + 1] - cuts[n], COEF_STEP, lambda x: [fluid_coef(first + x + i) for i in range(COEF_STEP)])
+
+    coef_part(0)
     solid_sweep(1)
     near_msgs = send_near(nb, lambda ref, column, rows: ref.at[column, :, rows, :])
-    loop(interior - half, 1, lambda x: fluid_coef(1 + half + x))
+    coef_part(1)
+    solid_sweep(2)
+    coef_part(2)
     arrived(a_x + u_x)
     fluid_coef(0)
     fluid_coef(nx - 1)
@@ -523,12 +537,10 @@
     t_msgs = send_planes(t1)
     loop(interior, FLUID_STEP, lambda x: fluid_planes(t0, [1 + x + i for i in range(FLUID_STEP)], all_chunks, put_first))
     t_msgs += send_rows(t1)
-    solid_sweep(2)
+    solid_sweep(3)
 
     arrived(near_msgs)
     loop(DEEP, 2, lambda z: [spread_near(z), spread_near(z + 1)])
-    loop(DEEP, 2, lambda z: [wedge_coef(z), wedge_coef(z + 1)])
-    solid_sweep(3)
 
     arrived(t_msgs)
     loop(nx, 4, lambda x: fluid_planes(t1, [x + i for i in range(4)], (0,), put_second))
@@ -537,7 +549,7 @@
     row_msgs = [Message(rows_s, rows_r.at[d], d).start() for d in range(4)]
 
     if fluid_chunks > 1:
-        loop(nx, FLUID_STEP, lambda x: fluid_planes(t1, [x + i for i in range(FLUID_STEP)], all_chunks[1:], put_second))
+        loop(nx, 4, lambda x: fluid_planes(t1, [x + i for i in range(4)], all_chunks[1:], put_second))
     solid_sweep(4)
 
     solid_sends[:] = [item for item in solid_sends if item[0] >= 0]
@@ -557,6 +569,7 @@
     fb[1, HALO:HALO + nx, :] = jnp.concatenate([sums, jnp.zeros((nx, 64), jnp.float32)], axis=1)
     film_msgs = send_near(fb, lambda ref, column, rows: ref.at[column, rows, :])
 
+    loop(DEEP, 2, lambda z: [wedge_coef(z), wedge_coef(z + 1)])
     solid_sweep(5)
 
     held_back[:] = film_msgs
@@ -572,7 +585,7 @@
         wedge_sweep(n)
     solid_sweep(6)
     for n in range(WEDGE_SPLIT, SWEEPS):
-        wedge_sweep(n)
+        wedge_sweep(n, 0, SWEEPS - n)
     solved = wxa if SWEEPS % 2 == 0 else wxb
 
     surface = pltpu.roll(solved[0, HALO:HALO + nx, :], 128 - HALO, axis=1)[:, 0:32]
@@ -584,12 +597,17 @@
     wall_s[...] = slots[:, 128:256]
     wall_msgs = [Message(wall_s, wall_r.at[d], d).start() for d in range(4)]
 
+    for n in range(WEDGE_SPLIT, SWEEPS):
+        wedge_sweep(n, SWEEPS - n)
+
     def turn_back(x, _):
         cells = jnp.concatenate([solved[0:HALO, pl.ds(HALO + x, 1), :].reshape(HALO, 128), jnp.zeros((128 - HALO, 128), jnp.float32)], axis=0)
         wz[x] = jnp.transpose(cells)[HALO:HALO + ny]
         return 0
     lax.fori_loop(0, nx, turn_back, 0, unroll=2)
 
+    held_back[:] = wall_msgs
+    drain()
     solid_sweep(7)
 
     arrived(wall_msgs)

time: 64.6 us -> 62.6 us (0.969)
  Pallas kernels: 60.2 us -> 58.3 us
    pallas_call x1, Pallas kernels: 60.2 us -> 58.3 us  [on_device(): pl.pallas_call(functools.partial(kernel, n_blk, n_sub), out_shape=(vmem(n...]
where the time goes in v5:
time: 62.6 us; the launch traced here: 62.5 us
  Pallas kernels  58.3 us (93%)
  local copies, waits for them, and re-layouts  2.89 us (5%)
  between operations  1.29 us (2%)
    pallas_call x1, Pallas kernels, on_device(): pl.pallas_call(functools.partial(kernel, n_blk, n_sub), out_shape=(vmem(n...  58.3 us
    unnamed x5, local copies, waits for them, and re-layouts  2.89 us

profile of v5, /device:TPU:5, one launch (start us, length us, event | category | flops | bytes accessed | tf_op | source)
XLA Modules:
  0.0 62.5 jit_solution(6958177055670748238)
XLA Ops:
  1.3 58.3 %shard_map.130 = (f32[32,32,512]{2,1,0:T(8,128)S(1)}, f32[32,32,256]{2,1,0:T(8,128)S(1)}, f32[8,128]{1,0:T(8,128)}) custom-call(s32[1]{0:T(128)S(6)} %copy.19.count_ref, f32[32,32,512]{2,1,0:T(8,128)} %t_hbm.1, f32[3,32,32,512]{3,2,1,0:T(8,128)} %vel_hbm.1, f32[32,32,512]{2,1,0:T(8,128)} %a_hbm.1, f32[32,32,256]{2,1,0:T(8,128)} %x_hbm.1, ...), custom_call_target="tpu_custom_call" | custom-call | tf_op jit(solution)/shard_map/pallas_call | solution.py:641
  59.6 1.3 %copy.17 = f32[32,32,512]{2,1,0:T(8,128)} copy(f32[32,32,512]{2,1,0:T(8,128)S(1)} %get-tuple-element.9) | data formatting | bytes 4194304
  60.9 0.0 copy-start
  60.9 1.0 %copy.18 = f32[32,32,256]{2,1,0:T(8,128)} copy(f32[32,32,256]{2,1,0:T(8,128)S(1)} %get-tuple-element.10) | data formatting | bytes 2097152
  61.9 0.0 copy-done
  61.9 0.6 copy.20
Async XLA Ops:
  60.9 1.0 %copy-start = (f32[8,128]{1,0:T(8,128)S(1)}, f32[8,128]{1,0:T(8,128)}, u32[]{:S(2)}) copy-start(f32[8,128]{1,0:T(8,128)} %get-tuple-element.8) | copy-start | bytes 12292

commit v6 on v5

--- a/solution.py
+++ b/solution.py
@@ -137,17 +137,15 @@
     ):
         planes = own_planes if dst.shape[1] > nx else slice(0, nx)
         rows = own_rows if dst.shape[2] > ny else slice(0, ny)
-        loads[name] = []
+        n = len(loads)
         for c in range(dst.shape[0]):
-            n = sum(len(v) for v in loads.values())
-            copy = pltpu.make_async_copy(src.at[:, :, 128 * c:128 * c + 128], dst.at[c, planes, rows, :], load_sem.at[n])
-            copy.start()
-            loads[name].append(copy)
+            pltpu.make_async_copy(src.at[:, :, 128 * c:128 * c + 128], dst.at[c, planes, rows, :], load_sem.at[n]).start()
+        whole = dst.at[:, planes, rows, :]
+        loads[name] = pltpu.make_async_copy(whole, whole, load_sem.at[n])
 
     def loaded(*names):
         for name in names:
-            for copy in loads[name]:
-                copy.wait()
+            loads[name].wait()
 
     barrier = pltpu.get_barrier_semaphore()
     for db, ds in DIRS:
@@ -624,6 +622,15 @@
 N_MESSAGES = 8 + 12 + 8 + 4 * (SWEEPS - 1) + 4 + 4 + 8 + 4
 
 
+def store_kernel(t_in, x_in, wall_in, t_out, x_out, wall_out, sems):
+    copies = [pltpu.make_async_copy(src, dst, sems.at[n]) for n, (src, dst) in enumerate(
+        ((t_in, t_out), (x_in, x_out), (wall_in, wall_out)))]
+    for copy in copies:
+        copy.start()
+    for copy in copies:
+        copy.wait()
+
+
 def on_device(n_blk, n_sub, fluid_temp, velocity, eddy_diff, wall_prev, row_count, owner_table, landing_cell, solid_temp, conductivity, sink, heat_source):
     nx, ny, nz = fluid_temp.shape
     nsz = solid_temp.shape[2]
@@ -643,7 +650,7 @@
         out_shape=(
             vmem(nx, ny, nz),
             vmem(nx, ny, nsz),
-            jax.ShapeDtypeStruct((8, 128), f32),
+            vmem(8, 128),
         ),
         in_specs=[pl.BlockSpec(memory_space=pltpu.SMEM)] + [any_space] * 7 + [vmem_space] * 3,
         out_specs=(vmem_space,) * 3,
@@ -659,7 +666,7 @@
             vmem(16, 128), vmem(4, 16, 128), vmem(8, 128), vmem(4, 8, 128),
             vmem(32, 2048), vmem(32, 2048),
             pltpu.VMEM((32, 2048), jnp.bfloat16), pltpu.VMEM((32, 2048), jnp.bfloat16), vmem(8, 256),
-            pltpu.SemaphoreType.DMA((6 * nz // 128 + 5 * nsz // 128,)),
+            pltpu.SemaphoreType.DMA((9,)),
             pltpu.SemaphoreType.DMA((N_MESSAGES,)),
             pltpu.SemaphoreType.DMA((N_MESSAGES,)),
         ],
@@ -667,6 +674,17 @@
             collective_id=0, has_side_effects=True, vmem_limit_bytes=60 * 1024 * 1024
         ),
     )(row_count, fluid_temp, velocity, eddy_diff, solid_temp, conductivity, sink, heat_source, wall_prev.reshape(8, 128), owner_table, landing_cell)
+    fluid_new, solid_new, wall_new = pl.pallas_call(
+        store_kernel,
+        out_shape=(
+            jax.ShapeDtypeStruct((nx, ny, nz), f32),
+            jax.ShapeDtypeStruct((nx, ny, nsz), f32),
+            jax.ShapeDtypeStruct((8, 128), f32),
+        ),
+        in_specs=[vmem_space] * 3,
+        out_specs=(any_space,) * 3,
+        scratch_shapes=[pltpu.SemaphoreType.DMA((3,))],
+    )(*[pltpu.with_memory_space_constraint(v, pltpu.VMEM) for v in (fluid_new, solid_new, wall_new)])
     return fluid_new, solid_new, wall_new.reshape(-1)
 
 

time: 62.6 us -> 65.8 us (1.051)
  local copies, waits for them, and re-layouts: 2.89 us -> 5.1 us
  Pallas kernels: 58.3 us -> 59.1 us
    unnamed x5 -> x8, local copies, waits for them, and re-layouts: 2.89 us -> 5.1 us
    pallas_call x0 -> x1, Pallas kernels: none -> 1.69 us  [on_device(): pl.pallas_call(store_kernel, out_shape=(jax.ShapeDtypeStruct((nx, ny, nz)...]
    pallas_call x1, Pallas kernels: 58.3 us -> 57.4 us  [on_device(): pl.pallas_call(functools.partial(kernel, n_blk, n_sub), out_shape=(vmem(n...]
where the time goes in v6:
time: 65.8 us; the launch traced here: 65.5 us
  Pallas kernels  59.1 us (90%)
  local copies, waits for them, and re-layouts  5.1 us (8%)
  between operations  1.3 us (2%)
    pallas_call x1, Pallas kernels, on_device(): pl.pallas_call(functools.partial(kernel, n_blk, n_sub), out_shape=(vmem(n...  57.4 us
    unnamed x8, local copies, waits for them, and re-layouts  5.1 us
    pallas_call x1, Pallas kernels, on_device(): pl.pallas_call(store_kernel, out_shape=(jax.ShapeDtypeStruct((nx, ny, nz)...  1.69 us

profile of v6, /device:TPU:5, one launch (start us, length us, event | category | flops | bytes accessed | tf_op | source)
XLA Modules:
  0.0 65.5 jit_solution(13632012190779979507)
XLA Ops:
  1.3 57.4 %shard_map.130 = (f32[32,32,512]{2,1,0:T(8,128)S(1)}, f32[32,32,256]{2,1,0:T(8,128)S(1)}, f32[8,128]{1,0:T(8,128)S(1)}) custom-call(s32[1]{0:T(128)S(6)} %copy.14.count_ref, f32[32,32,512]{2,1,0:T(8,128)} %t_hbm.1, f32[3,32,32,512]{3,2,1,0:T(8,128)} %vel_hbm.1, f32[32,32,512]{2,1,0:T(8,128)} %a_hbm.1, f32[32,32,256]{2,1,0:T(8,128)} %x_hbm.1, ...), custom_call_target="tpu_custom_call" | custom-call | tf_op jit(solution)/shard_map/pallas_call | solution.py:648
  58.7 0.0 copy-start
  58.7 1.3 %copy-done = f32[32,32,512]{2,1,0:T(8,128)} copy-done((f32[32,32,512]{2,1,0:T(8,128)}, f32[32,32,512]{2,1,0:T(8,128)S(1)}, u32[]{:S(2)}) %copy-start) | copy-done | bytes 2097176
  60.0 0.0 copy-start.2
  60.1 1.0 %copy-done.2 = f32[32,32,256]{2,1,0:T(8,128)} copy-done((f32[32,32,256]{2,1,0:T(8,128)}, f32[32,32,256]{2,1,0:T(8,128)S(1)}, u32[]{:S(2)}) %copy-start.2) | copy-done | bytes 1048600
  61.0 0.0 copy-start.1
  61.0 1.6 %copy-done.1 = f32[32,32,512]{2,1,0:T(8,128)S(1)} copy-done((f32[32,32,512]{2,1,0:T(8,128)S(1)}, f32[32,32,512]{2,1,0:T(8,128)}, u32[]{:S(2)}) %copy-start.1) | copy-done | bytes 2097176
  62.6 0.0 copy-start.3
  62.6 1.2 %copy-done.3 = f32[32,32,256]{2,1,0:T(8,128)S(1)} copy-done((f32[32,32,256]{2,1,0:T(8,128)S(1)}, f32[32,32,256]{2,1,0:T(8,128)}, u32[]{:S(2)}) %copy-start.3) | copy-done | bytes 1048600
  63.8 1.7 %shard_map.131 = (f32[32,32,512]{2,1,0:T(8,128)}, f32[32,32,256]{2,1,0:T(8,128)}, f32[8,128]{1,0:T(8,128)}) custom-call(f32[32,32,512]{2,1,0:T(8,128)S(1)} %copy-done.1, f32[32,32,256]{2,1,0:T(8,128)S(1)} %copy-done.3, f32[8,128]{1,0:T(8,128)S(1)} %get-tuple-element.11.wall_in), custom_call_target="tpu_custom_call" | custom-call | tf_op jit(solution)/shard_map/pallas_call | solution.py:677
Async XLA Ops:
  58.7 1.3 %copy-start = (f32[32,32,512]{2,1,0:T(8,128)}, f32[32,32,512]{2,1,0:T(8,128)S(1)}, u32[]{:S(2)}) copy-start(f32[32,32,512]{2,1,0:T(8,128)S(1)} %get-tuple-element.9.t_in) | copy-start | bytes 6291460
  60.0 1.0 %copy-start.2 = (f32[32,32,256]{2,1,0:T(8,128)}, f32[32,32,256]{2,1,0:T(8,128)S(1)}, u32[]{:S(2)}) copy-start(f32[32,32,256]{2,1,0:T(8,128)S(1)} %get-tuple-element.10.x_in) | copy-start | bytes 3145732
  61.0 1.6 %copy-start.1 = (f32[32,32,512]{2,1,0:T(8,128)S(1)}, f32[32,32,512]{2,1,0:T(8,128)}, u32[]{:S(2)}) copy-start(f32[32,32,512]{2,1,0:T(8,128)} %copy-done) | copy-start | bytes 6291460
  62.6 1.2 %copy-start.3 = (f32[32,32,256]{2,1,0:T(8,128)S(1)}, f32[32,32,256]{2,1,0:T(8,128)}, u32[]{:S(2)}) copy-start(f32[32,32,256]{2,1,0:T(8,128)} %copy-done.2) | copy-start | bytes 3145732

commit v7 on v6

--- a/solution.py
+++ b/solution.py
@@ -209,6 +209,11 @@
 
     def product16(x, y, dims):
         return lax.dot_general(x, y, (dims, ((), ())), preferred_element_type=jnp.float32)
+
+    def picked_by(v, hot, dims):
+        n = v.shape[0]
+        out = product16(jnp.concatenate(pieces(v), axis=0), hot.astype(jnp.bfloat16), dims)
+        return (out[0:n] + out[n:2 * n]) + out[2 * n:3 * n]
 
     lane, lane8, sub8 = iota((ny, 128), 1), iota((8, 128), 1), iota((8, 128), 0)
     keep = (lane8 & 7) == sub8
@@ -543,7 +548,7 @@
     arrived(t_msgs)
     loop(nx, 4, lambda x: fluid_planes(t1, [x + i for i in range(4)], (0,), put_second))
     gas = rows_of(lambda x: t_out[x, :, 0:128])
-    rows_s[...] = product(jnp.concatenate([film, gas], axis=0), select(), ((1,), (1,)))
+    rows_s[...] = picked_by(jnp.concatenate([film, gas], axis=0), select(), ((1,), (1,)))
     row_msgs = [Message(rows_s, rows_r.at[d], d).start() for d in range(4)]
 
     if fluid_chunks > 1:
@@ -610,9 +615,9 @@
 
     arrived(wall_msgs)
     back = bands([wall_r.at[d] for d in (1, 0, 3, 2)])
-    rows = (self_mask * slots[:, 0:128] + product(back, select(), ((1,), (0,)))) * live
+    rows = (self_mask * slots[:, 0:128] + picked_by(back, select(), ((1,), (0,)))) * live
     rows = jnp.concatenate([jnp.where(lane8 < 16, pltpu.roll(rows, (128 - 16 * n) % 128, axis=1), 0.0) for n in range(8)], axis=0)
-    rows = product(rows, compress, ((1,), (1,)))
+    rows = picked_by(rows, compress, ((1,), (1,)))
     for n in range(8):
         wall_out[n:n + 1, :] = jnp.sum(jnp.where(keep, rows[8 * n:8 * n + 8], 0.0), axis=0, keepdims=True)
     for m in list(pending):

time: 65.8 us -> 65.5 us (level)
  no operation moved by 1% of the time
where the time goes in v7:
time: 65.5 us; the launch traced here: 65.3 us
  Pallas kernels  58.9 us (90%)
  local copies, waits for them, and re-layouts  5.1 us (8%)
  between operations  1.3 us (2%)
    pallas_call x1, Pallas kernels, on_device(): pl.pallas_call(functools.partial(kernel, n_blk, n_sub), out_shape=(vmem(n...  57.2 us
    unnamed x8, local copies, waits for them, and re-layouts  5.1 us
    pallas_call x1, Pallas kernels, on_device(): pl.pallas_call(store_kernel, out_shape=(jax.ShapeDtypeStruct((nx, ny, nz)...  1.69 us

profile of v7, /device:TPU:5, one launch (start us, length us, event | category | flops | bytes accessed | tf_op | source)
XLA Modules:
  0.0 65.3 jit_solution(4038811881043038841)
XLA Ops:
  1.3 57.2 %shard_map.130 = (f32[32,32,512]{2,1,0:T(8,128)S(1)}, f32[32,32,256]{2,1,0:T(8,128)S(1)}, f32[8,128]{1,0:T(8,128)S(1)}) custom-call(s32[1]{0:T(128)S(6)} %copy.14.count_ref, f32[32,32,512]{2,1,0:T(8,128)} %t_hbm.1, f32[3,32,32,512]{3,2,1,0:T(8,128)} %vel_hbm.1, f32[32,32,512]{2,1,0:T(8,128)} %a_hbm.1, f32[32,32,256]{2,1,0:T(8,128)} %x_hbm.1, ...), custom_call_target="tpu_custom_call" | custom-call | tf_op jit(solution)/shard_map/pallas_call | solution.py:653
  58.5 0.0 copy-start
  58.5 1.3 %copy-done = f32[32,32,512]{2,1,0:T(8,128)} copy-done((f32[32,32,512]{2,1,0:T(8,128)}, f32[32,32,512]{2,1,0:T(8,128)S(1)}, u32[]{:S(2)}) %copy-start) | copy-done | bytes 2097176
  59.8 0.0 copy-start.2
  59.8 1.0 %copy-done.2 = f32[32,32,256]{2,1,0:T(8,128)} copy-done((f32[32,32,256]{2,1,0:T(8,128)}, f32[32,32,256]{2,1,0:T(8,128)S(1)}, u32[]{:S(2)}) %copy-start.2) | copy-done | bytes 1048600
  60.8 0.0 copy-start.1
  60.8 1.6 %copy-done.1 = f32[32,32,512]{2,1,0:T(8,128)S(1)} copy-done((f32[32,32,512]{2,1,0:T(8,128)S(1)}, f32[32,32,512]{2,1,0:T(8,128)}, u32[]{:S(2)}) %copy-start.1) | copy-done | bytes 2097176
  62.4 0.0 copy-start.3
  62.4 1.2 %copy-done.3 = f32[32,32,256]{2,1,0:T(8,128)S(1)} copy-done((f32[32,32,256]{2,1,0:T(8,128)S(1)}, f32[32,32,256]{2,1,0:T(8,128)}, u32[]{:S(2)}) %copy-start.3) | copy-done | bytes 1048600
  63.6 1.7 %shard_map.131 = (f32[32,32,512]{2,1,0:T(8,128)}, f32[32,32,256]{2,1,0:T(8,128)}, f32[8,128]{1,0:T(8,128)}) custom-call(f32[32,32,512]{2,1,0:T(8,128)S(1)} %copy-done.1, f32[32,32,256]{2,1,0:T(8,128)S(1)} %copy-done.3, f32[8,128]{1,0:T(8,128)S(1)} %get-tuple-element.11.wall_in), custom_call_target="tpu_custom_call" | custom-call | tf_op jit(solution)/shard_map/pallas_call | solution.py:682
Async XLA Ops:
  58.5 1.3 %copy-start = (f32[32,32,512]{2,1,0:T(8,128)}, f32[32,32,512]{2,1,0:T(8,128)S(1)}, u32[]{:S(2)}) copy-start(f32[32,32,512]{2,1,0:T(8,128)S(1)} %get-tuple-element.9.t_in) | copy-start | bytes 6291460
  59.8 1.0 %copy-start.2 = (f32[32,32,256]{2,1,0:T(8,128)}, f32[32,32,256]{2,1,0:T(8,128)S(1)}, u32[]{:S(2)}) copy-start(f32[32,32,256]{2,1,0:T(8,128)S(1)} %get-tuple-element.10.x_in) | copy-start | bytes 3145732
  60.8 1.6 %copy-start.1 = (f32[32,32,512]{2,1,0:T(8,128)S(1)}, f32[32,32,512]{2,1,0:T(8,128)}, u32[]{:S(2)}) copy-start(f32[32,32,512]{2,1,0:T(8,128)} %copy-done) | copy-start | bytes 6291460
  62.4 1.2 %copy-start.3 = (f32[32,32,256]{2,1,0:T(8,128)S(1)}, f32[32,32,256]{2,1,0:T(8,128)}, u32[]{:S(2)}) copy-start(f32[32,32,256]{2,1,0:T(8,128)} %copy-done.2) | copy-start | bytes 3145732
